TPU v7x, 1024 devices: a whole 4x8x16 slice. The times are simulated.
1024 devices in a mesh: ctx: 64 (over z, x), head: 16 (over y, core).
Axes of the slice: x: 4, y: 8, z: 16, core: 2. Of those that a mesh axis runs over, the one named last changes fastest.
Arguments:
- head_input: float32 [16384, 4096], P('ctx', 'head'), may hold values from -6 to 6
- step_size: float32 [64, 16384], P('head', 'ctx'), may hold values from 0.25 to 2
- log_decay: float32 [64, 16384], P('head', 'ctx'), may hold values from -1.6 to 0
- write_proj: float32 [16384, 128], P('ctx'), may hold values from -0.375 to 0.375
- read_proj: float32 [16384, 128], P('ctx'), may hold values from -0.5 to 0.5
- grad_out: float32 [16384, 4096], P('ctx', 'head'), may hold values from -6 to 6
Outputs:
- head_output: float32 [16384, 4096], P('ctx', 'head')
- grad_input: float32 [16384, 4096], P('ctx', 'head')
- grad_step: float32 [64, 16384], P('head', 'ctx')
- write_grad: float32 [16384, 128], P(('ctx', 'head'))
- read_grad: float32 [16384, 128], P(('ctx', 'head'))
All inputs are finite; a program needn't handle non-finite values.
Results may differ from a plain program's by a relative error of at most 0.00022.
Values sent between devices are 32-bit elements; how exact they have to be, the bound alone decides.
No kernel may reach another device: no remote copies, remote signals or barrier semaphores. Data moves between devices by JAX's collectives and lax.ppermute only.
A program may use at most 32 MiB of HBM per device.

v0:
```python
import jax
import jax.numpy as jnp
from jax import lax
from jax.sharding import PartitionSpec as P

GROUP = 128


def prefix(x, axis, combine, identity, reverse):
    size, here = (lax.axis_size(axis), lax.axis_index(axis))
    everything = jax.tree.map(lambda part: lax.all_gather(part, axis), x)
    start = jax.tree.map(
        lambda part, zero: jnp.broadcast_to(jnp.asarray(zero, part.dtype), part.shape), x, identity
    )

    def turn(k, before):
        at = size - 1 - k if reverse else k
        reached = at > here if reverse else at < here
        new = combine(before, jax.tree.map(lambda part: part[at], everything))
        return jax.tree.map(lambda a, b: jnp.where(reached, a, b), new, before)

    return lax.fori_loop(0, size, turn, start)


def combine_forward(first_part, second_part):
    return (
        first_part[0] * second_part[0],
        second_part[1] + second_part[0][:, None, None] * first_part[1],
    )


def combine_backward(first_part, second_part):
    return (
        first_part[0] * second_part[0],
        second_part[1] + second_part[0][:, None, None] * first_part[1],
    )


def shards(head_input, step_size, log_decay, write_proj, read_proj, grad_out):
    highest = lax.Precision.HIGHEST
    head_count = step_size.shape[0]
    row_count = head_input.shape[0]
    head_width = head_input.shape[1] // head_count
    state_width = write_proj.shape[1]
    group_count = row_count // GROUP
    inputs = head_input.reshape(row_count, head_count, head_width).transpose(1, 2, 0)
    scaled = inputs * step_size[:, None, :]
    upstream = grad_out.reshape(row_count, head_count, head_width).transpose(1, 2, 0)
    row_ids = lax.broadcasted_iota(jnp.int32, (GROUP, GROUP), 0)
    col_ids = lax.broadcasted_iota(jnp.int32, (GROUP, GROUP), 1)
    lower_mask = row_ids >= col_ids
    lower_ones = lower_mask.astype(jnp.float32)
    blocks = []
    for position in range(group_count):
        offset = position * GROUP
        group_rates = log_decay[:, offset : offset + GROUP]
        scaled_part = scaled[:, :, offset : offset + GROUP]
        upstream_part = upstream[:, :, offset : offset + GROUP]
        write_part = write_proj[offset : offset + GROUP]
        read_part = read_proj[offset : offset + GROUP]
        cumulated = jnp.dot(group_rates, lower_ones.T, precision=highest)
        final_cum = cumulated[:, -1:]
        gap_logs = cumulated[:, :, None] - cumulated[:, None, :]
        decay_mat = jnp.where(
            lower_mask[None], jnp.exp(jnp.where(lower_mask[None], gap_logs, 0.0)), 0.0
        )
        inner_prod = jnp.dot(read_part, write_part.T, precision=highest)
        mixed_mat = inner_prod[None] * decay_mat
        out_near = jnp.einsum("hts,hps->hpt", mixed_mat, scaled_part, precision=highest)
        back_near = jnp.einsum("hst,hps->hpt", mixed_mat, upstream_part, precision=highest)
        pair_prods = jnp.einsum("hpt,hps->hts", upstream_part, scaled_part, precision=highest)
        weight_sum = jnp.sum(decay_mat * pair_prods, axis=0)
        read_near = jnp.dot(weight_sum, write_part, precision=highest)
        write_near = jnp.dot(weight_sum.T, read_part, precision=highest)
        into_factor = jnp.exp(cumulated)[:, None, :]
        outof_factor = jnp.exp(final_cum - cumulated)[:, None, :]
        whole_decay = jnp.exp(final_cum[:, 0])
        into_upstream = into_factor * upstream_part
        outof_scaled = outof_factor * scaled_part
        fwd_part = jnp.einsum("hps,sn->hpn", outof_scaled, write_part, precision=highest)
        bwd_part = jnp.einsum("hps,sn->hpn", into_upstream, read_part, precision=highest)
        blocks.append(
            (
                into_upstream,
                outof_scaled,
                write_part,
                read_part,
                into_factor,
                outof_factor,
                whole_decay,
                out_near,
                back_near,
                write_near,
                read_near,
                fwd_part,
                bwd_part,
            )
        )
    unit_decay = jnp.ones((head_count,), dtype=jnp.float32)
    zero_state = jnp.zeros((head_count, head_width, state_width), dtype=jnp.float32)
    fwd_decay, fwd_state = (unit_decay, zero_state)
    for entry in blocks:
        fwd_decay = fwd_decay * entry[6]
        fwd_state = entry[6][:, None, None] * fwd_state + entry[11]
    bwd_decay, bwd_state = (unit_decay, zero_state)
    for entry in reversed(blocks):
        bwd_decay = bwd_decay * entry[6]
        bwd_state = entry[12] + entry[6][:, None, None] * bwd_state
    state_in = prefix(
        (fwd_decay, fwd_state), "ctx", combine_forward, (unit_decay, zero_state), False
    )[1]
    grad_in = prefix(
        (bwd_decay, bwd_state), "ctx", combine_backward, (unit_decay, zero_state), True
    )[1]
    entering = []
    current = state_in
    for entry in blocks:
        entering.append(current)
        current = entry[6][:, None, None] * current + entry[11]
    leaving = [None] * group_count
    current = grad_in
    for position in range(group_count - 1, -1, -1):
        leaving[position] = current
        current = blocks[position][12] + blocks[position][6][:, None, None] * current
    out_blocks, back_blocks, write_far, read_far = ([], [], [], [])
    for position in range(group_count):
        into_upstream, outof_scaled, write_part, read_part, into_factor, outof_factor = blocks[
            position
        ][:6]
        state_here = entering[position]
        state_after = leaving[position]
        out_blocks.append(
            blocks[position][7]
            + into_factor * jnp.einsum("tn,hpn->hpt", read_part, state_here, precision=highest)
        )
        back_blocks.append(
            blocks[position][8]
            + outof_factor * jnp.einsum("tn,hpn->hpt", write_part, state_after, precision=highest)
        )
        read_far.append(jnp.einsum("hpt,hpn->tn", into_upstream, state_here, precision=highest))
        write_far.append(jnp.einsum("hpt,hpn->tn", outof_scaled, state_after, precision=highest))
    result_rows = jnp.concatenate(out_blocks, axis=2)
    back_rows = jnp.concatenate(back_blocks, axis=2)
    write_carried = jnp.concatenate(write_far, axis=0)
    read_carried = jnp.concatenate(read_far, axis=0)
    write_total = jnp.concatenate([entry[9] for entry in blocks], axis=0) + write_carried
    read_total = jnp.concatenate([entry[10] for entry in blocks], axis=0) + read_carried
    write_grad, read_grad = (
        lax.psum_scatter(write_total, "head", scatter_dimension=0, tiled=True),
        lax.psum_scatter(read_total, "head", scatter_dimension=0, tiled=True),
    )
    grad_input = (
        (step_size[:, None, :] * back_rows)
        .transpose(2, 0, 1)
        .reshape(row_count, head_count * head_width)
    )
    grad_step = jnp.sum(inputs * back_rows, axis=1)
    head_output = result_rows.transpose(2, 0, 1).reshape(row_count, head_count * head_width)
    return (head_output, grad_input, grad_step, write_grad, read_grad)


def solution(mesh):
    placed = (
        P("ctx", "head"),
        P("head", "ctx"),
        P("head", "ctx"),
        P("ctx", None),
        P("ctx", None),
        P("ctx", "head"),
    )
    return jax.shard_map(
        shards,
        mesh=mesh,
        in_specs=placed,
        out_specs=(
            P("ctx", "head"),
            P("ctx", "head"),
            P("head", "ctx"),
            P(("ctx", "head"), None),
            P(("ctx", "head"), None),
        ),
        check_vma=False,
    )
```

profile of v0, /device:TPU:1, one launch (start us, length us, event | category | flops | bytes accessed | tf_op | source)
XLA Modules:
  0.0 553.7 jit_solution(5549522310239827743)
XLA Ops:
  9.3 1.1 copy.36
  10.4 1.1 fusion.38
  11.5 1.8 convolution_add_fusion.2
  13.3 1.3 dynamic-slice
  15.5 130.1 %all-reduce = f32[256]{0:T(256)S(1)} all-reduce(f32[256]{0:T(256)S(1)} %dynamic-update-slice), channel_id=3, replica_groups=mesh['ctx'=64,'head'=16] {'ctx'}, use_global_device_ids=true, to_apply=%add | all-reduce | flops 256 | bytes 2048
  145.7 1.1 copy.31
  146.8 1.1 fusion.81
  148.0 1.1 fusion.92
  149.1 28.2 %all-gather.8.cloned.1.call-done = f32[256,64,128]{2,1,0:T(8,128)} async-done(((f32[4,64,128]{2,1,0:T(8,128)}), f32[256,64,128]{2,1,0:T(8,128)}) %all-gather.8.cloned.1.call-update) | async-done | bytes 8388624 | tf_op jit(solution)/shard_map/all_gather | solution.py:11
  177.3 66.7 %while.31 = (s32[]{:T(128)}, f32[4,64,128]{2,1,0:T(8,128)S(1)}, s32[]{:T(128)}, f32[64,4,64,128]{3,2,1,0:T(8,128)}, f32[64,4]{1,0:T(8,128)S(1)}, /*index=5*/s32[]{:T(128)}, s32[]{:T(128)}, s32[]{:T(128)}, s32[]{:T(128)}) while((s32[]{:T(128)}, f32[4,64,128]{2,1,0:T(8,128)S(1)}, s32[]{:T(128)}, f32[64,4,64,128]{3,2,1,0:T(8,128)}, ...), condition=%wide.region_3.4_spmd.clone, body=%wide.region_2.3_spmd.clone.sunk | while | flops 131080 | bytes 393439 | solution.py:22
  244.1 1.1 convolution_multiply_fusion
  245.2 1.2 convolution_multiply_fusion.1
  247.8 1.3 multiply_reduce_fusion
  249.1 1.1 fusion.43
  250.2 1.8 convolution_add_fusion.3
  256.8 151.8 %all-gather.6.cloned.1.call-done = f32[256,64,128]{2,1,0:T(8,128)} async-done(((f32[4,64,128]{2,1,0:T(8,128)}), f32[256,64,128]{2,1,0:T(8,128)}) %all-gather.6.cloned.1.call-update) | async-done | bytes 8388624 | tf_op jit(solution)/shard_map/all_gather | solution.py:11
  408.6 66.4 %while.30 = (s32[]{:T(128)}, f32[4,64,128]{2,1,0:T(8,128)S(1)}, s32[]{:T(128)}, f32[64,4,64,128]{3,2,1,0:T(8,128)}, f32[64,4]{1,0:T(8,128)S(1)}, /*index=5*/s32[]{:T(128)}, s32[]{:T(128)}) while((s32[]{:T(128)}, f32[4,64,128]{2,1,0:T(8,128)S(1)}, s32[]{:T(128)}, f32[64,4,64,128]{3,2,1,0:T(8,128)}, f32[64,4]{1,0:T(8,128)S(1)}, ...), condition=%wide.region_1.2_spmd.clone, body=%wide.region_0.1_spmd.clone.sunk | while | flops 131076 | bytes 393377 | solution.py:22
  433.5 1.0 fusion.117
  434.5 1.0 fusion.117
  437.6 1.0 fusion.117
  438.7 1.0 fusion.117
  439.7 1.0 fusion.117
  443.8 1.0 fusion.117
  444.9 1.0 fusion.117
  450.1 1.0 fusion.117
  451.1 1.0 fusion.117
  452.2 1.0 fusion.117
  455.3 1.0 fusion.117
  456.3 1.0 fusion.117
  457.3 1.0 fusion.117
  472.9 1.0 fusion.117
  479.5 67.6 %reduce-scatter.5.cloned.1.call-done = f32[16,128]{1,0:T(8,128)} async-done(((f32[256,128]{1,0:T(8,128)}), f32[16,128]{1,0:T(8,128)}) %reduce-scatter.5.cloned.1.call-update) | async-done | bytes 8208 | tf_op jit(solution)/shard_map/reduce_scatter | solution.py:150
  (287 shorter events, 127.8 us)
Async XLA Ops:
  7.2 247.8 %copy-start.1 = (f32[256,128]{1,0:T(8,128)S(1)}, f32[256,128]{1,0:T(8,128)}, u32[]{:S(2)}) copy-start(f32[256,128]{1,0:T(8,128)} %param.14) | copy-start | bytes 393220
  7.2 248.9 %copy-start = (f32[256,128]{1,0:T(8,128)S(1)}, f32[256,128]{1,0:T(8,128)}, u32[]{:S(2)}) copy-start(f32[256,128]{1,0:T(8,128)} %param.13) | copy-start | bytes 393220
  7.2 170.1 %all-gather.8.cloned.1.call-start = ((), (), s32[]{:S(2)}) async-start(), calls=%async_computation.5 | async-start | bytes 8519680 | tf_op jit(solution)/shard_map/all_gather | solution.py:11
  13.3 395.3 %all-gather.6.cloned.1.call-start = ((), (), s32[]{:S(2)}) async-start(), calls=%async_computation.4 | async-start | bytes 8519680 | tf_op jit(solution)/shard_map/all_gather | solution.py:11
  252.0 227.5 %reduce-scatter.3.cloned.1.call-start = ((), (), s32[]{:S(2)}) async-start(), calls=%async_computation.2 | async-start | bytes 139264 | tf_op jit(solution)/shard_map/reduce_scatter | solution.py:149
  256.7 290.4 %reduce-scatter.5.cloned.1.call-start = ((), (), s32[]{:S(2)}) async-start(), calls=%async_computation.3 | async-start | bytes 139264 | tf_op jit(solution)/shard_map/reduce_scatter | solution.py:150
Sparse Core Ops, SparseCore 0:
  13.4 163.8 all-gather.7
  252.1 156.3 all-gather.5
  412.5 66.9 reduce-scatter.2
  483.3 63.8 reduce-scatter.4
where the time goes:
time: 557 us; the launch traced here: 554 us
  waiting for transfers between devices  248 us (45%)
  other arithmetic  130 us (23%)
  blocking collectives  130 us (23%)
  matrix products  18.7 us (3%)
  between operations  14.7 us (3%)
  local copies, waits for them, and re-layouts  6.72 us (1%)
    all_gather x2, waiting for transfers between devices, prefix(): everything = jax.tree.map(lambda part: lax.all_gather(part, axis), x)  180 us
    unnamed x1, blocking collectives  130 us
    select_n x128, other arithmetic, turn(): return jax.tree.map(lambda a, b: jnp.where(reached, a, b), new, before)  127 us
    reduce_scatter x1, waiting for transfers between devices, shards(): lax.psum_scatter(read_total, 'head', scatter_dimension=0, tiled=True)  67.6 us
  transfers between devices with their start and end apart: 4, of which 4 were waited for; matrix products, arithmetic and copies ran while one was open for 14% of the time, Pallas kernels for 0%

commit v1 on v0

--- a/solution.py
+++ b/solution.py
@@ -8,18 +8,29 @@
 
 def prefix(x, axis, combine, identity, reverse):
     size, here = (lax.axis_size(axis), lax.axis_index(axis))
-    everything = jax.tree.map(lambda part: lax.all_gather(part, axis), x)
-    start = jax.tree.map(
-        lambda part, zero: jnp.broadcast_to(jnp.asarray(zero, part.dtype), part.shape), x, identity
-    )
-
-    def turn(k, before):
-        at = size - 1 - k if reverse else k
-        reached = at > here if reverse else at < here
-        new = combine(before, jax.tree.map(lambda part: part[at], everything))
-        return jax.tree.map(lambda a, b: jnp.where(reached, a, b), new, before)
-
-    return lax.fori_loop(0, size, turn, start)
+    decay, state = x
+    unit = jnp.ones_like(decay)
+    kept_decay, kept_state = (unit, jnp.zeros_like(state))
+    shift = 1
+    while shift < size:
+        if reverse:
+            pairs = [(j, j - shift) for j in range(shift, size)]
+            reached = here < size - shift
+        else:
+            pairs = [(j, j + shift) for j in range(size - shift)]
+            reached = here >= shift
+        packed = jnp.concatenate(
+            [state, jnp.broadcast_to(decay[:, None, None], state.shape[:1] + (1,) + state.shape[2:])],
+            axis=1,
+        )
+        got = lax.ppermute(packed, axis, pairs)
+        got_decay = jnp.where(reached, got[:, -1, 0], unit)
+        got_state = got[:, :-1]
+        kept_decay, kept_state = combine((got_decay, got_state), (kept_decay, kept_state))
+        if shift * 2 < size:
+            decay, state = combine((got_decay, got_state), (decay, state))
+        shift *= 2
+    return (kept_decay, kept_state)
 
 
 def combine_forward(first_part, second_part):
@@ -145,10 +156,10 @@
     read_carried = jnp.concatenate(read_far, axis=0)
     write_total = jnp.concatenate([entry[9] for entry in blocks], axis=0) + write_carried
     read_total = jnp.concatenate([entry[10] for entry in blocks], axis=0) + read_carried
-    write_grad, read_grad = (
-        lax.psum_scatter(write_total, "head", scatter_dimension=0, tiled=True),
-        lax.psum_scatter(read_total, "head", scatter_dimension=0, tiled=True),
+    both_grads = lax.psum_scatter(
+        jnp.concatenate([write_total, read_total], axis=1), "head", scatter_dimension=0, tiled=True
     )
+    write_grad, read_grad = (both_grads[:, :state_width], both_grads[:, state_width:])
     grad_input = (
         (step_size[:, None, :] * back_rows)
         .transpose(2, 0, 1)

time: 557 us -> 246 us (0.44)
  blocking collectives: 130 us -> 0 us
  other arithmetic: 130 us -> 4.21 us
  waiting for transfers between devices: 248 us -> 139 us
  starting transfers between devices: 0.16 us -> 71.8 us
  matrix products: 18.7 us -> 9.94 us
    all_gather x2 -> x0, waiting for transfers between devices: 180 us -> none  [prefix(): everything = jax.tree.map(lambda part: lax.all_gather(part, axis), x)]
    unnamed x1 -> x0, blocking collectives: 130 us -> none
    select_n x128 -> x0, other arithmetic: 127 us -> none  [turn(): return jax.tree.map(lambda a, b: jnp.where(reached, a, b), new, before)]
    ppermute x0 -> x12, starting transfers between devices: none -> 71.8 us  [prefix(): got = lax.ppermute(packed, axis, pairs)]
    ppermute x0 -> x12, waiting for transfers between devices: none -> 59.8 us  [prefix(): got = lax.ppermute(packed, axis, pairs)]
    reduce_scatter x2 -> x1, waiting for transfers between devices: 68.3 us -> 79.5 us  [shards(): lax.psum_scatter(jnp.concatenate([write_total, read_total], axis=1), 'hea...]
  transfers between devices with their start and end apart: 4 -> 13, of which waited for: 4 -> 13; matrix products, arithmetic and copies ran while one was open for 14% -> 3% of each run, Pallas kernels for 0% -> 0%
where the time goes in v1:
time: 246 us; the launch traced here: 245 us
  waiting for transfers between devices  139 us (57%)
  starting transfers between devices  71.8 us (29%)
  between operations  14.6 us (6%)
  matrix products  9.94 us (4%)
  local copies, waits for them, and re-layouts  5.43 us (2%)
  other arithmetic  4.21 us (2%)
    reduce_scatter x1, waiting for transfers between devices, shards(): lax.psum_scatter(jnp.concatenate([write_total, read_total], axis=1), 'hea...  79.5 us
    ppermute x12, starting transfers between devices, prefix(): got = lax.ppermute(packed, axis, pairs)  71.8 us
    ppermute x12, waiting for transfers between devices, prefix(): got = lax.ppermute(packed, axis, pairs)  59.8 us
  transfers between devices with their start and end apart: 13, of which 13 were waited for; matrix products, arithmetic and copies ran while one was open for 3% of the time, Pallas kernels for 0%

profile of v1, /device:TPU:1, one launch (start us, length us, event | category | flops | bytes accessed | tf_op | source)
XLA Modules:
  0.0 245.4 jit_solution(9041090067460692375)
XLA Ops:
  7.2 0.8 convolution_bitcast_fusion.8
  8.6 1.1 copy.41
  10.3 1.3 collective-permute-start.6
  11.6 5.2 %collective-permute-done.6 = f32[4,65,128]{2,1,0:T(8,128)S(1)} collective-permute-done((f32[4,65,128]{2,1,0:T(8,128)S(1)}, f32[4,65,128]{2,1,0:T(8,128)S(1)}, u32[]{:S(2)}, u32[]{:S(2)}) %collective-permute-start.6) | collective-permute-done | bytes 133152 | tf_op jit(solution)/shard_map/ppermute | solution.py:26
  17.1 1.3 collective-permute-start.7
  18.4 6.9 %collective-permute-done.7 = f32[4,65,128]{2,1,0:T(8,128)S(1)} collective-permute-done((f32[4,65,128]{2,1,0:T(8,128)S(1)}, f32[4,65,128]{2,1,0:T(8,128)S(1)}, u32[]{:S(2)}, u32[]{:S(2)}) %collective-permute-start.7) | collective-permute-done | bytes 133152 | tf_op jit(solution)/shard_map/ppermute | solution.py:26
  25.5 1.3 collective-permute-start.8
  26.9 5.6 %collective-permute-done.8 = f32[4,65,128]{2,1,0:T(8,128)S(1)} collective-permute-done((f32[4,65,128]{2,1,0:T(8,128)S(1)}, f32[4,65,128]{2,1,0:T(8,128)S(1)}, u32[]{:S(2)}, u32[]{:S(2)}) %collective-permute-start.8) | collective-permute-done | bytes 133152 | tf_op jit(solution)/shard_map/ppermute | solution.py:26
  32.7 1.4 collective-permute-start.9
  34.6 6.6 %collective-permute-done.9 = f32[4,65,128]{2,1,0:T(8,128)S(1)} collective-permute-done((f32[4,65,128]{2,1,0:T(8,128)S(1)}, f32[4,65,128]{2,1,0:T(8,128)S(1)}, u32[]{:S(2)}, u32[]{:S(2)}) %collective-permute-start.9) | collective-permute-done | bytes 133152 | tf_op jit(solution)/shard_map/ppermute | solution.py:26
  41.5 1.3 collective-permute-start.10
  43.6 11.0 %collective-permute-done.10 = f32[4,65,128]{2,1,0:T(8,128)S(1)} collective-permute-done((f32[4,65,128]{2,1,0:T(8,128)S(1)}, f32[4,65,128]{2,1,0:T(8,128)S(1)}, u32[]{:S(2)}, u32[]{:S(2)}) %collective-permute-start.10) | collective-permute-done | bytes 133152 | tf_op jit(solution)/shard_map/ppermute | solution.py:26
  54.9 1.3 collective-permute-start.11
  56.4 15.5 %collective-permute-done.11 = f32[4,65,128]{2,1,0:T(8,128)S(1)} collective-permute-done((f32[4,65,128]{2,1,0:T(8,128)S(1)}, f32[4,65,128]{2,1,0:T(8,128)S(1)}, u32[]{:S(2)}, u32[]{:S(2)}) %collective-permute-start.11) | collective-permute-done | bytes 133152 | tf_op jit(solution)/shard_map/ppermute | solution.py:26
  72.4 0.7 fusion.4
  76.1 5.4 %collective-permute-start = (f32[4,65,128]{2,1,0:T(8,128)S(1)}, f32[4,65,128]{2,1,0:T(8,128)S(1)}, u32[]{:S(2)}, u32[]{:S(2)}) collective-permute-start(f32[4,65,128]{2,1,0:T(8,128)S(1)} %pad_maximum_fusion.4), channel_id=1, source_target_pairs={{0,16},{16,32},{32,48},{48,64},{64,80},{80,96},{96,112},{112,128},... | collective-permute-start | bytes 399368 | tf_op jit(solution)/shard_map/ppermute | solution.py:26
  81.7 1.9 collective-permute-done
  83.9 7.3 %collective-permute-start.1 = (f32[4,65,128]{2,1,0:T(8,128)S(1)}, f32[4,65,128]{2,1,0:T(8,128)S(1)}, u32[]{:S(2)}, u32[]{:S(2)}) collective-permute-start(f32[4,65,128]{2,1,0:T(8,128)S(1)} %pad_maximum_fusion.5), channel_id=1, source_target_pairs={{0,32},{16,48},{32,64},{48,80},{64,96},{80,112},{96,128},{112,144}... | collective-permute-start | bytes 399368 | tf_op jit(solution)/shard_map/ppermute | solution.py:26
  91.5 1.8 collective-permute-done.1
  93.6 11.8 %collective-permute-start.2 = (f32[4,65,128]{2,1,0:T(8,128)S(1)}, f32[4,65,128]{2,1,0:T(8,128)S(1)}, u32[]{:S(2)}, u32[]{:S(2)}) collective-permute-start(f32[4,65,128]{2,1,0:T(8,128)S(1)} %pad_maximum_fusion.6), channel_id=1, source_target_pairs={{0,64},{16,80},{32,96},{48,112},{64,128},{80,144},{96,160},{112,17... | collective-permute-start | bytes 399368 | tf_op jit(solution)/shard_map/ppermute | solution.py:26
  106.0 1.4 collective-permute-done.2
  107.7 9.6 %collective-permute-start.3 = (f32[4,65,128]{2,1,0:T(8,128)S(1)}, f32[4,65,128]{2,1,0:T(8,128)S(1)}, u32[]{:S(2)}, u32[]{:S(2)}) collective-permute-start(f32[4,65,128]{2,1,0:T(8,128)S(1)} %pad_maximum_fusion.7), channel_id=1, source_target_pairs={{0,128},{16,144},{32,160},{48,176},{64,192},{80,208},{96,224},{112... | collective-permute-start | bytes 399368 | tf_op jit(solution)/shard_map/ppermute | solution.py:26
  117.5 1.9 collective-permute-done.3
  119.7 13.6 %collective-permute-start.4 = (f32[4,65,128]{2,1,0:T(8,128)S(1)}, f32[4,65,128]{2,1,0:T(8,128)S(1)}, u32[]{:S(2)}, u32[]{:S(2)}) collective-permute-start(f32[4,65,128]{2,1,0:T(8,128)S(1)} %pad_maximum_fusion.8), channel_id=1, source_target_pairs={{0,256},{16,272},{32,288},{48,304},{64,320},{80,336},{96,352},{112... | collective-permute-start | bytes 399368 | tf_op jit(solution)/shard_map/ppermute | solution.py:26
  134.0 1.4 collective-permute-done.4
  135.8 16.2 %collective-permute-start.5 = (f32[4,65,128]{2,1,0:T(8,128)S(1)}, f32[4,65,128]{2,1,0:T(8,128)S(1)}, u32[]{:S(2)}, u32[]{:S(2)}) collective-permute-start(f32[4,65,128]{2,1,0:T(8,128)S(1)} %pad_maximum_fusion.9), channel_id=1, source_target_pairs={{0,512},{16,528},{32,544},{48,560},{64,576},{80,592},{96,608},{112... | collective-permute-start | bytes 399368 | tf_op jit(solution)/shard_map/ppermute | solution.py:26
  152.4 0.8 copy.46
  153.2 0.8 collective-permute-done.5
  155.3 0.7 pad_maximum_fusion.2
  156.9 0.8 copy.45
  157.7 79.5 %reduce-scatter.2.cloned.1.call-done = f32[16,256]{1,0:T(8,128)} async-done(((f32[256,256]{1,0:T(8,128)}), f32[16,256]{1,0:T(8,128)}) %reduce-scatter.2.cloned.1.call-update) | async-done | bytes 16400 | tf_op jit(solution)/shard_map/reduce_scatter | solution.py:159
  237.2 1.3 fusion.141
  (96 shorter events, 13.3 us)
Async XLA Ops:
  7.2 0.9 copy-start.4
  7.2 230.1 %reduce-scatter.2.cloned.1.call-start = ((), (), s32[]{:S(2)}) async-start(), calls=%async_computation.1 | async-start | bytes 278528 | tf_op jit(solution)/shard_map/reduce_scatter | solution.py:159
  8.5 1.1 copy-start.1
  10.3 6.5 %collective-permute-start.6 = (f32[4,65,128]{2,1,0:T(8,128)S(1)}, f32[4,65,128]{2,1,0:T(8,128)S(1)}, u32[]{:S(2)}, u32[]{:S(2)}) collective-permute-start(f32[4,65,128]{2,1,0:T(8,128)S(1)} %pad_maximum_fusion.3), channel_id=1, source_target_pairs={{16,0},{32,16},{48,32},{64,48},{80,64},{96,80},{112,96},{128,112},... | collective-permute-start | bytes 399368 | tf_op jit(solution)/shard_map/ppermute | solution.py:26
  17.1 8.2 %collective-permute-start.7 = (f32[4,65,128]{2,1,0:T(8,128)S(1)}, f32[4,65,128]{2,1,0:T(8,128)S(1)}, u32[]{:S(2)}, u32[]{:S(2)}) collective-permute-start(f32[4,65,128]{2,1,0:T(8,128)S(1)} %pad_maximum_fusion.10), channel_id=1, source_target_pairs={{32,0},{48,16},{64,32},{80,48},{96,64},{112,80},{128,96},{144,112}... | collective-permute-start | bytes 399368 | tf_op jit(solution)/shard_map/ppermute | solution.py:26
  25.5 6.9 %collective-permute-start.8 = (f32[4,65,128]{2,1,0:T(8,128)S(1)}, f32[4,65,128]{2,1,0:T(8,128)S(1)}, u32[]{:S(2)}, u32[]{:S(2)}) collective-permute-start(f32[4,65,128]{2,1,0:T(8,128)S(1)} %pad_maximum_fusion.11), channel_id=1, source_target_pairs={{64,0},{80,16},{96,32},{112,48},{128,64},{144,80},{160,96},{176,11... | collective-permute-start | bytes 399368 | tf_op jit(solution)/shard_map/ppermute | solution.py:26
  32.5 1.9 copy-start.2
  32.7 1.5 copy-start
  32.7 8.5 %collective-permute-start.9 = (f32[4,65,128]{2,1,0:T(8,128)S(1)}, f32[4,65,128]{2,1,0:T(8,128)S(1)}, u32[]{:S(2)}, u32[]{:S(2)}) collective-permute-start(f32[4,65,128]{2,1,0:T(8,128)S(1)} %pad_maximum_fusion.12), channel_id=1, source_target_pairs={{128,0},{144,16},{160,32},{176,48},{192,64},{208,80},{224,96},{240... | collective-permute-start | bytes 399368 | tf_op jit(solution)/shard_map/ppermute | solution.py:26
  41.5 13.0 %collective-permute-start.10 = (f32[4,65,128]{2,1,0:T(8,128)S(1)}, f32[4,65,128]{2,1,0:T(8,128)S(1)}, u32[]{:S(2)}, u32[]{:S(2)}) collective-permute-start(f32[4,65,128]{2,1,0:T(8,128)S(1)} %pad_maximum_fusion.13), channel_id=1, source_target_pairs={{256,0},{272,16},{288,32},{304,48},{320,64},{336,80},{352,96},{368... | collective-permute-start | bytes 399368 | tf_op jit(solution)/shard_map/ppermute | solution.py:26
  54.9 17.0 %collective-permute-start.11 = (f32[4,65,128]{2,1,0:T(8,128)S(1)}, f32[4,65,128]{2,1,0:T(8,128)S(1)}, u32[]{:S(2)}, u32[]{:S(2)}) collective-permute-start(f32[4,65,128]{2,1,0:T(8,128)S(1)} %pad_maximum_fusion.14), channel_id=1, source_target_pairs={{512,0},{528,16},{544,32},{560,48},{576,64},{592,80},{608,96},{624... | collective-permute-start | bytes 399368 | tf_op jit(solution)/shard_map/ppermute | solution.py:26
  73.1 0.7 copy-start.3
  76.1 7.5 %collective-permute-start = (f32[4,65,128]{2,1,0:T(8,128)S(1)}, f32[4,65,128]{2,1,0:T(8,128)S(1)}, u32[]{:S(2)}, u32[]{:S(2)}) collective-permute-start(f32[4,65,128]{2,1,0:T(8,128)S(1)} %pad_maximum_fusion.4), channel_id=1, source_target_pairs={{0,16},{16,32},{32,48},{48,64},{64,80},{80,96},{96,112},{112,128},... | collective-permute-start | bytes 399368 | tf_op jit(solution)/shard_map/ppermute | solution.py:26
  83.9 9.4 %collective-permute-start.1 = (f32[4,65,128]{2,1,0:T(8,128)S(1)}, f32[4,65,128]{2,1,0:T(8,128)S(1)}, u32[]{:S(2)}, u32[]{:S(2)}) collective-permute-start(f32[4,65,128]{2,1,0:T(8,128)S(1)} %pad_maximum_fusion.5), channel_id=1, source_target_pairs={{0,32},{16,48},{32,64},{48,80},{64,96},{80,112},{96,128},{112,144}... | collective-permute-start | bytes 399368 | tf_op jit(solution)/shard_map/ppermute | solution.py:26
  93.6 13.8 %collective-permute-start.2 = (f32[4,65,128]{2,1,0:T(8,128)S(1)}, f32[4,65,128]{2,1,0:T(8,128)S(1)}, u32[]{:S(2)}, u32[]{:S(2)}) collective-permute-start(f32[4,65,128]{2,1,0:T(8,128)S(1)} %pad_maximum_fusion.6), channel_id=1, source_target_pairs={{0,64},{16,80},{32,96},{48,112},{64,128},{80,144},{96,160},{112,17... | collective-permute-start | bytes 399368 | tf_op jit(solution)/shard_map/ppermute | solution.py:26
  107.7 11.7 %collective-permute-start.3 = (f32[4,65,128]{2,1,0:T(8,128)S(1)}, f32[4,65,128]{2,1,0:T(8,128)S(1)}, u32[]{:S(2)}, u32[]{:S(2)}) collective-permute-start(f32[4,65,128]{2,1,0:T(8,128)S(1)} %pad_maximum_fusion.7), channel_id=1, source_target_pairs={{0,128},{16,144},{32,160},{48,176},{64,192},{80,208},{96,224},{112... | collective-permute-start | bytes 399368 | tf_op jit(solution)/shard_map/ppermute | solution.py:26
  119.7 15.8 %collective-permute-start.4 = (f32[4,65,128]{2,1,0:T(8,128)S(1)}, f32[4,65,128]{2,1,0:T(8,128)S(1)}, u32[]{:S(2)}, u32[]{:S(2)}) collective-permute-start(f32[4,65,128]{2,1,0:T(8,128)S(1)} %pad_maximum_fusion.8), channel_id=1, source_target_pairs={{0,256},{16,272},{32,288},{48,304},{64,320},{80,336},{96,352},{112... | collective-permute-start | bytes 399368 | tf_op jit(solution)/shard_map/ppermute | solution.py:26
  135.8 18.3 %collective-permute-start.5 = (f32[4,65,128]{2,1,0:T(8,128)S(1)}, f32[4,65,128]{2,1,0:T(8,128)S(1)}, u32[]{:S(2)}, u32[]{:S(2)}) collective-permute-start(f32[4,65,128]{2,1,0:T(8,128)S(1)} %pad_maximum_fusion.9), channel_id=1, source_target_pairs={{0,512},{16,528},{32,544},{48,560},{64,576},{80,592},{96,608},{112... | collective-permute-start | bytes 399368 | tf_op jit(solution)/shard_map/ppermute | solution.py:26
Sparse Core Ops, SparseCore 0:
  156.2 80.9 reduce-scatter.1

commit v2 on v1

--- a/solution.py
+++ b/solution.py
@@ -6,31 +6,56 @@
 GROUP = 128
 
 
-def prefix(x, axis, combine, identity, reverse):
+def both_prefixes(decay, fwd_state, bwd_state, axis):
     size, here = (lax.axis_size(axis), lax.axis_index(axis))
-    decay, state = x
     unit = jnp.ones_like(decay)
-    kept_decay, kept_state = (unit, jnp.zeros_like(state))
+    zero = jnp.zeros_like(fwd_state)
+    before_decay, before_state = (unit, zero)
+    after_decay, after_state = (unit, zero)
+    span_decay, span_fwd, span_bwd = (decay, fwd_state, bwd_state)
+    extra = decay.shape[:1] + (1,) + fwd_state.shape[2:]
     shift = 1
     while shift < size:
-        if reverse:
-            pairs = [(j, j - shift) for j in range(shift, size)]
-            reached = here < size - shift
-        else:
-            pairs = [(j, j + shift) for j in range(size - shift)]
-            reached = here >= shift
+        pairs = [(j, j ^ shift) for j in range(size)]
         packed = jnp.concatenate(
-            [state, jnp.broadcast_to(decay[:, None, None], state.shape[:1] + (1,) + state.shape[2:])],
-            axis=1,
+            [span_fwd, span_bwd, jnp.broadcast_to(span_decay[:, None, None], extra)], axis=1
         )
         got = lax.ppermute(packed, axis, pairs)
-        got_decay = jnp.where(reached, got[:, -1, 0], unit)
-        got_state = got[:, :-1]
-        kept_decay, kept_state = combine((got_decay, got_state), (kept_decay, kept_state))
+        width = fwd_state.shape[1]
+        got_fwd, got_bwd, got_decay = (got[:, :width], got[:, width : 2 * width], got[:, -1, 0])
+        upper = (here & shift) != 0
+        scale = before_decay[:, None, None]
+        before_state = jnp.where(upper, before_state + scale * got_fwd, before_state)
+        before_decay = jnp.where(upper, before_decay * got_decay, before_decay)
+        scale = after_decay[:, None, None]
+        after_state = jnp.where(upper, after_state, after_state + scale * got_bwd)
+        after_decay = jnp.where(upper, after_decay, after_decay * got_decay)
         if shift * 2 < size:
-            decay, state = combine((got_decay, got_state), (decay, state))
+            mine = span_decay[:, None, None]
+            theirs = got_decay[:, None, None]
+            span_fwd = jnp.where(upper, span_fwd + mine * got_fwd, got_fwd + theirs * span_fwd)
+            span_bwd = jnp.where(upper, got_bwd + theirs * span_bwd, span_bwd + mine * got_bwd)
+            span_decay = span_decay * got_decay
         shift *= 2
-    return (kept_decay, kept_state)
+    return (before_state, after_state)
+
+
+def halving_scatter(total, axis):
+    size, here = (lax.axis_size(axis), lax.axis_index(axis))
+    rows = total.shape[0] // size
+    bits = size.bit_length() - 1
+    work = total.reshape((2,) * bits + (rows,) + total.shape[1:])
+    for bit in range(bits):
+        shift = 1 << bit
+        upper = (here & shift) != 0
+        place = bits - 1 - bit
+        low = lax.index_in_dim(work, 0, place, keepdims=False)
+        high = lax.index_in_dim(work, 1, place, keepdims=False)
+        keep = jnp.where(upper, high, low)
+        send = jnp.where(upper, low, high)
+        got = lax.ppermute(send, axis, [(j, j ^ shift) for j in range(size)])
+        work = keep + got
+    return work
 
 
 def combine_forward(first_part, second_part):
@@ -117,12 +142,7 @@
     for entry in reversed(blocks):
         bwd_decay = bwd_decay * entry[6]
         bwd_state = entry[12] + entry[6][:, None, None] * bwd_state
-    state_in = prefix(
-        (fwd_decay, fwd_state), "ctx", combine_forward, (unit_decay, zero_state), False
-    )[1]
-    grad_in = prefix(
-        (bwd_decay, bwd_state), "ctx", combine_backward, (unit_decay, zero_state), True
-    )[1]
+    state_in, grad_in = both_prefixes(fwd_decay, fwd_state, bwd_state, "ctx")
     entering = []
     current = state_in
     for entry in blocks:
@@ -156,9 +176,7 @@
     read_carried = jnp.concatenate(read_far, axis=0)
     write_total = jnp.concatenate([entry[9] for entry in blocks], axis=0) + write_carried
     read_total = jnp.concatenate([entry[10] for entry in blocks], axis=0) + read_carried
-    both_grads = lax.psum_scatter(
-        jnp.concatenate([write_total, read_total], axis=1), "head", scatter_dimension=0, tiled=True
-    )
+    both_grads = halving_scatter(jnp.concatenate([write_total, read_total], axis=1), "head")
     write_grad, read_grad = (both_grads[:, :state_width], both_grads[:, state_width:])
     grad_input = (
         (step_size[:, None, :] * back_rows)

time: 246 us -> 165 us (0.67)
  waiting for transfers between devices: 139 us -> 58.4 us
  between operations: 14.6 us -> 1.25 us
  local copies, waits for them, and re-layouts: 5.43 us -> 10.4 us
  matrix products: 9.94 us -> 13.7 us
    reduce_scatter x1 -> x0, waiting for transfers between devices: 79.5 us -> none  [shards(): lax.psum_scatter(jnp.concatenate([write_total, read_total], axis=1), 'hea...]
    unnamed x14 -> x64, local copies, waits for them, and re-layouts: 3.33 us -> 9.37 us
    select_n x0 -> x15, other arithmetic: none -> 3.64 us  [the longest x2 1.38 us: both_prefixes(): after_decay = jnp.where(upper, after_decay, after_decay * got_decay)]
    ppermute x12 -> x10, starting transfers between devices: 71.8 us -> 73.6 us  [the longest x6 55.9 us: both_prefixes(): got = lax.ppermute(packed, axis, pairs)]
    ppermute x12 -> x10, waiting for transfers between devices: 59.8 us -> 58.4 us  [the longest x6 55.5 us: both_prefixes(): got = lax.ppermute(packed, axis, pairs)]
  transfers between devices with their start and end apart: 13 -> 10, of which waited for: 13 -> 8; matrix products, arithmetic and copies ran while one was open for 3% -> 7% of each run, Pallas kernels for 0% -> 0%
where the time goes in v2:
time: 165 us; the launch traced here: 163 us
  starting transfers between devices  73.6 us (45%)
  waiting for transfers between devices  58.4 us (35%)
  matrix products  13.7 us (8%)
  local copies, waits for them, and re-layouts  10.4 us (6%)
  other arithmetic  5.57 us (3%)
    ppermute x6, starting transfers between devices, both_prefixes(): got = lax.ppermute(packed, axis, pairs)  55.9 us
    ppermute x6, waiting for transfers between devices, both_prefixes(): got = lax.ppermute(packed, axis, pairs)  55.5 us
    ppermute x4, starting transfers between devices, halving_scatter(): got = lax.ppermute(send, axis, [(j, j ^ shift) for j in range(size)])  17.7 us
    unnamed x64, local copies, waits for them, and re-layouts  9.37 us
  transfers between devices with their start and end apart: 10, of which 8 were waited for; matrix products, arithmetic and copies ran while one was open for 7% of the time, Pallas kernels for 0%

profile of v2, /device:TPU:1, one launch (start us, length us, event | category | flops | bytes accessed | tf_op | source)
XLA Modules:
  0.0 162.9 jit_solution(1774381899212763845)
XLA Ops:
  0.6 0.9 convolution_bitcast_fusion.8
  2.1 1.1 copy.37
  3.9 0.9 copy-done
  6.6 3.9 %collective-permute-start = (f32[4,129,128]{2,1,0:T(8,128)S(1)}, f32[4,129,128]{2,1,0:T(8,128)S(1)}, u32[]{:S(2)}, u32[]{:S(2)}) collective-permute-start(f32[4,129,128]{2,1,0:T(8,128)S(1)} %pad_maximum_fusion), channel_id=1, source_target_pairs={{0,16},{16,0},{32,48},{48,32},{64,80},{80,64},{96,112},{112,96},{1... | collective-permute-start | bytes 792584 | tf_op jit(solution)/shard_map/ppermute | solution.py:23
  10.6 3.9 %collective-permute-done = f32[4,129,128]{2,1,0:T(8,128)S(1)} collective-permute-done((f32[4,129,128]{2,1,0:T(8,128)S(1)}, f32[4,129,128]{2,1,0:T(8,128)S(1)}, u32[]{:S(2)}, u32[]{:S(2)}) %collective-permute-start) | collective-permute-done | bytes 264224 | tf_op jit(solution)/shard_map/ppermute | solution.py:23
  15.4 7.0 %collective-permute-start.1 = (f32[4,129,128]{2,1,0:T(8,128)S(1)}, f32[4,129,128]{2,1,0:T(8,128)S(1)}, u32[]{:S(2)}, u32[]{:S(2)}) collective-permute-start(f32[4,129,128]{2,1,0:T(8,128)S(1)} %pad_maximum_fusion.1), channel_id=1, source_target_pairs={{0,32},{16,48},{32,0},{48,16},{64,96},{80,112},{96,64},{112,80},{1... | collective-permute-start | bytes 792584 | tf_op jit(solution)/shard_map/ppermute | solution.py:23
  22.4 6.0 %collective-permute-done.1 = f32[4,129,128]{2,1,0:T(8,128)S(1)} collective-permute-done((f32[4,129,128]{2,1,0:T(8,128)S(1)}, f32[4,129,128]{2,1,0:T(8,128)S(1)}, u32[]{:S(2)}, u32[]{:S(2)}) %collective-permute-start.1) | collective-permute-done | bytes 264224 | tf_op jit(solution)/shard_map/ppermute | solution.py:23
  29.3 3.4 %collective-permute-start.2 = (f32[4,129,128]{2,1,0:T(8,128)S(1)}, f32[4,129,128]{2,1,0:T(8,128)S(1)}, u32[]{:S(2)}, u32[]{:S(2)}) collective-permute-start(f32[4,129,128]{2,1,0:T(8,128)S(1)} %pad_maximum_fusion.2), channel_id=1, source_target_pairs={{0,64},{16,80},{32,96},{48,112},{64,0},{80,16},{96,32},{112,48},{1... | collective-permute-start | bytes 792584 | tf_op jit(solution)/shard_map/ppermute | solution.py:23
  33.4 0.9 fusion.83
  34.3 2.4 %collective-permute-done.2 = f32[4,129,128]{2,1,0:T(8,128)S(1)} collective-permute-done((f32[4,129,128]{2,1,0:T(8,128)S(1)}, f32[4,129,128]{2,1,0:T(8,128)S(1)}, u32[]{:S(2)}, u32[]{:S(2)}) %collective-permute-start.2) | collective-permute-done | bytes 264224 | tf_op jit(solution)/shard_map/ppermute | solution.py:23
  37.6 6.5 %collective-permute-start.3 = (f32[4,129,128]{2,1,0:T(8,128)S(1)}, f32[4,129,128]{2,1,0:T(8,128)S(1)}, u32[]{:S(2)}, u32[]{:S(2)}) collective-permute-start(f32[4,129,128]{2,1,0:T(8,128)S(1)} %pad_maximum_fusion.3), channel_id=1, source_target_pairs={{0,128},{16,144},{32,160},{48,176},{64,192},{80,208},{96,224},{112... | collective-permute-start | bytes 792584 | tf_op jit(solution)/shard_map/ppermute | solution.py:23
  44.1 1.3 fusion.2
  45.4 0.8 fusion.77
  46.2 4.9 %collective-permute-done.3 = f32[4,129,128]{2,1,0:T(8,128)S(1)} collective-permute-done((f32[4,129,128]{2,1,0:T(8,128)S(1)}, f32[4,129,128]{2,1,0:T(8,128)S(1)}, u32[]{:S(2)}, u32[]{:S(2)}) %collective-permute-start.3) | collective-permute-done | bytes 264224 | tf_op jit(solution)/shard_map/ppermute | solution.py:23
  52.0 15.8 %collective-permute-start.4 = (f32[4,129,128]{2,1,0:T(8,128)S(1)}, f32[4,129,128]{2,1,0:T(8,128)S(1)}, u32[]{:S(2)}, u32[]{:S(2)}) collective-permute-start(f32[4,129,128]{2,1,0:T(8,128)S(1)} %pad_maximum_fusion.4), channel_id=1, source_target_pairs={{0,256},{16,272},{32,288},{48,304},{64,320},{80,336},{96,352},{112... | collective-permute-start | bytes 792584 | tf_op jit(solution)/shard_map/ppermute | solution.py:23
  67.8 0.9 fusion.88
  68.7 0.8 fusion.94
  69.5 22.3 %collective-permute-done.4 = f32[4,129,128]{2,1,0:T(8,128)S(1)} collective-permute-done((f32[4,129,128]{2,1,0:T(8,128)S(1)}, f32[4,129,128]{2,1,0:T(8,128)S(1)}, u32[]{:S(2)}, u32[]{:S(2)}) %collective-permute-start.4) | collective-permute-done | bytes 264224 | tf_op jit(solution)/shard_map/ppermute | solution.py:23
  91.7 0.7 fusion.101
  93.3 19.2 %collective-permute-start.5 = (f32[4,129,128]{2,1,0:T(8,128)S(1)}, f32[4,129,128]{2,1,0:T(8,128)S(1)}, u32[]{:S(2)}, u32[]{:S(2)}) collective-permute-start(f32[4,129,128]{2,1,0:T(8,128)S(1)} %pad_maximum_fusion.5), channel_id=1, source_target_pairs={{0,512},{16,528},{32,544},{48,560},{64,576},{80,592},{96,608},{112... | collective-permute-start | bytes 792584 | tf_op jit(solution)/shard_map/ppermute | solution.py:23
  112.5 0.9 fusion.91
  113.7 16.1 %collective-permute-done.5 = f32[4,129,128]{2,1,0:T(8,128)S(1)} collective-permute-done((f32[4,129,128]{2,1,0:T(8,128)S(1)}, f32[4,129,128]{2,1,0:T(8,128)S(1)}, u32[]{:S(2)}, u32[]{:S(2)}) %collective-permute-start.5) | collective-permute-done | bytes 264224 | tf_op jit(solution)/shard_map/ppermute | solution.py:23
  135.5 0.8 copy-done.5
  136.5 2.4 %collective-permute-start.6 = (f32[2,2,2,16,256]{4,3,0,1,2:T(8,128)S(1)}, f32[2,2,2,16,256]{4,3,0,1,2:T(8,128)S(1)}, u32[]{:S(2)}, u32[]{:S(2)}) collective-permute-start(f32[2,2,2,16,256]{4,3,0,1,2:T(8,128)S(1)} %select_bitcast_fusion), channel_id=1, source_target_pairs={{0,1},{1,0},{2,3},{3,2},{4,5},{5,4},{6,7},{7,6},{8,9},{9,8},{10,11... | collective-permute-start | bytes 393224 | tf_op jit(solution)/shard_map/ppermute | solution.py:56
  139.7 0.7 fusion.4
  141.6 3.2 %collective-permute-start.7 = (f32[2,2,16,256]{3,2,0,1:T(8,128)S(1)}, f32[2,2,16,256]{3,2,0,1:T(8,128)S(1)}, u32[]{:S(2)}, u32[]{:S(2)}) collective-permute-start(f32[2,2,16,256]{3,2,0,1:T(8,128)S(1)} %select_bitcast_fusion.1), channel_id=1, source_target_pairs={{0,2},{1,3},{2,0},{3,1},{4,6},{5,7},{6,4},{7,5},{8,10},{9,11},{10,... | collective-permute-start | bytes 196616 | tf_op jit(solution)/shard_map/ppermute | solution.py:56
  145.1 2.0 %collective-permute-done.7 = f32[2,2,16,256]{3,2,0,1:T(8,128)S(1)} collective-permute-done((f32[2,2,16,256]{3,2,0,1:T(8,128)S(1)}, f32[2,2,16,256]{3,2,0,1:T(8,128)S(1)}, u32[]{:S(2)}, u32[]{:S(2)}) %collective-permute-start.7) | collective-permute-done | bytes 65568 | tf_op jit(solution)/shard_map/ppermute | solution.py:56
  147.2 4.3 %collective-permute-start.8 = (f32[2,16,256]{2,1,0:T(8,128)S(1)}, f32[2,16,256]{2,1,0:T(8,128)S(1)}, u32[]{:S(2)}, u32[]{:S(2)}) collective-permute-start(f32[2,16,256]{2,1,0:T(8,128)S(1)} %select_bitcast_fusion.2), channel_id=1, source_target_pairs={{0,4},{1,5},{2,6},{3,7},{4,0},{5,1},{6,2},{7,3},{8,12},{9,13},{10,... | collective-permute-start | bytes 98312 | tf_op jit(solution)/shard_map/ppermute | solution.py:56
  151.9 0.8 collective-permute-done.8
  152.7 7.8 %collective-permute-start.9 = (f32[16,256]{1,0:T(8,128)S(1)}, f32[16,256]{1,0:T(8,128)S(1)}, u32[]{:S(2)}, u32[]{:S(2)}) collective-permute-start(f32[16,256]{1,0:T(8,128)S(1)} %select_bitcast_fusion.3), channel_id=1, source_target_pairs={{0,8},{1,9},{2,10},{3,11},{4,12},{5,13},{6,14},{7,15},{8,0},{9,1},... | collective-permute-start | bytes 49160 | tf_op jit(solution)/shard_map/ppermute | solution.py:56
  160.6 0.8 copy.49
  161.4 0.8 copy.48
  (123 shorter events, 17.3 us)
Async XLA Ops:
  0.6 0.9 copy-start.29
  1.5 31.2 %copy-start.10 = (f32[4,128]{1,0:T(4,128)}, f32[4,128]{1,0:T(4,128)S(1)}, u32[]{:S(2)}) copy-start(f32[4,128]{1,0:T(4,128)S(1)} %convolution_bitcast_fusion.8) | copy-start | bytes 6148
  1.7 42.5 %copy-start.12 = (f32[4,128]{1,0:T(4,128)}, f32[4,128]{1,0:T(4,128)S(1)}, u32[]{:S(2)}) copy-start(f32[4,128]{1,0:T(4,128)S(1)} %convolution_bitcast_fusion.9) | copy-start | bytes 6148
  2.0 3.9 %copy-start.16 = (f32[4]{0:T(128)}, f32[4]{0:T(128)S(1)}, u32[]{:S(2)}) copy-start(f32[4]{0:T(128)S(1)} %get-tuple-element.88) | copy-start | bytes 52
  2.0 4.2 %copy-start.14 = (f32[4]{0:T(128)}, f32[4]{0:T(128)S(1)}, u32[]{:S(2)}) copy-start(f32[4]{0:T(128)S(1)} %get-tuple-element.90) | copy-start | bytes 52
  2.0 1.1 copy-start.3
  3.2 0.7 copy-start.9
  3.9 0.9 copy-start
  4.8 0.9 copy-start.1
  6.6 7.9 %collective-permute-start = (f32[4,129,128]{2,1,0:T(8,128)S(1)}, f32[4,129,128]{2,1,0:T(8,128)S(1)}, u32[]{:S(2)}, u32[]{:S(2)}) collective-permute-start(f32[4,129,128]{2,1,0:T(8,128)S(1)} %pad_maximum_fusion), channel_id=1, source_target_pairs={{0,16},{16,0},{32,48},{48,32},{64,80},{80,64},{96,112},{112,96},{1... | collective-permute-start | bytes 792584 | tf_op jit(solution)/shard_map/ppermute | solution.py:23
  15.4 13.1 %collective-permute-start.1 = (f32[4,129,128]{2,1,0:T(8,128)S(1)}, f32[4,129,128]{2,1,0:T(8,128)S(1)}, u32[]{:S(2)}, u32[]{:S(2)}) collective-permute-start(f32[4,129,128]{2,1,0:T(8,128)S(1)} %pad_maximum_fusion.1), channel_id=1, source_target_pairs={{0,32},{16,48},{32,0},{48,16},{64,96},{80,112},{96,64},{112,80},{1... | collective-permute-start | bytes 792584 | tf_op jit(solution)/shard_map/ppermute | solution.py:23
  29.3 7.3 %collective-permute-start.2 = (f32[4,129,128]{2,1,0:T(8,128)S(1)}, f32[4,129,128]{2,1,0:T(8,128)S(1)}, u32[]{:S(2)}, u32[]{:S(2)}) collective-permute-start(f32[4,129,128]{2,1,0:T(8,128)S(1)} %pad_maximum_fusion.2), channel_id=1, source_target_pairs={{0,64},{16,80},{32,96},{48,112},{64,0},{80,16},{96,32},{112,48},{1... | collective-permute-start | bytes 792584 | tf_op jit(solution)/shard_map/ppermute | solution.py:23
  37.6 13.6 %collective-permute-start.3 = (f32[4,129,128]{2,1,0:T(8,128)S(1)}, f32[4,129,128]{2,1,0:T(8,128)S(1)}, u32[]{:S(2)}, u32[]{:S(2)}) collective-permute-start(f32[4,129,128]{2,1,0:T(8,128)S(1)} %pad_maximum_fusion.3), channel_id=1, source_target_pairs={{0,128},{16,144},{32,160},{48,176},{64,192},{80,208},{96,224},{112... | collective-permute-start | bytes 792584 | tf_op jit(solution)/shard_map/ppermute | solution.py:23
  51.9 15.8 %copy-start.2 = (f32[128,128]{0,1:T(8,128)S(1)}, f32[128,128]{0,1:T(8,128)}, u32[]{:S(2)}) copy-start(f32[128,128]{0,1:T(8,128)} %fusion.2) | copy-start | bytes 196612
  52.0 39.8 %collective-permute-start.4 = (f32[4,129,128]{2,1,0:T(8,128)S(1)}, f32[4,129,128]{2,1,0:T(8,128)S(1)}, u32[]{:S(2)}, u32[]{:S(2)}) collective-permute-start(f32[4,129,128]{2,1,0:T(8,128)S(1)} %pad_maximum_fusion.4), channel_id=1, source_target_pairs={{0,256},{16,272},{32,288},{48,304},{64,320},{80,336},{96,352},{112... | collective-permute-start | bytes 792584 | tf_op jit(solution)/shard_map/ppermute | solution.py:23
  93.3 36.5 %collective-permute-start.5 = (f32[4,129,128]{2,1,0:T(8,128)S(1)}, f32[4,129,128]{2,1,0:T(8,128)S(1)}, u32[]{:S(2)}, u32[]{:S(2)}) collective-permute-start(f32[4,129,128]{2,1,0:T(8,128)S(1)} %pad_maximum_fusion.5), channel_id=1, source_target_pairs={{0,512},{16,528},{32,544},{48,560},{64,576},{80,592},{96,608},{112... | collective-permute-start | bytes 792584 | tf_op jit(solution)/shard_map/ppermute | solution.py:23
  113.4 16.4 %copy-start.25 = (f32[4]{0:T(128)S(1)}, f32[4]{0:T(128)}, u32[]{:S(2)}) copy-start(f32[4]{0:T(128)} %get-tuple-element.39) | copy-start | bytes 52
  113.4 16.4 %copy-start.27 = (f32[4]{0:T(128)S(1)}, f32[4]{0:T(128)}, u32[]{:S(2)}) copy-start(f32[4]{0:T(128)} %get-tuple-element.37) | copy-start | bytes 52
  131.9 0.7 copy-start.19
  131.9 0.7 copy-start.22
  132.6 0.7 copy-start.17
  134.6 0.8 copy-start.4
  134.7 0.9 copy-start.6
  135.5 0.8 copy-start.5
  135.5 0.9 copy-start.7
  136.4 2.5 %copy-start.8 = (f32[128,128]{0,1:T(8,128)S(1)}, f32[128,128]{0,1:T(8,128)}, u32[]{:S(2)}) copy-start(f32[128,128]{0,1:T(8,128)} %fusion.91) | copy-start | bytes 196612
  136.4 2.5 %copy-start.13 = (f32[4,128]{1,0:T(4,128)S(1)}, f32[4,128]{1,0:T(4,128)}, u32[]{:S(2)}) copy-start(f32[4,128]{1,0:T(4,128)} %copy-done.12) | copy-start | bytes 6148
  136.5 3.2 %copy-start.11 = (f32[4,128]{1,0:T(4,128)S(1)}, f32[4,128]{1,0:T(4,128)}, u32[]{:S(2)}) copy-start(f32[4,128]{1,0:T(4,128)} %copy-done.10) | copy-start | bytes 6148
  136.5 5.0 %collective-permute-start.6 = (f32[2,2,2,16,256]{4,3,0,1,2:T(8,128)S(1)}, f32[2,2,2,16,256]{4,3,0,1,2:T(8,128)S(1)}, u32[]{:S(2)}, u32[]{:S(2)}) collective-permute-start(f32[2,2,2,16,256]{4,3,0,1,2:T(8,128)S(1)} %select_bitcast_fusion), channel_id=1, source_target_pairs={{0,1},{1,0},{2,3},{3,2},{4,5},{5,4},{6,7},{7,6},{8,9},{9,8},{10,11... | collective-permute-start | bytes 393224 | tf_op jit(solution)/shard_map/ppermute | solution.py:56
  141.6 5.5 %collective-permute-start.7 = (f32[2,2,16,256]{3,2,0,1:T(8,128)S(1)}, f32[2,2,16,256]{3,2,0,1:T(8,128)S(1)}, u32[]{:S(2)}, u32[]{:S(2)}) collective-permute-start(f32[2,2,16,256]{3,2,0,1:T(8,128)S(1)} %select_bitcast_fusion.1), channel_id=1, source_target_pairs={{0,2},{1,3},{2,0},{3,1},{4,6},{5,7},{6,4},{7,5},{8,10},{9,11},{10,... | collective-permute-start | bytes 196616 | tf_op jit(solution)/shard_map/ppermute | solution.py:56
  147.2 5.6 %collective-permute-start.8 = (f32[2,16,256]{2,1,0:T(8,128)S(1)}, f32[2,16,256]{2,1,0:T(8,128)S(1)}, u32[]{:S(2)}, u32[]{:S(2)}) collective-permute-start(f32[2,16,256]{2,1,0:T(8,128)S(1)} %select_bitcast_fusion.2), channel_id=1, source_target_pairs={{0,4},{1,5},{2,6},{3,7},{4,0},{5,1},{6,2},{7,3},{8,12},{9,13},{10,... | collective-permute-start | bytes 98312 | tf_op jit(solution)/shard_map/ppermute | solution.py:56
  152.7 9.5 %collective-permute-start.9 = (f32[16,256]{1,0:T(8,128)S(1)}, f32[16,256]{1,0:T(8,128)S(1)}, u32[]{:S(2)}, u32[]{:S(2)}) collective-permute-start(f32[16,256]{1,0:T(8,128)S(1)} %select_bitcast_fusion.3), channel_id=1, source_target_pairs={{0,8},{1,9},{2,10},{3,11},{4,12},{5,13},{6,14},{7,15},{8,0},{9,1},... | collective-permute-start | bytes 49160 | tf_op jit(solution)/shard_map/ppermute | solution.py:56
  (8 other events, 5.0 us)

commit v3 on v2

--- a/solution.py
+++ b/solution.py
@@ -6,38 +6,81 @@
 GROUP = 128
 
 
-def both_prefixes(decay, fwd_state, bwd_state, axis):
-    size, here = (lax.axis_size(axis), lax.axis_index(axis))
-    unit = jnp.ones_like(decay)
-    zero = jnp.zeros_like(fwd_state)
-    before_decay, before_state = (unit, zero)
-    after_decay, after_state = (unit, zero)
-    span_decay, span_fwd, span_bwd = (decay, fwd_state, bwd_state)
-    extra = decay.shape[:1] + (1,) + fwd_state.shape[2:]
-    shift = 1
-    while shift < size:
+def butterfly_rounds(shifts, size, here, span, before, after, final):
+    span_decay, span_fwd, span_bwd = span
+    before_decay, before_state = before
+    after_decay, after_state = after
+    width = span_fwd.shape[1]
+    extra = span_decay.shape[:1] + (1,) + span_fwd.shape[2:]
+    for at, shift in enumerate(shifts):
+        last = final and at == len(shifts) - 1
+        upper = (here & shift) != 0
         pairs = [(j, j ^ shift) for j in range(size)]
-        packed = jnp.concatenate(
-            [span_fwd, span_bwd, jnp.broadcast_to(span_decay[:, None, None], extra)], axis=1
-        )
-        got = lax.ppermute(packed, axis, pairs)
-        width = fwd_state.shape[1]
-        got_fwd, got_bwd, got_decay = (got[:, :width], got[:, width : 2 * width], got[:, -1, 0])
-        upper = (here & shift) != 0
+        tail = jnp.broadcast_to(span_decay[:, None, None], extra)
+        if last:
+            packed = jnp.concatenate([jnp.where(upper, span_bwd, span_fwd), tail], axis=1)
+        else:
+            packed = jnp.concatenate([span_fwd, span_bwd, tail], axis=1)
+        got = lax.ppermute(packed, "ctx", pairs)
+        got_decay = got[:, -1, 0]
+        if last:
+            got_fwd = got_bwd = got[:, :width]
+        else:
+            got_fwd, got_bwd = (got[:, :width], got[:, width : 2 * width])
         scale = before_decay[:, None, None]
         before_state = jnp.where(upper, before_state + scale * got_fwd, before_state)
         before_decay = jnp.where(upper, before_decay * got_decay, before_decay)
         scale = after_decay[:, None, None]
         after_state = jnp.where(upper, after_state, after_state + scale * got_bwd)
         after_decay = jnp.where(upper, after_decay, after_decay * got_decay)
-        if shift * 2 < size:
+        if not last:
             mine = span_decay[:, None, None]
             theirs = got_decay[:, None, None]
             span_fwd = jnp.where(upper, span_fwd + mine * got_fwd, got_fwd + theirs * span_fwd)
             span_bwd = jnp.where(upper, got_bwd + theirs * span_bwd, span_bwd + mine * got_bwd)
             span_decay = span_decay * got_decay
+    return ((span_decay, span_fwd, span_bwd), (before_decay, before_state), (after_decay, after_state))
+
+
+def both_prefixes(decay, fwd_state, bwd_state, axis):
+    size, here = (lax.axis_size(axis), lax.axis_index(axis))
+    heads = decay.shape[0]
+    unit = jnp.ones_like(decay)
+    zero = jnp.zeros_like(fwd_state)
+    inner = 1
+    while inner < heads and inner < size:
+        inner *= 2
+    inner_shifts = []
+    shift = 1
+    while shift < inner:
+        inner_shifts.append(shift)
         shift *= 2
-    return (before_state, after_state)
+    outer_shifts = []
+    while shift < size:
+        outer_shifts.append(shift)
+        shift *= 2
+    span, before, after = butterfly_rounds(
+        inner_shifts, size, here, (decay, fwd_state, bwd_state), (unit, zero), (unit, zero), False
+    )
+    part = heads // inner
+    slot = here % inner
+    span = jax.tree.map(lambda a: lax.dynamic_slice_in_dim(a, slot * part, part, axis=0), span)
+    unit_part = jnp.ones_like(span[0])
+    zero_part = jnp.zeros_like(span[1])
+    _, outer_before, outer_after = butterfly_rounds(
+        outer_shifts, size, here, span, (unit_part, zero_part), (unit_part, zero_part), True
+    )
+    shared = jnp.concatenate([outer_before[1], outer_after[1]], axis=1)
+    for shift in inner_shifts:
+        upper = (here & shift) != 0
+        got = lax.ppermute(shared, axis, [(j, j ^ shift) for j in range(size)])
+        shared = jnp.where(
+            upper, jnp.concatenate([got, shared], axis=0), jnp.concatenate([shared, got], axis=0)
+        )
+    width = fwd_state.shape[1]
+    state_in = before[1] + before[0][:, None, None] * shared[:, :width]
+    grad_in = after[1] + after[0][:, None, None] * shared[:, width:]
+    return (state_in, grad_in)
 
 
 def halving_scatter(total, axis):

time: 165 us -> 137 us (0.83)
  waiting for transfers between devices: 58.4 us -> 25.4 us
  between operations: 1.25 us -> 7.74 us
  matrix products: 13.7 us -> 9.98 us
  other arithmetic: 5.57 us -> 7.33 us
    ppermute x6 -> x8, waiting for transfers between devices: 55.5 us -> 17.4 us  [the longest x6 13.2 us: butterfly_rounds(): got = lax.ppermute(packed, 'ctx', pairs)]
    ppermute x4, waiting for transfers between devices: 2.85 us -> 7.98 us  [halving_scatter(): got = lax.ppermute(send, axis, [(j, j ^ shift) for j in range(size)])]
    ppermute x4, starting transfers between devices: 17.7 us -> 22.1 us  [halving_scatter(): got = lax.ppermute(send, axis, [(j, j ^ shift) for j in range(size)])]
    unnamed x64 -> x14, local copies, waits for them, and re-layouts: 9.37 us -> 5 us
    ppermute x6 -> x8, starting transfers between devices: 55.9 us -> 52.2 us  [the longest x6 44.5 us: butterfly_rounds(): got = lax.ppermute(packed, 'ctx', pairs)]
    select_n x11, other arithmetic: 3.59 us -> 5.68 us  [the longest x4 3.4 us: butterfly_rounds(): jnp.where(upper, got_bwd + theirs * span_bwd, span_bwd + mine * got_bwd)]
    dynamic_slice x0 -> x3, local copies, waits for them, and re-layouts: none -> 1.76 us  [both_prefixes(): lax.dynamic_slice_in_dim(a, slot * part, part, axis=0)]
  transfers between devices with their start and end apart: 10 -> 12, of which waited for: 8 -> 10; matrix products, arithmetic and copies ran while one was open for 7% -> 6% of each run, Pallas kernels for 0% -> 0%
where the time goes in v3:
time: 137 us; the launch traced here: 135 us
  starting transfers between devices  74.4 us (54%)
  waiting for transfers between devices  25.4 us (19%)
  matrix products  9.98 us (7%)
  local copies, waits for them, and re-layouts  9.73 us (7%)
  between operations  7.74 us (6%)
  other arithmetic  7.33 us (5%)
    ppermute x6, starting transfers between devices, butterfly_rounds(): got = lax.ppermute(packed, 'ctx', pairs)  44.5 us
    ppermute x4, starting transfers between devices, halving_scatter(): got = lax.ppermute(send, axis, [(j, j ^ shift) for j in range(size)])  22.1 us
    ppermute x6, waiting for transfers between devices, butterfly_rounds(): got = lax.ppermute(packed, 'ctx', pairs)  13.2 us
    ppermute x4, waiting for transfers between devices, halving_scatter(): got = lax.ppermute(send, axis, [(j, j ^ shift) for j in range(size)])  7.98 us
    ppermute x2, starting transfers between devices, both_prefixes(): got = lax.ppermute(shared, axis, [(j, j ^ shift) for j in range(size)])  7.77 us
    unnamed x14, local copies, waits for them, and re-layouts  5 us
    ppermute x2, waiting for transfers between devices, both_prefixes(): got = lax.ppermute(shared, axis, [(j, j ^ shift) for j in range(size)])  4.22 us
    select_n x4, other arithmetic, butterfly_rounds(): jnp.where(upper, got_bwd + theirs * span_bwd, span_bwd + mine * got_bwd)  3.4 us
  transfers between devices with their start and end apart: 12, of which 10 were waited for; matrix products, arithmetic and copies ran while one was open for 6% of the time, Pallas kernels for 0%

profile of v3, /device:TPU:1, one launch (start us, length us, event | category | flops | bytes accessed | tf_op | source)
XLA Modules:
  0.0 134.5 jit_solution(12372587271805351459)
XLA Ops:
  0.6 0.9 convolution_bitcast_fusion.8
  2.0 1.1 copy.37
  3.9 0.9 copy-done
  6.6 3.9 %collective-permute-start = (f32[4,129,128]{2,1,0:T(8,128)S(1)}, f32[4,129,128]{2,1,0:T(8,128)S(1)}, u32[]{:S(2)}, u32[]{:S(2)}) collective-permute-start(f32[4,129,128]{2,1,0:T(8,128)S(1)} %pad_maximum_fusion), channel_id=1, source_target_pairs={{0,16},{16,0},{32,48},{48,32},{64,80},{80,64},{96,112},{112,96},{1... | collective-permute-start | bytes 792584 | tf_op jit(solution)/shard_map/ppermute | solution.py:24
  10.8 3.7 %collective-permute-done = f32[4,129,128]{2,1,0:T(8,128)S(1)} collective-permute-done((f32[4,129,128]{2,1,0:T(8,128)S(1)}, f32[4,129,128]{2,1,0:T(8,128)S(1)}, u32[]{:S(2)}, u32[]{:S(2)}) %collective-permute-start) | collective-permute-done | bytes 264224 | tf_op jit(solution)/shard_map/ppermute | solution.py:24
  14.8 7.0 %collective-permute-start.1 = (f32[4,129,128]{2,1,0:T(8,128)S(1)}, f32[4,129,128]{2,1,0:T(8,128)S(1)}, u32[]{:S(2)}, u32[]{:S(2)}) collective-permute-start(f32[4,129,128]{2,1,0:T(8,128)S(1)} %pad_maximum_fusion.1), channel_id=1, source_target_pairs={{0,32},{16,48},{32,0},{48,16},{64,96},{80,112},{96,64},{112,80},{1... | collective-permute-start | bytes 792584 | tf_op jit(solution)/shard_map/ppermute | solution.py:24
  22.1 5.2 %collective-permute-done.1 = f32[4,129,128]{2,1,0:T(8,128)S(1)} collective-permute-done((f32[4,129,128]{2,1,0:T(8,128)S(1)}, f32[4,129,128]{2,1,0:T(8,128)S(1)}, u32[]{:S(2)}, u32[]{:S(2)}) %collective-permute-start.1) | collective-permute-done | bytes 264224 | tf_op jit(solution)/shard_map/ppermute | solution.py:24
  28.6 1.3 add_select_fusion.14
  29.9 1.3 add_select_fusion.15
  32.6 4.0 %collective-permute-start.2 = (f32[1,129,128]{2,1,0:T(8,128)S(1)}, f32[1,129,128]{2,1,0:T(8,128)S(1)}, u32[]{:S(2)}, u32[]{:S(2)}) collective-permute-start(f32[1,129,128]{2,1,0:T(8,128)S(1)} %maximum_maximum_fusion), channel_id=1, source_target_pairs={{0,64},{16,80},{32,96},{48,112},{64,0},{80,16},{96,32},{112,48},{1... | collective-permute-start | bytes 198152 | tf_op jit(solution)/shard_map/ppermute | solution.py:24
  37.2 1.3 collective-permute-done.2
  40.4 1.3 add_select_fusion.12
  41.8 5.5 %collective-permute-start.3 = (f32[1,129,128]{2,1,0:T(8,128)S(1)}, f32[1,129,128]{2,1,0:T(8,128)S(1)}, u32[]{:S(2)}, u32[]{:S(2)}) collective-permute-start(f32[1,129,128]{2,1,0:T(8,128)S(1)} %maximum_maximum_fusion.1), channel_id=1, source_target_pairs={{0,128},{16,144},{32,160},{48,176},{64,192},{80,208},{96,224},{112... | collective-permute-start | bytes 198152 | tf_op jit(solution)/shard_map/ppermute | solution.py:24
  47.5 1.6 %collective-permute-done.3 = f32[1,129,128]{2,1,0:T(8,128)S(1)} collective-permute-done((f32[1,129,128]{2,1,0:T(8,128)S(1)}, f32[1,129,128]{2,1,0:T(8,128)S(1)}, u32[]{:S(2)}, u32[]{:S(2)}) %collective-permute-start.3) | collective-permute-done | bytes 66080 | tf_op jit(solution)/shard_map/ppermute | solution.py:24
  51.0 10.5 %collective-permute-start.4 = (f32[1,129,128]{2,1,0:T(8,128)S(1)}, f32[1,129,128]{2,1,0:T(8,128)S(1)}, u32[]{:S(2)}, u32[]{:S(2)}) collective-permute-start(f32[1,129,128]{2,1,0:T(8,128)S(1)} %maximum_maximum_fusion.2), channel_id=1, source_target_pairs={{0,256},{16,272},{32,288},{48,304},{64,320},{80,336},{96,352},{112... | collective-permute-start | bytes 198152 | tf_op jit(solution)/shard_map/ppermute | solution.py:24
  61.8 1.4 %collective-permute-done.4 = f32[1,129,128]{2,1,0:T(8,128)S(1)} collective-permute-done((f32[1,129,128]{2,1,0:T(8,128)S(1)}, f32[1,129,128]{2,1,0:T(8,128)S(1)}, u32[]{:S(2)}, u32[]{:S(2)}) %collective-permute-start.4) | collective-permute-done | bytes 66080 | tf_op jit(solution)/shard_map/ppermute | solution.py:24
  65.1 13.5 %collective-permute-start.5 = (f32[1,65,128]{2,1,0:T(8,128)S(1)}, f32[1,65,128]{2,1,0:T(8,128)S(1)}, u32[]{:S(2)}, u32[]{:S(2)}) collective-permute-start(f32[1,65,128]{2,1,0:T(8,128)S(1)} %concatenate.60), channel_id=1, source_target_pairs={{0,512},{16,528},{32,544},{48,560},{64,576},{80,592},{96,608},{112... | collective-permute-start | bytes 99848 | tf_op jit(solution)/shard_map/ppermute | solution.py:24
  83.2 3.1 %collective-permute-start.6 = (f32[1,128,128]{2,1,0:T(8,128)S(1)}, f32[1,128,128]{2,1,0:T(8,128)S(1)}, u32[]{:S(2)}, u32[]{:S(2)}) collective-permute-start(f32[1,128,128]{2,1,0:T(8,128)S(1)} %pad_maximum_fusion.5), channel_id=1, source_target_pairs={{0,16},{16,0},{32,48},{48,32},{64,80},{80,64},{96,112},{112,96},{1... | collective-permute-start | bytes 196616 | tf_op jit(solution)/shard_map/ppermute | solution.py:76
  86.6 2.0 %collective-permute-done.6 = f32[1,128,128]{2,1,0:T(8,128)S(1)} collective-permute-done((f32[1,128,128]{2,1,0:T(8,128)S(1)}, f32[1,128,128]{2,1,0:T(8,128)S(1)}, u32[]{:S(2)}, u32[]{:S(2)}) %collective-permute-start.6) | collective-permute-done | bytes 65568 | tf_op jit(solution)/shard_map/ppermute | solution.py:76
  88.5 4.6 %collective-permute-start.7 = (f32[2,128,128]{2,1,0:T(8,128)S(1)}, f32[2,128,128]{2,1,0:T(8,128)S(1)}, u32[]{:S(2)}, u32[]{:S(2)}) collective-permute-start(f32[2,128,128]{2,1,0:T(8,128)S(1)} %maximum_select_fusion.1), channel_id=1, source_target_pairs={{0,32},{16,48},{32,0},{48,16},{64,96},{80,112},{96,64},{112,80},{1... | collective-permute-start | bytes 393224 | tf_op jit(solution)/shard_map/ppermute | solution.py:76
  93.5 2.3 %collective-permute-done.7 = f32[2,128,128]{2,1,0:T(8,128)S(1)} collective-permute-done((f32[2,128,128]{2,1,0:T(8,128)S(1)}, f32[2,128,128]{2,1,0:T(8,128)S(1)}, u32[]{:S(2)}, u32[]{:S(2)}) %collective-permute-start.7) | collective-permute-done | bytes 131104 | tf_op jit(solution)/shard_map/ppermute | solution.py:76
  98.6 12.8 %collective-permute-start.8 = (f32[2,2,2,16,256]{4,3,0,1,2:T(8,128)S(1)}, f32[2,2,2,16,256]{4,3,0,1,2:T(8,128)S(1)}, u32[]{:S(2)}, u32[]{:S(2)}) collective-permute-start(f32[2,2,2,16,256]{4,3,0,1,2:T(8,128)S(1)} %select_bitcast_fusion), channel_id=1, source_target_pairs={{0,1},{1,0},{2,3},{3,2},{4,5},{5,4},{6,7},{7,6},{8,9},{9,8},{10,11... | collective-permute-start | bytes 393224 | tf_op jit(solution)/shard_map/ppermute | solution.py:99
  111.4 0.7 fusion.4
  112.1 0.7 fusion.5
  114.0 1.9 %collective-permute-start.9 = (f32[2,2,16,256]{3,2,0,1:T(8,128)S(1)}, f32[2,2,16,256]{3,2,0,1:T(8,128)S(1)}, u32[]{:S(2)}, u32[]{:S(2)}) collective-permute-start(f32[2,2,16,256]{3,2,0,1:T(8,128)S(1)} %select_bitcast_fusion.1), channel_id=1, source_target_pairs={{0,2},{1,3},{2,0},{3,1},{4,6},{5,7},{6,4},{7,5},{8,10},{9,11},{10,... | collective-permute-start | bytes 196616 | tf_op jit(solution)/shard_map/ppermute | solution.py:99
  116.2 3.3 %collective-permute-done.9 = f32[2,2,16,256]{3,2,0,1:T(8,128)S(1)} collective-permute-done((f32[2,2,16,256]{3,2,0,1:T(8,128)S(1)}, f32[2,2,16,256]{3,2,0,1:T(8,128)S(1)}, u32[]{:S(2)}, u32[]{:S(2)}) %collective-permute-start.9) | collective-permute-done | bytes 65568 | tf_op jit(solution)/shard_map/ppermute | solution.py:99
  119.6 2.1 %collective-permute-start.10 = (f32[2,16,256]{2,1,0:T(8,128)S(1)}, f32[2,16,256]{2,1,0:T(8,128)S(1)}, u32[]{:S(2)}, u32[]{:S(2)}) collective-permute-start(f32[2,16,256]{2,1,0:T(8,128)S(1)} %select_bitcast_fusion.2), channel_id=1, source_target_pairs={{0,4},{1,5},{2,6},{3,7},{4,0},{5,1},{6,2},{7,3},{8,12},{9,13},{10,... | collective-permute-start | bytes 98312 | tf_op jit(solution)/shard_map/ppermute | solution.py:99
  122.2 3.3 %collective-permute-done.10 = f32[2,16,256]{2,1,0:T(8,128)S(1)} collective-permute-done((f32[2,16,256]{2,1,0:T(8,128)S(1)}, f32[2,16,256]{2,1,0:T(8,128)S(1)}, u32[]{:S(2)}, u32[]{:S(2)}) %collective-permute-start.10) | collective-permute-done | bytes 32800 | tf_op jit(solution)/shard_map/ppermute | solution.py:99
  125.5 5.3 %collective-permute-start.11 = (f32[16,256]{1,0:T(8,128)S(1)}, f32[16,256]{1,0:T(8,128)S(1)}, u32[]{:S(2)}, u32[]{:S(2)}) collective-permute-start(f32[16,256]{1,0:T(8,128)S(1)} %select_bitcast_fusion.3), channel_id=1, source_target_pairs={{0,8},{1,9},{2,10},{3,11},{4,12},{5,13},{6,14},{7,15},{8,0},{9,1},... | collective-permute-start | bytes 49160 | tf_op jit(solution)/shard_map/ppermute | solution.py:99
  130.9 0.8 copy.48
  131.7 0.8 copy.49
  132.5 1.3 collective-permute-done.11
  (83 shorter events, 17.2 us)
Async XLA Ops:
  0.6 0.9 copy-start.4
  2.0 1.1 copy-start.2
  3.2 0.7 copy-start.3
  3.9 0.9 copy-start
  4.8 0.9 copy-start.1
  6.6 7.9 %collective-permute-start = (f32[4,129,128]{2,1,0:T(8,128)S(1)}, f32[4,129,128]{2,1,0:T(8,128)S(1)}, u32[]{:S(2)}, u32[]{:S(2)}) collective-permute-start(f32[4,129,128]{2,1,0:T(8,128)S(1)} %pad_maximum_fusion), channel_id=1, source_target_pairs={{0,16},{16,0},{32,48},{48,32},{64,80},{80,64},{96,112},{112,96},{1... | collective-permute-start | bytes 792584 | tf_op jit(solution)/shard_map/ppermute | solution.py:24
  14.8 12.5 %collective-permute-start.1 = (f32[4,129,128]{2,1,0:T(8,128)S(1)}, f32[4,129,128]{2,1,0:T(8,128)S(1)}, u32[]{:S(2)}, u32[]{:S(2)}) collective-permute-start(f32[4,129,128]{2,1,0:T(8,128)S(1)} %pad_maximum_fusion.1), channel_id=1, source_target_pairs={{0,32},{16,48},{32,0},{48,16},{64,96},{80,112},{96,64},{112,80},{1... | collective-permute-start | bytes 792584 | tf_op jit(solution)/shard_map/ppermute | solution.py:24
  32.6 5.9 %collective-permute-start.2 = (f32[1,129,128]{2,1,0:T(8,128)S(1)}, f32[1,129,128]{2,1,0:T(8,128)S(1)}, u32[]{:S(2)}, u32[]{:S(2)}) collective-permute-start(f32[1,129,128]{2,1,0:T(8,128)S(1)} %maximum_maximum_fusion), channel_id=1, source_target_pairs={{0,64},{16,80},{32,96},{48,112},{64,0},{80,16},{96,32},{112,48},{1... | collective-permute-start | bytes 198152 | tf_op jit(solution)/shard_map/ppermute | solution.py:24
  41.8 7.3 %collective-permute-start.3 = (f32[1,129,128]{2,1,0:T(8,128)S(1)}, f32[1,129,128]{2,1,0:T(8,128)S(1)}, u32[]{:S(2)}, u32[]{:S(2)}) collective-permute-start(f32[1,129,128]{2,1,0:T(8,128)S(1)} %maximum_maximum_fusion.1), channel_id=1, source_target_pairs={{0,128},{16,144},{32,160},{48,176},{64,192},{80,208},{96,224},{112... | collective-permute-start | bytes 198152 | tf_op jit(solution)/shard_map/ppermute | solution.py:24
  51.0 12.2 %collective-permute-start.4 = (f32[1,129,128]{2,1,0:T(8,128)S(1)}, f32[1,129,128]{2,1,0:T(8,128)S(1)}, u32[]{:S(2)}, u32[]{:S(2)}) collective-permute-start(f32[1,129,128]{2,1,0:T(8,128)S(1)} %maximum_maximum_fusion.2), channel_id=1, source_target_pairs={{0,256},{16,272},{32,288},{48,304},{64,320},{80,336},{96,352},{112... | collective-permute-start | bytes 198152 | tf_op jit(solution)/shard_map/ppermute | solution.py:24
  65.1 18.1 %collective-permute-start.5 = (f32[1,65,128]{2,1,0:T(8,128)S(1)}, f32[1,65,128]{2,1,0:T(8,128)S(1)}, u32[]{:S(2)}, u32[]{:S(2)}) collective-permute-start(f32[1,65,128]{2,1,0:T(8,128)S(1)} %concatenate.60), channel_id=1, source_target_pairs={{0,512},{16,528},{32,544},{48,560},{64,576},{80,592},{96,608},{112... | collective-permute-start | bytes 99848 | tf_op jit(solution)/shard_map/ppermute | solution.py:24
  83.2 5.3 %collective-permute-start.6 = (f32[1,128,128]{2,1,0:T(8,128)S(1)}, f32[1,128,128]{2,1,0:T(8,128)S(1)}, u32[]{:S(2)}, u32[]{:S(2)}) collective-permute-start(f32[1,128,128]{2,1,0:T(8,128)S(1)} %pad_maximum_fusion.5), channel_id=1, source_target_pairs={{0,16},{16,0},{32,48},{48,32},{64,80},{80,64},{96,112},{112,96},{1... | collective-permute-start | bytes 196616 | tf_op jit(solution)/shard_map/ppermute | solution.py:76
  88.5 7.2 %collective-permute-start.7 = (f32[2,128,128]{2,1,0:T(8,128)S(1)}, f32[2,128,128]{2,1,0:T(8,128)S(1)}, u32[]{:S(2)}, u32[]{:S(2)}) collective-permute-start(f32[2,128,128]{2,1,0:T(8,128)S(1)} %maximum_select_fusion.1), channel_id=1, source_target_pairs={{0,32},{16,48},{32,0},{48,16},{64,96},{80,112},{96,64},{112,80},{1... | collective-permute-start | bytes 393224 | tf_op jit(solution)/shard_map/ppermute | solution.py:76
  98.6 15.4 %collective-permute-start.8 = (f32[2,2,2,16,256]{4,3,0,1,2:T(8,128)S(1)}, f32[2,2,2,16,256]{4,3,0,1,2:T(8,128)S(1)}, u32[]{:S(2)}, u32[]{:S(2)}) collective-permute-start(f32[2,2,2,16,256]{4,3,0,1,2:T(8,128)S(1)} %select_bitcast_fusion), channel_id=1, source_target_pairs={{0,1},{1,0},{2,3},{3,2},{4,5},{5,4},{6,7},{7,6},{8,9},{9,8},{10,11... | collective-permute-start | bytes 393224 | tf_op jit(solution)/shard_map/ppermute | solution.py:99
  114.0 5.5 %collective-permute-start.9 = (f32[2,2,16,256]{3,2,0,1:T(8,128)S(1)}, f32[2,2,16,256]{3,2,0,1:T(8,128)S(1)}, u32[]{:S(2)}, u32[]{:S(2)}) collective-permute-start(f32[2,2,16,256]{3,2,0,1:T(8,128)S(1)} %select_bitcast_fusion.1), channel_id=1, source_target_pairs={{0,2},{1,3},{2,0},{3,1},{4,6},{5,7},{6,4},{7,5},{8,10},{9,11},{10,... | collective-permute-start | bytes 196616 | tf_op jit(solution)/shard_map/ppermute | solution.py:99
  119.6 5.9 %collective-permute-start.10 = (f32[2,16,256]{2,1,0:T(8,128)S(1)}, f32[2,16,256]{2,1,0:T(8,128)S(1)}, u32[]{:S(2)}, u32[]{:S(2)}) collective-permute-start(f32[2,16,256]{2,1,0:T(8,128)S(1)} %select_bitcast_fusion.2), channel_id=1, source_target_pairs={{0,4},{1,5},{2,6},{3,7},{4,0},{5,1},{6,2},{7,3},{8,12},{9,13},{10,... | collective-permute-start | bytes 98312 | tf_op jit(solution)/shard_map/ppermute | solution.py:99
  125.5 8.4 %collective-permute-start.11 = (f32[16,256]{1,0:T(8,128)S(1)}, f32[16,256]{1,0:T(8,128)S(1)}, u32[]{:S(2)}, u32[]{:S(2)}) collective-permute-start(f32[16,256]{1,0:T(8,128)S(1)} %select_bitcast_fusion.3), channel_id=1, source_target_pairs={{0,8},{1,9},{2,10},{3,11},{4,12},{5,13},{6,14},{7,15},{8,0},{9,1},... | collective-permute-start | bytes 49160 | tf_op jit(solution)/shard_map/ppermute | solution.py:99

commit v4 on v3

--- a/solution.py
+++ b/solution.py
@@ -1,12 +1,12 @@
 import jax
 import jax.numpy as jnp
 from jax import lax
-from jax.sharding import PartitionSpec as P
+from jax.sharding import Mesh, PartitionSpec as P
 
 GROUP = 128
 
 
-def butterfly_rounds(shifts, size, here, span, before, after, final):
+def butterfly_rounds(shifts, size, here, span, before, after, final, axis):
     span_decay, span_fwd, span_bwd = span
     before_decay, before_state = before
     after_decay, after_state = after
@@ -21,7 +21,7 @@
             packed = jnp.concatenate([jnp.where(upper, span_bwd, span_fwd), tail], axis=1)
         else:
             packed = jnp.concatenate([span_fwd, span_bwd, tail], axis=1)
-        got = lax.ppermute(packed, "ctx", pairs)
+        got = lax.ppermute(packed, axis, pairs)
         got_decay = got[:, -1, 0]
         if last:
             got_fwd = got_bwd = got[:, :width]
@@ -42,63 +42,63 @@
     return ((span_decay, span_fwd, span_bwd), (before_decay, before_state), (after_decay, after_state))
 
 
-def both_prefixes(decay, fwd_state, bwd_state, axis):
-    size, here = (lax.axis_size(axis), lax.axis_index(axis))
-    heads = decay.shape[0]
-    unit = jnp.ones_like(decay)
-    zero = jnp.zeros_like(fwd_state)
-    inner = 1
-    while inner < heads and inner < size:
-        inner *= 2
-    inner_shifts = []
+def both_prefixes(decay, fwd_state, bwd_state):
+    outer_size, here = (lax.axis_size("outer"), lax.axis_index("outer"))
+    members = lax.axis_size("inner")
+    width = fwd_state.shape[1]
+    packed = jnp.concatenate(
+        [fwd_state, bwd_state, jnp.broadcast_to(decay[:, None, None], decay.shape[:1] + (1,) + fwd_state.shape[2:])],
+        axis=1,
+    )
+    mine = lax.all_to_all(packed, "inner", 0, 0, tiled=True)
+    part = mine.shape[0] // members
+    rows = mine.reshape((members, part) + mine.shape[1:])
+    fwd_rows, bwd_rows, decay_rows = (rows[:, :, :width], rows[:, :, width : 2 * width], rows[:, :, -1, 0])
+    unit = jnp.ones_like(decay_rows[0])
+    zero = jnp.zeros_like(fwd_rows[0])
+    run_decay, run_state = (unit, zero)
+    before_decays, before_states = ([], [])
+    for m in range(members):
+        before_decays.append(run_decay)
+        before_states.append(run_state)
+        run_state = decay_rows[m][:, None, None] * run_state + fwd_rows[m]
+        run_decay = run_decay * decay_rows[m]
+    group = (run_decay, run_state)
+    run_decay, run_state = (unit, zero)
+    after_decays, after_states = ([None] * members, [None] * members)
+    for m in range(members - 1, -1, -1):
+        after_decays[m] = run_decay
+        after_states[m] = run_state
+        run_state = bwd_rows[m] + decay_rows[m][:, None, None] * run_state
+        run_decay = run_decay * decay_rows[m]
+    shifts = []
     shift = 1
-    while shift < inner:
-        inner_shifts.append(shift)
+    while shift < outer_size:
+        shifts.append(shift)
         shift *= 2
-    outer_shifts = []
-    while shift < size:
-        outer_shifts.append(shift)
-        shift *= 2
-    span, before, after = butterfly_rounds(
-        inner_shifts, size, here, (decay, fwd_state, bwd_state), (unit, zero), (unit, zero), False
-    )
-    part = heads // inner
-    slot = here % inner
-    span = jax.tree.map(lambda a: lax.dynamic_slice_in_dim(a, slot * part, part, axis=0), span)
-    unit_part = jnp.ones_like(span[0])
-    zero_part = jnp.zeros_like(span[1])
     _, outer_before, outer_after = butterfly_rounds(
-        outer_shifts, size, here, span, (unit_part, zero_part), (unit_part, zero_part), True
-    )
-    shared = jnp.concatenate([outer_before[1], outer_after[1]], axis=1)
-    for shift in inner_shifts:
-        upper = (here & shift) != 0
-        got = lax.ppermute(shared, axis, [(j, j ^ shift) for j in range(size)])
-        shared = jnp.where(
-            upper, jnp.concatenate([got, shared], axis=0), jnp.concatenate([shared, got], axis=0)
-        )
-    width = fwd_state.shape[1]
-    state_in = before[1] + before[0][:, None, None] * shared[:, :width]
-    grad_in = after[1] + after[0][:, None, None] * shared[:, width:]
-    return (state_in, grad_in)
-
-
-def halving_scatter(total, axis):
-    size, here = (lax.axis_size(axis), lax.axis_index(axis))
-    rows = total.shape[0] // size
-    bits = size.bit_length() - 1
-    work = total.reshape((2,) * bits + (rows,) + total.shape[1:])
-    for bit in range(bits):
-        shift = 1 << bit
-        upper = (here & shift) != 0
-        place = bits - 1 - bit
-        low = lax.index_in_dim(work, 0, place, keepdims=False)
-        high = lax.index_in_dim(work, 1, place, keepdims=False)
-        keep = jnp.where(upper, high, low)
-        send = jnp.where(upper, low, high)
-        got = lax.ppermute(send, axis, [(j, j ^ shift) for j in range(size)])
-        work = keep + got
-    return work
+        shifts, outer_size, here, (group[0], group[1], run_state), (unit, zero), (unit, zero), True, "outer"
+    )
+    back = jnp.stack(
+        [
+            jnp.concatenate(
+                [
+                    before_states[m] + before_decays[m][:, None, None] * outer_before[1],
+                    after_states[m] + after_decays[m][:, None, None] * outer_after[1],
+                ],
+                axis=1,
+            )
+            for m in range(members)
+        ]
+    )
+    shared = lax.all_to_all(back.reshape((members * part,) + back.shape[2:]), "inner", 0, 0, tiled=True)
+    return (shared[:, :width], shared[:, width:])
+
+
+def head_scatter(total, axis):
+    size = lax.axis_size(axis)
+    pieces = total.reshape((size, total.shape[0] // size) + total.shape[1:])
+    return jnp.sum(lax.all_to_all(pieces, axis, 0, 0), axis=0)
 
 
 def combine_forward(first_part, second_part):
@@ -185,7 +185,7 @@
     for entry in reversed(blocks):
         bwd_decay = bwd_decay * entry[6]
         bwd_state = entry[12] + entry[6][:, None, None] * bwd_state
-    state_in, grad_in = both_prefixes(fwd_decay, fwd_state, bwd_state, "ctx")
+    state_in, grad_in = both_prefixes(fwd_decay, fwd_state, bwd_state)
     entering = []
     current = state_in
     for entry in blocks:
@@ -219,7 +219,7 @@
     read_carried = jnp.concatenate(read_far, axis=0)
     write_total = jnp.concatenate([entry[9] for entry in blocks], axis=0) + write_carried
     read_total = jnp.concatenate([entry[10] for entry in blocks], axis=0) + read_carried
-    both_grads = halving_scatter(jnp.concatenate([write_total, read_total], axis=1), "head")
+    both_grads = head_scatter(jnp.concatenate([write_total, read_total], axis=1), "head")
     write_grad, read_grad = (both_grads[:, :state_width], both_grads[:, state_width:])
     grad_input = (
         (step_size[:, None, :] * back_rows)
@@ -232,24 +232,37 @@
 
 
 def solution(mesh):
-    placed = (
-        P("ctx", "head"),
-        P("head", "ctx"),
-        P("head", "ctx"),
-        P("ctx", None),
-        P("ctx", None),
-        P("ctx", "head"),
-    )
-    return jax.shard_map(
-        shards,
-        mesh=mesh,
-        in_specs=placed,
-        out_specs=(
-            P("ctx", "head"),
-            P("ctx", "head"),
-            P("head", "ctx"),
-            P(("ctx", "head"), None),
-            P(("ctx", "head"), None),
-        ),
-        check_vma=False,
-    )
+    def run(*args):
+        heads_here = args[1].shape[0] // mesh.shape["head"]
+        ctx_count = mesh.shape["ctx"]
+        inner = 1
+        while inner < heads_here and inner < ctx_count and heads_here % (inner * 2) == 0:
+            inner *= 2
+        fine = Mesh(
+            mesh.devices.reshape((ctx_count // inner, inner) + mesh.devices.shape[1:]),
+            ("outer", "inner", "head"),
+        )
+        ctx = ("outer", "inner")
+        placed = (
+            P(ctx, "head"),
+            P("head", ctx),
+            P("head", ctx),
+            P(ctx, None),
+            P(ctx, None),
+            P(ctx, "head"),
+        )
+        return jax.shard_map(
+            shards,
+            mesh=fine,
+            in_specs=placed,
+            out_specs=(
+                P(ctx, "head"),
+                P(ctx, "head"),
+                P("head", ctx),
+                P(ctx + ("head",), None),
+                P(ctx + ("head",), None),
+            ),
+            check_vma=False,
+        )(*args)
+
+    return run

time: 137 us -> 117 us (0.85); the launches traced: 135 us -> 116 us
  starting transfers between devices: 74.4 us -> 56.1 us
  waiting for transfers between devices: 25.4 us -> 19.5 us
  between operations: 7.74 us -> 12.4 us
  other arithmetic: 7.33 us -> 10.5 us
  local copies, waits for them, and re-layouts: 9.73 us -> 8.07 us
    ppermute x12 -> x4, starting transfers between devices: 74.4 us -> 33.8 us  [butterfly_rounds(): got = lax.ppermute(packed, axis, pairs)]
    all_to_all x0 -> x3, starting transfers between devices: none -> 22.3 us  [the longest x1 14.1 us: head_scatter(): return jnp.sum(lax.all_to_all(pieces, axis, 0, 0), axis=0)]
    ppermute x12 -> x4, waiting for transfers between devices: 25.4 us -> 4.19 us  [butterfly_rounds(): got = lax.ppermute(packed, axis, pairs)]
    all_to_all x0 -> x3, waiting for transfers between devices: none -> 15.3 us  [the longest x1 5.65 us: head_scatter(): return jnp.sum(lax.all_to_all(pieces, axis, 0, 0), axis=0)]
    add x5, other arithmetic: 0.2 us -> 5.27 us  [the longest x1 2.61 us: both_prefixes(): run_state = decay_rows[m][:, None, None] * run_state + fwd_rows[m]]
    select_n x4 -> x2, other arithmetic: 3.4 us -> 1.21 us  [butterfly_rounds(): jnp.where(upper, got_bwd + theirs * span_bwd, span_bwd + mine * got_bwd)]
    dynamic_slice x3 -> x0, local copies, waits for them, and re-layouts: 1.76 us -> none  [both_prefixes(): lax.dynamic_slice_in_dim(a, slot * part, part, axis=0)]
    select_n x10 -> x0, other arithmetic: 1.67 us -> none  [the longest x1 1.31 us: butterfly_rounds(): jnp.where(upper, span_fwd + mine * got_fwd, got_fwd + theirs * span_fwd)]
  transfers between devices with their start and end apart: 12 -> 7, of which waited for: 10 -> 6; matrix products, arithmetic and copies ran while one was open for 6% -> 7% of each run, Pallas kernels for 0% -> 0%
where the time goes in v4:
time: 117 us; the launch traced here: 116 us
  starting transfers between devices  56.1 us (48%)
  waiting for transfers between devices  19.5 us (17%)
  between operations  12.4 us (11%)
  other arithmetic  10.5 us (9%)
  matrix products  9.95 us (9%)
  local copies, waits for them, and re-layouts  8.07 us (7%)
    ppermute x4, starting transfers between devices, butterfly_rounds(): got = lax.ppermute(packed, axis, pairs)  33.8 us
    all_to_all x1, starting transfers between devices, head_scatter(): return jnp.sum(lax.all_to_all(pieces, axis, 0, 0), axis=0)  14.1 us
    all_to_all x1, waiting for transfers between devices, head_scatter(): return jnp.sum(lax.all_to_all(pieces, axis, 0, 0), axis=0)  5.65 us
    all_to_all x1, waiting for transfers between devices, both_prefixes(): lax.all_to_all(back.reshape((members * part,) + back.shape[2:]), 'inner',...  5.23 us
    unnamed x14, local copies, waits for them, and re-layouts  5.01 us
    all_to_all x1, starting transfers between devices, both_prefixes(): mine = lax.all_to_all(packed, 'inner', 0, 0, tiled=True)  4.83 us
    all_to_all x1, waiting for transfers between devices, both_prefixes(): mine = lax.all_to_all(packed, 'inner', 0, 0, tiled=True)  4.46 us
    ppermute x4, waiting for transfers between devices, butterfly_rounds(): got = lax.ppermute(packed, axis, pairs)  4.19 us
  transfers between devices with their start and end apart: 7, of which 6 were waited for; matrix products, arithmetic and copies ran while one was open for 7% of the time, Pallas kernels for 0%

profile of v4, /device:TPU:1, one launch (start us, length us, event | category | flops | bytes accessed | tf_op | source)
XLA Modules:
  0.0 116.5 jit_solution(13421095828727360196)
XLA Ops:
  0.6 0.9 convolution_bitcast_fusion.8
  2.1 1.1 copy.45
  3.9 0.9 copy-done
  5.1 0.6 copy-done.1
  6.6 0.7 pad_maximum_fusion
  7.3 4.8 %all-to-all-start = ((f32[4,129,128]{2,1,0:T(8,128)}), f32[4,129,128]{2,1,0:T(8,128)S(1)}, u32[]{:S(2)}, u32[]{:S(2)}) async-start(f32[4,129,128]{2,1,0:T(8,128)} %pad_maximum_fusion), calls=%async_computation | async-start | bytes 557056 | tf_op jit(solution)/shard_map/all_to_all | solution.py:53
  13.3 4.5 %all-to-all-done = f32[4,129,128]{2,1,0:T(8,128)S(1)} async-done(((f32[4,129,128]{2,1,0:T(8,128)}), f32[4,129,128]{2,1,0:T(8,128)S(1)}, u32[]{:S(2)}, u32[]{:S(2)}) %all-to-all-start) | async-done | bytes 264224 | tf_op jit(solution)/shard_map/all_to_all | solution.py:53
  22.2 2.6 %fusion.105 = (f32[1,64,128]{2,1,0:T(8,128)S(1)}, f32[1,64,128]{2,1,0:T(8,128)S(1)}, f32[1,64,128]{2,1,0:T(8,128)S(1)}, f32[1,64,128]{2,1,0:T(8,128)S(1)}) fusion(f32[4,1,129,128]{3,2,1,0:T(8,128)S(1)} %bitcast.182, f32[]{:T(128)} %bitcast.12, f32[]{:T(128)} %bitcast.13, f32[]{:T(128)} %bitcast.16, f32[]{:T(128)} %bitcast.14, f32[]{:T(128)} %bitcast.33, ...), kind=kLoop, calls=%fused_computation.151 | loop fusion | flops 114688 | bytes 393240 | tf_op jit(solution)/shard_map/add | solution.py:64
  24.9 4.1 %collective-permute-start = (f32[1,129,128]{2,1,0:T(8,128)S(1)}, f32[1,129,128]{2,1,0:T(8,128)S(1)}, u32[]{:S(2)}, u32[]{:S(2)}) collective-permute-start(f32[1,129,128]{2,1,0:T(8,128)S(1)} %maximum_maximum_fusion), channel_id=1, source_target_pairs={{0,64},{64,0},{128,192},{192,128},{256,320},{320,256},{384,448},{4... | collective-permute-start | bytes 198152 | tf_op jit(solution)/shard_map/ppermute | solution.py:24
  29.6 1.3 %collective-permute-done = f32[1,129,128]{2,1,0:T(8,128)S(1)} collective-permute-done((f32[1,129,128]{2,1,0:T(8,128)S(1)}, f32[1,129,128]{2,1,0:T(8,128)S(1)}, u32[]{:S(2)}, u32[]{:S(2)}) %collective-permute-start) | collective-permute-done | bytes 66080 | tf_op jit(solution)/shard_map/ppermute | solution.py:24
  32.7 5.5 %collective-permute-start.1 = (f32[1,129,128]{2,1,0:T(8,128)S(1)}, f32[1,129,128]{2,1,0:T(8,128)S(1)}, u32[]{:S(2)}, u32[]{:S(2)}) collective-permute-start(f32[1,129,128]{2,1,0:T(8,128)S(1)} %maximum_maximum_fusion.1), channel_id=1, source_target_pairs={{0,128},{64,192},{128,0},{192,64},{256,384},{320,448},{384,256},{4... | collective-permute-start | bytes 198152 | tf_op jit(solution)/shard_map/ppermute | solution.py:24
  38.5 1.5 %collective-permute-done.1 = f32[1,129,128]{2,1,0:T(8,128)S(1)} collective-permute-done((f32[1,129,128]{2,1,0:T(8,128)S(1)}, f32[1,129,128]{2,1,0:T(8,128)S(1)}, u32[]{:S(2)}, u32[]{:S(2)}) %collective-permute-start.1) | collective-permute-done | bytes 66080 | tf_op jit(solution)/shard_map/ppermute | solution.py:24
  41.1 0.6 add_select_fusion.6
  41.8 10.6 %collective-permute-start.2 = (f32[1,129,128]{2,1,0:T(8,128)S(1)}, f32[1,129,128]{2,1,0:T(8,128)S(1)}, u32[]{:S(2)}, u32[]{:S(2)}) collective-permute-start(f32[1,129,128]{2,1,0:T(8,128)S(1)} %maximum_maximum_fusion.2), channel_id=1, source_target_pairs={{0,256},{64,320},{128,384},{192,448},{256,0},{320,64},{384,128},{4... | collective-permute-start | bytes 198152 | tf_op jit(solution)/shard_map/ppermute | solution.py:24
  52.8 1.4 %collective-permute-done.2 = f32[1,129,128]{2,1,0:T(8,128)S(1)} collective-permute-done((f32[1,129,128]{2,1,0:T(8,128)S(1)}, f32[1,129,128]{2,1,0:T(8,128)S(1)}, u32[]{:S(2)}, u32[]{:S(2)}) %collective-permute-start.2) | collective-permute-done | bytes 66080 | tf_op jit(solution)/shard_map/ppermute | solution.py:24
  55.3 0.6 select_select_fusion
  56.0 13.5 %collective-permute-start.3 = (f32[1,65,128]{2,1,0:T(8,128)S(1)}, f32[1,65,128]{2,1,0:T(8,128)S(1)}, u32[]{:S(2)}, u32[]{:S(2)}) collective-permute-start(f32[1,65,128]{2,1,0:T(8,128)S(1)} %concatenate.53), channel_id=1, source_target_pairs={{0,512},{64,576},{128,640},{192,704},{256,768},{320,832},{384,896}... | collective-permute-start | bytes 99848 | tf_op jit(solution)/shard_map/ppermute | solution.py:24
  75.4 0.7 multiply_add_fusion.6
  76.1 0.7 multiply_add_fusion.7
  76.8 0.7 multiply_add_fusion.5
  77.5 0.7 multiply_add_fusion.4
  78.2 0.7 maximum_bitcast_fusion
  78.9 3.4 %all-to-all-start.1 = ((f32[4,128,128]{2,1,0:T(8,128)}), f32[4,128,128]{2,1,0:T(8,128)S(1)}, u32[]{:S(2)}, u32[]{:S(2)}) async-start(f32[4,128,128]{2,1,0:T(8,128)} %maximum_bitcast_fusion), calls=%async_computation.1 | async-start | bytes 524288 | tf_op jit(solution)/shard_map/all_to_all | solution.py:94
  82.6 5.2 %all-to-all-done.1 = f32[4,128,128]{2,1,0:T(8,128)S(1)} async-done(((f32[4,128,128]{2,1,0:T(8,128)}), f32[4,128,128]{2,1,0:T(8,128)S(1)}, u32[]{:S(2)}, u32[]{:S(2)}) %all-to-all-start.1) | async-done | bytes 262176 | tf_op jit(solution)/shard_map/all_to_all | solution.py:94
  89.5 0.7 pad_maximum_fusion.3
  90.2 14.1 %all-to-all-start.2 = ((f32[16,16,256]{2,1,0:T(8,128)}), f32[16,16,256]{2,1,0:T(8,128)S(1)}, u32[]{:S(2)}, u32[]{:S(2)}) async-start(f32[16,16,256]{2,1,0:T(8,128)} %pad_maximum_fusion.3), calls=%async_computation.2 | async-start | bytes 524288 | tf_op jit(solution)/shard_map/all_to_all | solution.py:101
  104.6 0.7 fusion.5
  105.6 0.7 fusion.4
  106.3 0.6 multiply_reduce_fusion
  107.0 0.8 copy.61
  109.4 0.8 copy.60
  110.2 5.6 %all-to-all-done.2 = f32[16,16,256]{2,1,0:T(8,128)S(1)} async-done(((f32[16,16,256]{2,1,0:T(8,128)}), f32[16,16,256]{2,1,0:T(8,128)S(1)}, u32[]{:S(2)}, u32[]{:S(2)}) %all-to-all-start.2) | async-done | bytes 262176 | tf_op jit(solution)/shard_map/all_to_all | solution.py:101
  (61 shorter events, 12.5 us)
Async XLA Ops:
  0.6 0.9 copy-start.4
  2.1 1.2 copy-start.2
  3.2 0.7 copy-start.3
  3.9 0.9 copy-start
  4.8 0.9 copy-start.1
  7.3 10.5 %all-to-all-start = ((f32[4,129,128]{2,1,0:T(8,128)}), f32[4,129,128]{2,1,0:T(8,128)S(1)}, u32[]{:S(2)}, u32[]{:S(2)}) async-start(f32[4,129,128]{2,1,0:T(8,128)} %pad_maximum_fusion), calls=%async_computation | async-start | bytes 557056 | tf_op jit(solution)/shard_map/all_to_all | solution.py:53
  24.9 6.1 %collective-permute-start = (f32[1,129,128]{2,1,0:T(8,128)S(1)}, f32[1,129,128]{2,1,0:T(8,128)S(1)}, u32[]{:S(2)}, u32[]{:S(2)}) collective-permute-start(f32[1,129,128]{2,1,0:T(8,128)S(1)} %maximum_maximum_fusion), channel_id=1, source_target_pairs={{0,64},{64,0},{128,192},{192,128},{256,320},{320,256},{384,448},{4... | collective-permute-start | bytes 198152 | tf_op jit(solution)/shard_map/ppermute | solution.py:24
  32.7 7.2 %collective-permute-start.1 = (f32[1,129,128]{2,1,0:T(8,128)S(1)}, f32[1,129,128]{2,1,0:T(8,128)S(1)}, u32[]{:S(2)}, u32[]{:S(2)}) collective-permute-start(f32[1,129,128]{2,1,0:T(8,128)S(1)} %maximum_maximum_fusion.1), channel_id=1, source_target_pairs={{0,128},{64,192},{128,0},{192,64},{256,384},{320,448},{384,256},{4... | collective-permute-start | bytes 198152 | tf_op jit(solution)/shard_map/ppermute | solution.py:24
  41.8 12.3 %collective-permute-start.2 = (f32[1,129,128]{2,1,0:T(8,128)S(1)}, f32[1,129,128]{2,1,0:T(8,128)S(1)}, u32[]{:S(2)}, u32[]{:S(2)}) collective-permute-start(f32[1,129,128]{2,1,0:T(8,128)S(1)} %maximum_maximum_fusion.2), channel_id=1, source_target_pairs={{0,256},{64,320},{128,384},{192,448},{256,0},{320,64},{384,128},{4... | collective-permute-start | bytes 198152 | tf_op jit(solution)/shard_map/ppermute | solution.py:24
  56.0 19.4 %collective-permute-start.3 = (f32[1,65,128]{2,1,0:T(8,128)S(1)}, f32[1,65,128]{2,1,0:T(8,128)S(1)}, u32[]{:S(2)}, u32[]{:S(2)}) collective-permute-start(f32[1,65,128]{2,1,0:T(8,128)S(1)} %concatenate.53), channel_id=1, source_target_pairs={{0,512},{64,576},{128,640},{192,704},{256,768},{320,832},{384,896}... | collective-permute-start | bytes 99848 | tf_op jit(solution)/shard_map/ppermute | solution.py:24
  78.9 8.9 %all-to-all-start.1 = ((f32[4,128,128]{2,1,0:T(8,128)}), f32[4,128,128]{2,1,0:T(8,128)S(1)}, u32[]{:S(2)}, u32[]{:S(2)}) async-start(f32[4,128,128]{2,1,0:T(8,128)} %maximum_bitcast_fusion), calls=%async_computation.1 | async-start | bytes 524288 | tf_op jit(solution)/shard_map/all_to_all | solution.py:94
  90.2 25.7 %all-to-all-start.2 = ((f32[16,16,256]{2,1,0:T(8,128)}), f32[16,16,256]{2,1,0:T(8,128)S(1)}, u32[]{:S(2)}, u32[]{:S(2)}) async-start(f32[16,16,256]{2,1,0:T(8,128)} %pad_maximum_fusion.3), calls=%async_computation.2 | async-start | bytes 524288 | tf_op jit(solution)/shard_map/all_to_all | solution.py:101

commit v5 on v4

--- a/solution.py
+++ b/solution.py
@@ -1,3 +1,5 @@
+import functools
+
 import jax
 import jax.numpy as jnp
 from jax import lax
@@ -42,8 +44,46 @@
     return ((span_decay, span_fwd, span_bwd), (before_decay, before_state), (after_decay, after_state))
 
 
-def both_prefixes(decay, fwd_state, bwd_state):
-    outer_size, here = (lax.axis_size("outer"), lax.axis_index("outer"))
+def level_exchange(aggregate, axis, last):
+    count, here = (lax.axis_size(axis), lax.axis_index(axis))
+    decay, fwd, bwd = aggregate
+    width = fwd.shape[1]
+    tail = jnp.broadcast_to(decay[:, None, None], decay.shape[:1] + (1,) + fwd.shape[2:])
+    if last:
+        sent = jnp.stack(
+            [jnp.concatenate([jnp.where(m < here, bwd, fwd), tail], axis=1) for m in range(count)]
+        )
+    else:
+        packed = jnp.concatenate([fwd, bwd, tail], axis=1)
+        sent = jnp.broadcast_to(packed[None], (count,) + packed.shape)
+    got = lax.all_to_all(sent, axis, 0, 0)
+    got_decay = got[:, :, -1, 0]
+    got_fwd = got[:, :, :width]
+    got_bwd = got_fwd if last else got[:, :, width : 2 * width]
+    unit = jnp.ones_like(decay)
+    zero = jnp.zeros_like(fwd)
+    before_decay, before_state = (unit, zero)
+    for s in range(count):
+        take = s < here
+        before_state = jnp.where(take, got_decay[s][:, None, None] * before_state + got_fwd[s], before_state)
+        before_decay = jnp.where(take, before_decay * got_decay[s], before_decay)
+    after_decay, after_state = (unit, zero)
+    for s in range(count - 1, -1, -1):
+        take = s > here
+        after_state = jnp.where(take, got_bwd[s] + got_decay[s][:, None, None] * after_state, after_state)
+        after_decay = jnp.where(take, after_decay * got_decay[s], after_decay)
+    if last:
+        return ((before_decay, before_state), (after_decay, after_state), None)
+    span_decay, span_fwd, span_bwd = (unit, zero, zero)
+    for s in range(count):
+        span_fwd = got_decay[s][:, None, None] * span_fwd + got_fwd[s]
+        span_decay = span_decay * got_decay[s]
+    for s in range(count - 1, -1, -1):
+        span_bwd = got_bwd[s] + got_decay[s][:, None, None] * span_bwd
+    return ((before_decay, before_state), (after_decay, after_state), (span_decay, span_fwd, span_bwd))
+
+
+def both_prefixes(decay, fwd_state, bwd_state, levels):
     members = lax.axis_size("inner")
     width = fwd_state.shape[1]
     packed = jnp.concatenate(
@@ -63,7 +103,7 @@
         before_states.append(run_state)
         run_state = decay_rows[m][:, None, None] * run_state + fwd_rows[m]
         run_decay = run_decay * decay_rows[m]
-    group = (run_decay, run_state)
+    aggregate = (run_decay, run_state, None)
     run_decay, run_state = (unit, zero)
     after_decays, after_states = ([None] * members, [None] * members)
     for m in range(members - 1, -1, -1):
@@ -71,20 +111,19 @@
         after_states[m] = run_state
         run_state = bwd_rows[m] + decay_rows[m][:, None, None] * run_state
         run_decay = run_decay * decay_rows[m]
-    shifts = []
-    shift = 1
-    while shift < outer_size:
-        shifts.append(shift)
-        shift *= 2
-    _, outer_before, outer_after = butterfly_rounds(
-        shifts, outer_size, here, (group[0], group[1], run_state), (unit, zero), (unit, zero), True, "outer"
-    )
+    aggregate = (aggregate[0], aggregate[1], run_state)
+    total_before = (unit, zero)
+    total_after = (unit, zero)
+    for at, axis in enumerate(levels):
+        before, after, aggregate = level_exchange(aggregate, axis, at == len(levels) - 1)
+        total_before = (before[0] * total_before[0], total_before[1] + total_before[0][:, None, None] * before[1])
+        total_after = (after[0] * total_after[0], total_after[1] + total_after[0][:, None, None] * after[1])
     back = jnp.stack(
         [
             jnp.concatenate(
                 [
-                    before_states[m] + before_decays[m][:, None, None] * outer_before[1],
-                    after_states[m] + after_decays[m][:, None, None] * outer_after[1],
+                    before_states[m] + before_decays[m][:, None, None] * total_before[1],
+                    after_states[m] + after_decays[m][:, None, None] * total_after[1],
                 ],
                 axis=1,
             )
@@ -115,7 +154,7 @@
     )
 
 
-def shards(head_input, step_size, log_decay, write_proj, read_proj, grad_out):
+def shards(head_input, step_size, log_decay, write_proj, read_proj, grad_out, levels):
     highest = lax.Precision.HIGHEST
     head_count = step_size.shape[0]
     row_count = head_input.shape[0]
@@ -185,7 +224,7 @@
     for entry in reversed(blocks):
         bwd_decay = bwd_decay * entry[6]
         bwd_state = entry[12] + entry[6][:, None, None] * bwd_state
-    state_in, grad_in = both_prefixes(fwd_decay, fwd_state, bwd_state)
+    state_in, grad_in = both_prefixes(fwd_decay, fwd_state, bwd_state, levels)
     entering = []
     current = state_in
     for entry in blocks:
@@ -238,11 +277,18 @@
         inner = 1
         while inner < heads_here and inner < ctx_count and heads_here % (inner * 2) == 0:
             inner *= 2
+        rest = ctx_count // inner
+        factors = []
+        while rest > 1:
+            factor = 4 if rest % 4 == 0 else (2 if rest % 2 == 0 else rest)
+            factors.append(factor)
+            rest //= factor
+        levels = tuple(f"level{k}" for k in range(len(factors)))
         fine = Mesh(
-            mesh.devices.reshape((ctx_count // inner, inner) + mesh.devices.shape[1:]),
-            ("outer", "inner", "head"),
-        )
-        ctx = ("outer", "inner")
+            mesh.devices.reshape(tuple(reversed(factors)) + (inner,) + mesh.devices.shape[1:]),
+            tuple(reversed(levels)) + ("inner", "head"),
+        )
+        ctx = tuple(reversed(levels)) + ("inner",)
         placed = (
             P(ctx, "head"),
             P("head", ctx),
@@ -252,7 +298,7 @@
             P(ctx, "head"),
         )
         return jax.shard_map(
-            shards,
+            functools.partial(shards, levels=levels),
             mesh=fine,
             in_specs=placed,
             out_specs=(

time: 117 us -> 125 us (1.068)
  starting transfers between devices: 56.1 us -> 44.2 us
  other arithmetic: 10.5 us -> 18.7 us
  waiting for transfers between devices: 19.5 us -> 24.9 us
  between operations: 12.4 us -> 17.2 us
  local copies, waits for them, and re-layouts: 8.07 us -> 9.36 us
    ppermute x4 -> x0, starting transfers between devices: 33.8 us -> none  [butterfly_rounds(): got = lax.ppermute(packed, axis, pairs)]
    all_to_all x0 -> x2, starting transfers between devices: none -> 22.8 us  [level_exchange(): got = lax.all_to_all(sent, axis, 0, 0)]
    all_to_all x0 -> x2, waiting for transfers between devices: none -> 9.03 us  [level_exchange(): got = lax.all_to_all(sent, axis, 0, 0)]
    add x4, other arithmetic: 2.66 us -> 10.3 us  [the longest x2 5.21 us: both_prefixes(): before_states[m] + before_decays[m][:, None, None] * total_before[1]]
    ppermute x4 -> x0, waiting for transfers between devices: 4.19 us -> none  [butterfly_rounds(): got = lax.ppermute(packed, axis, pairs)]
    select_n x3 -> x2, other arithmetic: 1.86 us -> 2.59 us  [level_exchange(): jnp.where(m < here, bwd, fwd)]
  transfers between devices with their start and end apart: 7 -> 5, of which waited for: 6 -> 5; matrix products, arithmetic and copies ran while one was open for 7% -> 7% of each run, Pallas kernels for 0% -> 0%
where the time goes in v5:
time: 125 us; the launch traced here: 124 us
  starting transfers between devices  44.2 us (35%)
  waiting for transfers between devices  24.9 us (20%)
  other arithmetic  18.7 us (15%)
  between operations  17.2 us (14%)
  matrix products  9.95 us (8%)
  local copies, waits for them, and re-layouts  9.36 us (7%)
    all_to_all x2, starting transfers between devices, level_exchange(): got = lax.all_to_all(sent, axis, 0, 0)  22.8 us
    all_to_all x1, starting transfers between devices, head_scatter(): return jnp.sum(lax.all_to_all(pieces, axis, 0, 0), axis=0)  13.2 us
    all_to_all x2, waiting for transfers between devices, level_exchange(): got = lax.all_to_all(sent, axis, 0, 0)  9.03 us
    all_to_all x1, waiting for transfers between devices, head_scatter(): return jnp.sum(lax.all_to_all(pieces, axis, 0, 0), axis=0)  5.65 us
    all_to_all x1, waiting for transfers between devices, both_prefixes(): lax.all_to_all(back.reshape((members * part,) + back.shape[2:]), 'inner',...  5.23 us
    add x2, other arithmetic, both_prefixes(): before_states[m] + before_decays[m][:, None, None] * total_before[1]  5.21 us
    add x2, other arithmetic, both_prefixes(): after_states[m] + after_decays[m][:, None, None] * total_after[1]  5.11 us
    unnamed x14, local copies, waits for them, and re-layouts  5.01 us
  transfers between devices with their start and end apart: 5, of which 5 were waited for; matrix products, arithmetic and copies ran while one was open for 7% of the time, Pallas kernels for 0%

profile of v5, /device:TPU:1, one launch (start us, length us, event | category | flops | bytes accessed | tf_op | source)
XLA Modules:
  0.0 124.3 jit_solution(7863796744182136254)
XLA Ops:
  0.6 0.9 convolution_bitcast_fusion.8
  2.1 1.1 copy.45
  3.9 0.9 copy-done
  5.1 0.6 copy-done.1
  6.6 0.7 pad_maximum_fusion
  7.3 4.8 %all-to-all-start = ((f32[4,129,128]{2,1,0:T(8,128)}), f32[4,129,128]{2,1,0:T(8,128)S(1)}, u32[]{:S(2)}, u32[]{:S(2)}) async-start(f32[4,129,128]{2,1,0:T(8,128)} %pad_maximum_fusion), calls=%async_computation | async-start | bytes 557056 | tf_op jit(solution)/shard_map/all_to_all | solution.py:93
  12.2 0.6 fusion.3
  12.8 5.0 %all-to-all-done = f32[4,129,128]{2,1,0:T(8,128)S(1)} async-done(((f32[4,129,128]{2,1,0:T(8,128)}), f32[4,129,128]{2,1,0:T(8,128)S(1)}, u32[]{:S(2)}, u32[]{:S(2)}) %all-to-all-start) | async-done | bytes 264224 | tf_op jit(solution)/shard_map/all_to_all | solution.py:93
  22.2 2.6 %fusion.105 = (f32[1,64,128]{2,1,0:T(8,128)S(1)}, f32[1,64,128]{2,1,0:T(8,128)S(1)}, f32[1,64,128]{2,1,0:T(8,128)S(1)}, f32[1,64,128]{2,1,0:T(8,128)S(1)}) fusion(f32[4,1,129,128]{3,2,1,0:T(8,128)S(1)} %bitcast.275, f32[]{:T(128)} %bitcast.12, f32[]{:T(128)} %bitcast.13, f32[]{:T(128)} %bitcast.16, f32[]{:T(128)} %bitcast.14, f32[]{:T(128)} %bitcast.33, ...), kind=kLoop, calls=%fused_computation.148 | loop fusion | flops 114688 | bytes 393240 | tf_op jit(solution)/shard_map/add | solution.py:104
  24.9 0.8 broadcast_in_dim.51
  25.7 7.0 %all-to-all-start.1 = ((f32[4,1,129,128]{3,1,2,0:T(1,128)}), f32[4,1,129,128]{3,1,2,0:T(1,128)S(1)}, u32[]{:S(2)}, u32[]{:S(2)}) async-start(f32[4,1,129,128]{3,1,2,0:T(1,128)} %broadcast_in_dim.51), calls=%async_computation.1 | async-start | bytes 528384 | tf_op jit(solution)/shard_map/all_to_all | solution.py:59
  32.8 0.6 fusion.2
  34.1 4.3 %all-to-all-done.1 = f32[4,1,129,128]{3,1,2,0:T(1,128)S(1)} async-done(((f32[4,1,129,128]{3,1,2,0:T(1,128)}), f32[4,1,129,128]{3,1,2,0:T(1,128)S(1)}, u32[]{:S(2)}, u32[]{:S(2)}) %all-to-all-start.1) | async-done | bytes 264224 | tf_op jit(solution)/shard_map/all_to_all | solution.py:59
  42.9 2.6 %broadcast_select_fusion.2 = (f32[1,64,128]{2,1,0:T(8,128)S(1)}, f32[1,64,128]{2,1,0:T(8,128)S(1)}, f32[1,64,128]{2,1,0:T(8,128)S(1)}) fusion(pred[]{:T(512)S(6)} %gt.33, f32[1,64,128]{2,1,0:T(8,128)S(1)} %bitcast.292, f32[1,64,128]{2,1,0:T(8,128)S(1)} %bitcast.294, f32[1,64,128]{2,1,0:T(8,128)S(1)} %bitcast.296, f32[1,1,64,128]{3,2,1,0:T(8,128)S(1)} %bitcast.298, ...), kind=kLoop, calls=%fused_computation.181 | loop fusion | flops 122880 | bytes 360473 | tf_op jit(solution)/shard_map/jit(_where)/select_n | solution.py:54
  45.6 0.8 copy.64
  46.4 15.8 %all-to-all-start.2 = ((f32[4,1,65,128]{3,1,2,0:T(1,128)}), f32[4,1,65,128]{3,1,2,0:T(1,128)S(1)}, u32[]{:S(2)}, u32[]{:S(2)}) async-start(f32[4,1,65,128]{3,1,2,0:T(1,128)} %copy.64), calls=%async_computation.2 | async-start | bytes 266240 | tf_op jit(solution)/shard_map/all_to_all | solution.py:59
  69.8 4.7 %all-to-all-done.2 = f32[4,1,65,128]{3,1,2,0:T(1,128)S(1)} async-done(((f32[4,1,65,128]{3,1,2,0:T(1,128)}), f32[4,1,65,128]{3,1,2,0:T(1,128)S(1)}, u32[]{:S(2)}, u32[]{:S(2)}) %all-to-all-start.2) | async-done | bytes 133152 | tf_op jit(solution)/shard_map/all_to_all | solution.py:59
  76.5 4.5 %multiply_add_fusion.6 = (f32[1,64,128]{2,1,0:T(8,128)S(1)}, f32[1,64,128]{2,1,0:T(8,128)S(1)}) fusion(f32[4,1,129,128]{3,2,1,0:T(8,128)S(1)} %bitcast.276, f32[]{:T(128)} %bitcast.27, f32[]{:T(128)} %bitcast.16, f32[1,64,128]{2,1,0:T(8,128)S(1)} %bitcast.300, f32[1,64,128]{2,1,0:T(8,128)S(1)} %bitcast.302, f32[1,64,128]{2,1,0:T(8,128)S(1)} %bitcast.304, ...), kind=kLoop, calls=%fused_computation.175 | loop fusion | flops 221184 | bytes 360500 | tf_op jit(solution)/shard_map/add | solution.py:125
  81.1 4.5 %multiply_add_fusion.7 = (f32[1,64,128]{2,1,0:T(8,128)S(1)}, f32[1,64,128]{2,1,0:T(8,128)S(1)}) fusion(f32[]{:T(128)} %bitcast.76, f32[1,64,128]{2,1,0:T(8,128)S(1)} %get-tuple-element.32, f32[]{:T(128)} %bitcast.14, f32[4,1,129,128]{3,2,1,0:T(8,128)S(1)} %bitcast.277, f32[1,64,128]{2,1,0:T(8,128)S(1)} %bitcast.307, f32[1,64,128]{2,1,0:T(8,128)S(1)} %bitcast.305, ...), kind=kLoop, calls=%fused_computation.176 | loop fusion | flops 229376 | bytes 393268 | tf_op jit(solution)/shard_map/add | solution.py:126
  85.6 0.7 multiply_add_fusion.5
  86.2 0.7 multiply_add_fusion.4
  86.9 0.7 maximum_bitcast_fusion
  87.7 3.4 %all-to-all-start.3 = ((f32[4,128,128]{2,1,0:T(8,128)}), f32[4,128,128]{2,1,0:T(8,128)S(1)}, u32[]{:S(2)}, u32[]{:S(2)}) async-start(f32[4,128,128]{2,1,0:T(8,128)} %maximum_bitcast_fusion), calls=%async_computation.3 | async-start | bytes 524288 | tf_op jit(solution)/shard_map/all_to_all | solution.py:133
  91.3 5.2 %all-to-all-done.3 = f32[4,128,128]{2,1,0:T(8,128)S(1)} async-done(((f32[4,128,128]{2,1,0:T(8,128)}), f32[4,128,128]{2,1,0:T(8,128)S(1)}, u32[]{:S(2)}, u32[]{:S(2)}) %all-to-all-start.3) | async-done | bytes 262176 | tf_op jit(solution)/shard_map/all_to_all | solution.py:133
  98.2 0.7 pad_maximum_fusion.3
  98.9 13.2 %all-to-all-start.4 = ((f32[16,16,256]{2,1,0:T(8,128)}), f32[16,16,256]{2,1,0:T(8,128)S(1)}, u32[]{:S(2)}, u32[]{:S(2)}) async-start(f32[16,16,256]{2,1,0:T(8,128)} %pad_maximum_fusion.3), calls=%async_computation.4 | async-start | bytes 524288 | tf_op jit(solution)/shard_map/all_to_all | solution.py:140
  112.4 0.7 fusion.5
  113.4 0.7 fusion.4
  114.2 0.6 multiply_reduce_fusion
  114.8 0.8 copy.74
  117.2 0.8 copy.73
  118.1 5.7 %all-to-all-done.4 = f32[16,16,256]{2,1,0:T(8,128)S(1)} async-done(((f32[16,16,256]{2,1,0:T(8,128)}), f32[16,16,256]{2,1,0:T(8,128)S(1)}, u32[]{:S(2)}, u32[]{:S(2)}) %all-to-all-start.4) | async-done | bytes 262176 | tf_op jit(solution)/shard_map/all_to_all | solution.py:140
  (59 shorter events, 10.2 us)
Async XLA Ops:
  0.6 0.9 copy-start.4
  2.1 1.2 copy-start.2
  3.2 0.7 copy-start.3
  3.9 0.9 copy-start
  4.8 0.9 copy-start.1
  7.3 10.4 %all-to-all-start = ((f32[4,129,128]{2,1,0:T(8,128)}), f32[4,129,128]{2,1,0:T(8,128)S(1)}, u32[]{:S(2)}, u32[]{:S(2)}) async-start(f32[4,129,128]{2,1,0:T(8,128)} %pad_maximum_fusion), calls=%async_computation | async-start | bytes 557056 | tf_op jit(solution)/shard_map/all_to_all | solution.py:93
  25.7 12.7 %all-to-all-start.1 = ((f32[4,1,129,128]{3,1,2,0:T(1,128)}), f32[4,1,129,128]{3,1,2,0:T(1,128)S(1)}, u32[]{:S(2)}, u32[]{:S(2)}) async-start(f32[4,1,129,128]{3,1,2,0:T(1,128)} %broadcast_in_dim.51), calls=%async_computation.1 | async-start | bytes 528384 | tf_op jit(solution)/shard_map/all_to_all | solution.py:59
  46.4 28.2 %all-to-all-start.2 = ((f32[4,1,65,128]{3,1,2,0:T(1,128)}), f32[4,1,65,128]{3,1,2,0:T(1,128)S(1)}, u32[]{:S(2)}, u32[]{:S(2)}) async-start(f32[4,1,65,128]{3,1,2,0:T(1,128)} %copy.64), calls=%async_computation.2 | async-start | bytes 266240 | tf_op jit(solution)/shard_map/all_to_all | solution.py:59
  87.7 8.9 %all-to-all-start.3 = ((f32[4,128,128]{2,1,0:T(8,128)}), f32[4,128,128]{2,1,0:T(8,128)S(1)}, u32[]{:S(2)}, u32[]{:S(2)}) async-start(f32[4,128,128]{2,1,0:T(8,128)} %maximum_bitcast_fusion), calls=%async_computation.3 | async-start | bytes 524288 | tf_op jit(solution)/shard_map/all_to_all | solution.py:133
  98.9 24.8 %all-to-all-start.4 = ((f32[16,16,256]{2,1,0:T(8,128)}), f32[16,16,256]{2,1,0:T(8,128)S(1)}, u32[]{:S(2)}, u32[]{:S(2)}) async-start(f32[16,16,256]{2,1,0:T(8,128)} %pad_maximum_fusion.3), calls=%async_computation.4 | async-start | bytes 524288 | tf_op jit(solution)/shard_map/all_to_all | solution.py:140

commit v6 on v5

--- a/solution.py
+++ b/solution.py
@@ -3,6 +3,8 @@
 import jax
 import jax.numpy as jnp
 from jax import lax
+from jax.experimental import pallas as pl
+from jax.experimental.pallas import tpu as pltpu
 from jax.sharding import Mesh, PartitionSpec as P
 
 GROUP = 128
@@ -44,6 +46,61 @@
     return ((span_decay, span_fwd, span_bwd), (before_decay, before_state), (after_decay, after_state))
 
 
+INTERPRET = False
+
+
+def level_kernel(count, width, last):
+    rows = width + 1 if last else 2 * width + 1
+
+    def kernel(here_ref, got_ref, *outs):
+        here = here_ref[0]
+        decays = [got_ref[s, rows - 1 : rows, :] for s in range(count)]
+        fwds = [got_ref[s, 0:width, :] for s in range(count)]
+        bwds = fwds if last else [got_ref[s, width : 2 * width, :] for s in range(count)]
+        before_state = jnp.zeros((width, 128), jnp.float32)
+        before_decay = jnp.ones((1, 128), jnp.float32)
+        for s in range(count):
+            take = s < here
+            factor = jnp.where(take, decays[s], 1.0)
+            before_state = factor * before_state + jnp.where(take, fwds[s], 0.0)
+            before_decay = before_decay * factor
+        after_state = jnp.zeros((width, 128), jnp.float32)
+        after_decay = jnp.ones((1, 128), jnp.float32)
+        for s in range(count - 1, -1, -1):
+            take = s > here
+            factor = jnp.where(take, decays[s], 1.0)
+            after_state = jnp.where(take, bwds[s], 0.0) + factor * after_state
+            after_decay = after_decay * factor
+        outs[0][...] = before_state
+        outs[1][...] = before_decay
+        outs[2][...] = after_state
+        outs[3][...] = after_decay
+        if not last:
+            span_fwd = jnp.zeros((width, 128), jnp.float32)
+            span_decay = jnp.ones((1, 128), jnp.float32)
+            for s in range(count):
+                span_fwd = decays[s] * span_fwd + fwds[s]
+                span_decay = span_decay * decays[s]
+            span_bwd = jnp.zeros((width, 128), jnp.float32)
+            for s in range(count - 1, -1, -1):
+                span_bwd = bwds[s] + decays[s] * span_bwd
+            outs[4][...] = span_fwd
+            outs[5][...] = span_bwd
+            outs[6][...] = span_decay
+
+    state = jax.ShapeDtypeStruct((width, 128), jnp.float32)
+    row = jax.ShapeDtypeStruct((1, 128), jnp.float32)
+    shapes = (state, row, state, row) + (() if last else (state, state, row))
+    vmem = pl.BlockSpec(memory_space=pltpu.VMEM)
+    return pl.pallas_call(
+        kernel,
+        out_shape=shapes,
+        in_specs=[pl.BlockSpec(memory_space=pltpu.SMEM), vmem],
+        out_specs=tuple(vmem for _ in shapes),
+        interpret=INTERPRET,
+    )
+
+
 def level_exchange(aggregate, axis, last):
     count, here = (lax.axis_size(axis), lax.axis_index(axis))
     decay, fwd, bwd = aggregate
@@ -57,30 +114,13 @@
         packed = jnp.concatenate([fwd, bwd, tail], axis=1)
         sent = jnp.broadcast_to(packed[None], (count,) + packed.shape)
     got = lax.all_to_all(sent, axis, 0, 0)
-    got_decay = got[:, :, -1, 0]
-    got_fwd = got[:, :, :width]
-    got_bwd = got_fwd if last else got[:, :, width : 2 * width]
-    unit = jnp.ones_like(decay)
-    zero = jnp.zeros_like(fwd)
-    before_decay, before_state = (unit, zero)
-    for s in range(count):
-        take = s < here
-        before_state = jnp.where(take, got_decay[s][:, None, None] * before_state + got_fwd[s], before_state)
-        before_decay = jnp.where(take, before_decay * got_decay[s], before_decay)
-    after_decay, after_state = (unit, zero)
-    for s in range(count - 1, -1, -1):
-        take = s > here
-        after_state = jnp.where(take, got_bwd[s] + got_decay[s][:, None, None] * after_state, after_state)
-        after_decay = jnp.where(take, after_decay * got_decay[s], after_decay)
+    got = got.reshape((count,) + got.shape[2:])
+    outs = level_kernel(count, width, last)(jnp.reshape(here, (1,)).astype(jnp.int32), got)
+    before = (outs[1][:, 0], outs[0][None])
+    after = (outs[3][:, 0], outs[2][None])
     if last:
-        return ((before_decay, before_state), (after_decay, after_state), None)
-    span_decay, span_fwd, span_bwd = (unit, zero, zero)
-    for s in range(count):
-        span_fwd = got_decay[s][:, None, None] * span_fwd + got_fwd[s]
-        span_decay = span_decay * got_decay[s]
-    for s in range(count - 1, -1, -1):
-        span_bwd = got_bwd[s] + got_decay[s][:, None, None] * span_bwd
-    return ((before_decay, before_state), (after_decay, after_state), (span_decay, span_fwd, span_bwd))
+        return (before, after, None)
+    return (before, after, (outs[6][:, 0], outs[4][None], outs[5][None]))
 
 
 def both_prefixes(decay, fwd_state, bwd_state, levels):

time: 125 us -> 118 us (0.944)
  between operations: 17.2 us -> 6.94 us
  other arithmetic: 18.7 us -> 11.3 us
  waiting for transfers between devices: 24.9 us -> 30 us
  Pallas kernels: 0 us -> 3.2 us
  local copies, waits for them, and re-layouts: 9.36 us -> 11 us
    all_to_all x2, waiting for transfers between devices: 9.03 us -> 14.1 us  [level_exchange(): got = lax.all_to_all(sent, axis, 0, 0)]
    pallas_call x0 -> x2, Pallas kernels: none -> 3.2 us  [level_exchange(): level_kernel(count, width, last)]
    add x2 -> x1, other arithmetic: 5.11 us -> 1.99 us  [both_prefixes(): after_states[m] + after_decays[m][:, None, None] * total_after[1]]
    add x2 -> x1, other arithmetic: 5.21 us -> 2.74 us  [both_prefixes(): before_states[m] + before_decays[m][:, None, None] * total_before[1]]
    unnamed x14 -> x25, local copies, waits for them, and re-layouts: 5.01 us -> 7.02 us
    select_n x2 -> x1, other arithmetic: 2.59 us -> 0.79 us  [level_exchange(): jnp.where(m < here, bwd, fwd)]
where the time goes in v6:
time: 118 us; the launch traced here: 117 us
  starting transfers between devices  44.2 us (37%)
  waiting for transfers between devices  30 us (25%)
  other arithmetic  11.3 us (10%)
  local copies, waits for them, and re-layouts  11 us (9%)
  matrix products  9.95 us (8%)
  between operations  6.94 us (6%)
  Pallas kernels  3.2 us (3%)
    all_to_all x2, starting transfers between devices, level_exchange(): got = lax.all_to_all(sent, axis, 0, 0)  22.8 us
    all_to_all x2, waiting for transfers between devices, level_exchange(): got = lax.all_to_all(sent, axis, 0, 0)  14.1 us
    all_to_all x1, starting transfers between devices, head_scatter(): return jnp.sum(lax.all_to_all(pieces, axis, 0, 0), axis=0)  13.2 us
    unnamed x25, local copies, waits for them, and re-layouts  7.02 us
    all_to_all x1, waiting for transfers between devices, head_scatter(): return jnp.sum(lax.all_to_all(pieces, axis, 0, 0), axis=0)  5.65 us
    all_to_all x1, waiting for transfers between devices, both_prefixes(): lax.all_to_all(back.reshape((members * part,) + back.shape[2:]), 'inner',...  5.23 us
    all_to_all x1, waiting for transfers between devices, both_prefixes(): mine = lax.all_to_all(packed, 'inner', 0, 0, tiled=True)  4.96 us
    all_to_all x1, starting transfers between devices, both_prefixes(): mine = lax.all_to_all(packed, 'inner', 0, 0, tiled=True)  4.83 us
  transfers between devices with their start and end apart: 5, of which 5 were waited for; matrix products, arithmetic and copies ran while one was open for 7% of the time, Pallas kernels for 0%

profile of v6, /device:TPU:1, one launch (start us, length us, event | category | flops | bytes accessed | tf_op | source)
XLA Modules:
  0.0 116.6 jit_solution(9383642701277487661)
XLA Ops:
  0.6 0.9 convolution_bitcast_fusion.8
  2.1 1.1 copy.66
  3.9 0.9 copy-done
  6.6 0.7 pad_maximum_fusion
  7.3 4.8 %all-to-all-start = ((f32[4,129,128]{2,1,0:T(8,128)}), f32[4,129,128]{2,1,0:T(8,128)S(1)}, u32[]{:S(2)}, u32[]{:S(2)}) async-start(f32[4,129,128]{2,1,0:T(8,128)} %pad_maximum_fusion), calls=%async_computation | async-start | bytes 557056 | tf_op jit(solution)/shard_map/all_to_all | solution.py:133
  12.8 5.0 %all-to-all-done = f32[4,129,128]{2,1,0:T(8,128)S(1)} async-done(((f32[4,129,128]{2,1,0:T(8,128)}), f32[4,129,128]{2,1,0:T(8,128)S(1)}, u32[]{:S(2)}, u32[]{:S(2)}) %all-to-all-start) | async-done | bytes 264224 | tf_op jit(solution)/shard_map/all_to_all | solution.py:133
  22.3 2.6 %fusion.102 = (f32[1,64,128]{2,1,0:T(8,128)S(1)}, f32[1,64,128]{2,1,0:T(8,128)S(1)}) fusion(f32[4,1,129,128]{3,2,1,0:T(8,128)S(1)} %bitcast.214, f32[]{:T(128)} %bitcast.13, f32[]{:T(128)} %bitcast.17, f32[]{:T(128)} %bitcast.15, f32[]{:T(128)} %bitcast.14, f32[]{:T(128)} %bitcast.28, f32[4,1,129,128]{3,2,0,1:T(8,128)S(1)} %bitcast.215, f32[]{:T(128)} %bitcast.24), kind=kLoop, calls=%fused_computation.145 | loop fusion | flops 114688 | bytes 327704 | tf_op jit(solution)/shard_map/add | solution.py:144
  25.0 0.8 broadcast_in_dim.51
  25.9 7.0 %all-to-all-start.1 = ((f32[4,1,129,128]{3,1,2,0:T(1,128)}), f32[4,1,129,128]{3,1,2,0:T(1,128)S(1)}, u32[]{:S(2)}, u32[]{:S(2)}) async-start(f32[4,1,129,128]{3,1,2,0:T(1,128)} %broadcast_in_dim.51), calls=%async_computation.1 | async-start | bytes 528384 | tf_op jit(solution)/shard_map/all_to_all | solution.py:116
  34.3 4.3 %all-to-all-done.1 = f32[4,1,129,128]{3,1,2,0:T(1,128)S(1)} async-done(((f32[4,1,129,128]{3,1,2,0:T(1,128)}), f32[4,1,129,128]{3,1,2,0:T(1,128)S(1)}, u32[]{:S(2)}, u32[]{:S(2)}) %all-to-all-start.1) | async-done | bytes 264224 | tf_op jit(solution)/shard_map/all_to_all | solution.py:116
  38.6 0.7 copy.96
  39.3 1.6 %shard_map.101 = (f32[64,128]{1,0:T(8,128)}, f32[1,128]{1,0:T(1,128)}, f32[64,128]{1,0:T(8,128)}, f32[1,128]{1,0:T(1,128)}, f32[64,128]{1,0:T(8,128)}, /*index=5*/f32[64,128]{1,0:T(8,128)}, f32[1,128]{1,0:T(1,128)}) custom-call(s32[1]{0:T(128)} %bitcast.3.here_ref, f32[4,129,128]{2,1,0:T(8,128)} %bitcast.229), custom_call_target="tpu_custom_call" | custom-call | tf_op jit(solution)/shard_map/pallas_call | solution.py:118
  40.9 0.8 select_bitcast_fusion.3
  41.7 0.7 copy-done.6
  42.6 0.8 copy.78
  43.4 15.8 %all-to-all-start.2 = ((f32[4,1,65,128]{3,1,2,0:T(1,128)}), f32[4,1,65,128]{3,1,2,0:T(1,128)S(1)}, u32[]{:S(2)}, u32[]{:S(2)}) async-start(f32[4,1,65,128]{3,1,2,0:T(1,128)} %copy.78), calls=%async_computation.2 | async-start | bytes 266240 | tf_op jit(solution)/shard_map/all_to_all | solution.py:116
  61.7 9.8 %all-to-all-done.2 = f32[4,1,65,128]{3,1,2,0:T(1,128)S(1)} async-done(((f32[4,1,65,128]{3,1,2,0:T(1,128)}), f32[4,1,65,128]{3,1,2,0:T(1,128)S(1)}, u32[]{:S(2)}, u32[]{:S(2)}) %all-to-all-start.2) | async-done | bytes 133152 | tf_op jit(solution)/shard_map/all_to_all | solution.py:116
  71.6 0.7 copy.80.got_ref
  72.2 1.6 %shard_map.102 = (f32[64,128]{1,0:T(8,128)}, f32[1,128]{1,0:T(1,128)}, f32[64,128]{1,0:T(8,128)}, f32[1,128]{1,0:T(1,128)}) custom-call(s32[1]{0:T(128)} %bitcast.36.here_ref, f32[4,65,128]{2,1,0:T(8,128)} %copy.80.got_ref), custom_call_target="tpu_custom_call" | custom-call | tf_op jit(solution)/shard_map/pallas_call | solution.py:118
  74.4 2.7 %fusion.105 = (f32[1,64,128]{2,1,0:T(8,128)S(1)}, f32[64,128]{1,0:T(8,128)S(1)}, f32[1,64,128]{2,1,0:T(8,128)S(1)}, f32[64,128]{1,0:T(8,128)S(1)}) fusion(f32[4,1,129,128]{3,2,1,0:T(8,128)S(1)} %bitcast.216, f32[]{:T(128)} %bitcast.24, f32[]{:T(128)} %bitcast.17, f32[64,128]{1,0:T(8,128)S(1)} %copy-done.3, f32[64,128]{1,0:T(8,128)} %get-tuple-element.19, ...), kind=kLoop, calls=%fused_computation.153 | loop fusion | flops 114688 | bytes 393248 | tf_op jit(solution)/shard_map/add | solution.py:165
  77.2 2.0 %add_bitcast_fusion.1 = (f32[1,64,128]{2,1,0:T(8,128)S(1)}, f32[1,64,128]{2,1,0:T(8,128)S(1)}, f32[1,64,128]{2,1,0:T(8,128)S(1)}, f32[1,64,128]{2,1,0:T(8,128)S(1)}) fusion(f32[64,128]{1,0:T(8,128)S(1)} %get-tuple-element.54, f32[]{:T(128)} %bitcast.57, f32[]{:T(128)} %bitcast.28, f32[4,1,129,128]{3,2,0,1:T(8,128)S(1)} %bitcast.219, f32[]{:T(128)} %bitcast.14, ...), kind=kLoop, calls=%fused_computation.167 | loop fusion | flops 131072 | bytes 360480 | tf_op jit(solution)/shard_map/add | solution.py:166
  79.2 0.7 maximum_bitcast_fusion
  80.0 3.4 %all-to-all-start.3 = ((f32[4,128,128]{2,1,0:T(8,128)}), f32[4,128,128]{2,1,0:T(8,128)S(1)}, u32[]{:S(2)}, u32[]{:S(2)}) async-start(f32[4,128,128]{2,1,0:T(8,128)} %maximum_bitcast_fusion), calls=%async_computation.3 | async-start | bytes 524288 | tf_op jit(solution)/shard_map/all_to_all | solution.py:173
  83.6 5.2 %all-to-all-done.3 = f32[4,128,128]{2,1,0:T(8,128)S(1)} async-done(((f32[4,128,128]{2,1,0:T(8,128)}), f32[4,128,128]{2,1,0:T(8,128)S(1)}, u32[]{:S(2)}, u32[]{:S(2)}) %all-to-all-start.3) | async-done | bytes 262176 | tf_op jit(solution)/shard_map/all_to_all | solution.py:173
  90.5 0.7 pad_maximum_fusion.3
  91.3 13.2 %all-to-all-start.4 = ((f32[16,16,256]{2,1,0:T(8,128)}), f32[16,16,256]{2,1,0:T(8,128)S(1)}, u32[]{:S(2)}, u32[]{:S(2)}) async-start(f32[16,16,256]{2,1,0:T(8,128)} %pad_maximum_fusion.3), calls=%async_computation.4 | async-start | bytes 524288 | tf_op jit(solution)/shard_map/all_to_all | solution.py:180
  104.7 0.7 fusion.5
  105.7 0.7 fusion.4
  106.5 0.6 multiply_reduce_fusion
  107.1 0.8 copy.86
  109.5 0.8 copy.85
  110.4 5.7 %all-to-all-done.4 = f32[16,16,256]{2,1,0:T(8,128)S(1)} async-done(((f32[16,16,256]{2,1,0:T(8,128)}), f32[16,16,256]{2,1,0:T(8,128)S(1)}, u32[]{:S(2)}, u32[]{:S(2)}) %all-to-all-start.4) | async-done | bytes 262176 | tf_op jit(solution)/shard_map/all_to_all | solution.py:180
  (67 shorter events, 11.7 us)
Async XLA Ops:
  0.6 0.9 copy-start.9
  2.1 1.2 copy-start.2
  3.2 0.7 copy-start.5
  3.9 0.9 copy-start
  4.8 0.9 copy-start.1
  7.3 10.4 %all-to-all-start = ((f32[4,129,128]{2,1,0:T(8,128)}), f32[4,129,128]{2,1,0:T(8,128)S(1)}, u32[]{:S(2)}, u32[]{:S(2)}) async-start(f32[4,129,128]{2,1,0:T(8,128)} %pad_maximum_fusion), calls=%async_computation | async-start | bytes 557056 | tf_op jit(solution)/shard_map/all_to_all | solution.py:133
  25.9 12.7 %all-to-all-start.1 = ((f32[4,1,129,128]{3,1,2,0:T(1,128)}), f32[4,1,129,128]{3,1,2,0:T(1,128)S(1)}, u32[]{:S(2)}, u32[]{:S(2)}) async-start(f32[4,1,129,128]{3,1,2,0:T(1,128)} %broadcast_in_dim.51), calls=%async_computation.1 | async-start | bytes 528384 | tf_op jit(solution)/shard_map/all_to_all | solution.py:116
  41.7 0.7 copy-start.6
  43.4 28.2 %all-to-all-start.2 = ((f32[4,1,65,128]{3,1,2,0:T(1,128)}), f32[4,1,65,128]{3,1,2,0:T(1,128)S(1)}, u32[]{:S(2)}, u32[]{:S(2)}) async-start(f32[4,1,65,128]{3,1,2,0:T(1,128)} %copy.78), calls=%async_computation.2 | async-start | bytes 266240 | tf_op jit(solution)/shard_map/all_to_all | solution.py:116
  72.2 1.6 %copy-start.3 = (f32[64,128]{1,0:T(8,128)S(1)}, f32[64,128]{1,0:T(8,128)}, u32[]{:S(2)}) copy-start(f32[64,128]{1,0:T(8,128)} %get-tuple-element.14) | copy-start | bytes 98308
  72.2 1.6 %copy-start.4 = (f32[64,128]{1,0:T(8,128)S(1)}, f32[64,128]{1,0:T(8,128)}, u32[]{:S(2)}) copy-start(f32[64,128]{1,0:T(8,128)} %get-tuple-element.20) | copy-start | bytes 98308
  73.8 0.6 copy-start.7
  73.8 0.6 copy-start.8
  80.0 8.9 %all-to-all-start.3 = ((f32[4,128,128]{2,1,0:T(8,128)}), f32[4,128,128]{2,1,0:T(8,128)S(1)}, u32[]{:S(2)}, u32[]{:S(2)}) async-start(f32[4,128,128]{2,1,0:T(8,128)} %maximum_bitcast_fusion), calls=%async_computation.3 | async-start | bytes 524288 | tf_op jit(solution)/shard_map/all_to_all | solution.py:173
  91.3 24.8 %all-to-all-start.4 = ((f32[16,16,256]{2,1,0:T(8,128)}), f32[16,16,256]{2,1,0:T(8,128)S(1)}, u32[]{:S(2)}, u32[]{:S(2)}) async-start(f32[16,16,256]{2,1,0:T(8,128)} %pad_maximum_fusion.3), calls=%async_computation.4 | async-start | bytes 524288 | tf_op jit(solution)/shard_map/all_to_all | solution.py:180

commit v7 on v6

--- a/solution.py
+++ b/solution.py
@@ -123,6 +123,68 @@
     return (before, after, (outs[6][:, 0], outs[4][None], outs[5][None]))
 
 
+def inner_kernel(members, width):
+    def kernel(mine_ref, bs_ref, bd_ref, as_ref, ad_ref, sf_ref, sb_ref, sd_ref):
+        rows = 2 * width + 1
+        decays = [mine_ref[m, rows - 1 : rows, :] for m in range(members)]
+        run_state = jnp.zeros((width, 128), jnp.float32)
+        run_decay = jnp.ones((1, 128), jnp.float32)
+        for m in range(members):
+            bs_ref[m] = run_state
+            bd_ref[m] = run_decay
+            run_state = decays[m] * run_state + mine_ref[m, 0:width, :]
+            run_decay = run_decay * decays[m]
+        sf_ref[...] = run_state
+        sd_ref[...] = run_decay
+        run_state = jnp.zeros((width, 128), jnp.float32)
+        run_decay = jnp.ones((1, 128), jnp.float32)
+        for m in range(members - 1, -1, -1):
+            as_ref[m] = run_state
+            ad_ref[m] = run_decay
+            run_state = mine_ref[m, width : 2 * width, :] + decays[m] * run_state
+            run_decay = run_decay * decays[m]
+        sb_ref[...] = run_state
+
+    many = jax.ShapeDtypeStruct((members, width, 128), jnp.float32)
+    many_rows = jax.ShapeDtypeStruct((members, 1, 128), jnp.float32)
+    state = jax.ShapeDtypeStruct((width, 128), jnp.float32)
+    row = jax.ShapeDtypeStruct((1, 128), jnp.float32)
+    shapes = (many, many_rows, many, many_rows, state, state, row)
+    vmem = pl.BlockSpec(memory_space=pltpu.VMEM)
+    return pl.pallas_call(
+        kernel, out_shape=shapes, in_specs=[vmem], out_specs=tuple(vmem for _ in shapes), interpret=INTERPRET
+    )
+
+
+def back_kernel(members, width, level_count):
+    def kernel(*refs):
+        bs_ref, bd_ref, as_ref, ad_ref = refs[:4]
+        level_refs = refs[4 : 4 + 4 * level_count]
+        out_ref = refs[-1]
+        before_state = jnp.zeros((width, 128), jnp.float32)
+        before_decay = jnp.ones((1, 128), jnp.float32)
+        after_state = jnp.zeros((width, 128), jnp.float32)
+        after_decay = jnp.ones((1, 128), jnp.float32)
+        for k in range(level_count):
+            lbs, lbd, las, lad = level_refs[4 * k : 4 * k + 4]
+            before_state = before_state + before_decay * lbs[...]
+            before_decay = before_decay * lbd[...]
+            after_state = after_state + after_decay * las[...]
+            after_decay = after_decay * lad[...]
+        for m in range(members):
+            out_ref[m, 0:width, :] = bs_ref[m] + bd_ref[m] * before_state
+            out_ref[m, width : 2 * width, :] = as_ref[m] + ad_ref[m] * after_state
+
+    vmem = pl.BlockSpec(memory_space=pltpu.VMEM)
+    return pl.pallas_call(
+        kernel,
+        out_shape=jax.ShapeDtypeStruct((members, 2 * width, 128), jnp.float32),
+        in_specs=[vmem] * (4 + 4 * level_count),
+        out_specs=vmem,
+        interpret=INTERPRET,
+    )
+
+
 def both_prefixes(decay, fwd_state, bwd_state, levels):
     members = lax.axis_size("inner")
     width = fwd_state.shape[1]
@@ -131,46 +193,15 @@
         axis=1,
     )
     mine = lax.all_to_all(packed, "inner", 0, 0, tiled=True)
-    part = mine.shape[0] // members
-    rows = mine.reshape((members, part) + mine.shape[1:])
-    fwd_rows, bwd_rows, decay_rows = (rows[:, :, :width], rows[:, :, width : 2 * width], rows[:, :, -1, 0])
-    unit = jnp.ones_like(decay_rows[0])
-    zero = jnp.zeros_like(fwd_rows[0])
-    run_decay, run_state = (unit, zero)
-    before_decays, before_states = ([], [])
-    for m in range(members):
-        before_decays.append(run_decay)
-        before_states.append(run_state)
-        run_state = decay_rows[m][:, None, None] * run_state + fwd_rows[m]
-        run_decay = run_decay * decay_rows[m]
-    aggregate = (run_decay, run_state, None)
-    run_decay, run_state = (unit, zero)
-    after_decays, after_states = ([None] * members, [None] * members)
-    for m in range(members - 1, -1, -1):
-        after_decays[m] = run_decay
-        after_states[m] = run_state
-        run_state = bwd_rows[m] + decay_rows[m][:, None, None] * run_state
-        run_decay = run_decay * decay_rows[m]
-    aggregate = (aggregate[0], aggregate[1], run_state)
-    total_before = (unit, zero)
-    total_after = (unit, zero)
+    prefixes = inner_kernel(members, width)(mine)
+    aggregate = (prefixes[6][:, 0], prefixes[4][None], prefixes[5][None])
+    level_parts = []
     for at, axis in enumerate(levels):
         before, after, aggregate = level_exchange(aggregate, axis, at == len(levels) - 1)
-        total_before = (before[0] * total_before[0], total_before[1] + total_before[0][:, None, None] * before[1])
-        total_after = (after[0] * total_after[0], total_after[1] + total_after[0][:, None, None] * after[1])
-    back = jnp.stack(
-        [
-            jnp.concatenate(
-                [
-                    before_states[m] + before_decays[m][:, None, None] * total_before[1],
-                    after_states[m] + after_decays[m][:, None, None] * total_after[1],
-                ],
-                axis=1,
-            )
-            for m in range(members)
-        ]
-    )
-    shared = lax.all_to_all(back.reshape((members * part,) + back.shape[2:]), "inner", 0, 0, tiled=True)
+        level_parts += [before[1][0], jnp.broadcast_to(before[0][:, None], (1, 128)),
+                        after[1][0], jnp.broadcast_to(after[0][:, None], (1, 128))]
+    back = back_kernel(members, width, len(levels))(*prefixes[:4], *level_parts)
+    shared = lax.all_to_all(back, "inner", 0, 0, tiled=True)
     return (shared[:, :width], shared[:, width:])
 
 

time: 118 us -> 115 us (0.975)
  other arithmetic: 11.3 us -> 4.02 us
  between operations: 6.94 us -> 0.97 us
  local copies, waits for them, and re-layouts: 11 us -> 16 us
  Pallas kernels: 3.2 us -> 6.64 us
  waiting for transfers between devices: 30 us -> 31.9 us
    add x3 -> x0, other arithmetic: 7.36 us -> none  [the longest x1 2.74 us: both_prefixes(): before_states[m] + before_decays[m][:, None, None] * total_before[1]]
    pallas_call x0 -> x2, Pallas kernels: none -> 3.46 us  [the longest x1 1.77 us: both_prefixes(): back = back_kernel(members, width, len(levels))(*prefixes[:4], *level_parts)]
    unnamed x25 -> x29, local copies, waits for them, and re-layouts: 7.02 us -> 10.2 us
    broadcast_in_dim x0 -> x4, local copies, waits for them, and re-layouts: none -> 2.3 us  [the longest x2 1.18 us: both_prefixes(): jnp.broadcast_to(after[0][:, None], (1, 128))]
    all_to_all x2, waiting for transfers between devices: 14.1 us -> 16.1 us  [level_exchange(): got = lax.all_to_all(sent, axis, 0, 0)]
  transfers between devices with their start and end apart: 5 -> 5, of which waited for: 5 -> 5; matrix products, arithmetic and copies ran while one was open for 7% -> 8% of each run, Pallas kernels for 0% -> 0%
where the time goes in v7:
time: 115 us; the launch traced here: 114 us
  starting transfers between devices  44.2 us (38%)
  waiting for transfers between devices  31.9 us (28%)
  local copies, waits for them, and re-layouts  16 us (14%)
  matrix products  9.96 us (9%)
  Pallas kernels  6.64 us (6%)
  other arithmetic  4.02 us (3%)
    all_to_all x2, starting transfers between devices, level_exchange(): got = lax.all_to_all(sent, axis, 0, 0)  22.8 us
    all_to_all x2, waiting for transfers between devices, level_exchange(): got = lax.all_to_all(sent, axis, 0, 0)  16.1 us
    all_to_all x1, starting transfers between devices, head_scatter(): return jnp.sum(lax.all_to_all(pieces, axis, 0, 0), axis=0)  13.2 us
    unnamed x29, local copies, waits for them, and re-layouts  10.2 us
    all_to_all x1, waiting for transfers between devices, head_scatter(): return jnp.sum(lax.all_to_all(pieces, axis, 0, 0), axis=0)  5.64 us
    all_to_all x1, waiting for transfers between devices, both_prefixes(): shared = lax.all_to_all(back, 'inner', 0, 0, tiled=True)  5.23 us
    all_to_all x1, waiting for transfers between devices, both_prefixes(): mine = lax.all_to_all(packed, 'inner', 0, 0, tiled=True)  4.96 us
    all_to_all x1, starting transfers between devices, both_prefixes(): mine = lax.all_to_all(packed, 'inner', 0, 0, tiled=True)  4.83 us
  transfers between devices with their start and end apart: 5, of which 5 were waited for; matrix products, arithmetic and copies ran while one was open for 8% of the time, Pallas kernels for 0%

profile of v7, /device:TPU:1, one launch (start us, length us, event | category | flops | bytes accessed | tf_op | source)
XLA Modules:
  0.0 113.7 jit_solution(13709969775272994785)
XLA Ops:
  0.6 0.9 convolution_bitcast_fusion.8
  2.1 1.1 %copy.42 = f32[256,256]{0,1:T(8,128)S(1)} copy(f32[256,256]{1,0:T(8,128)} %param.6) | data formatting | bytes 524288 | tf_op args[0]
  3.9 0.9 copy-done
  6.6 0.7 pad_maximum_fusion
  7.3 4.8 %all-to-all-start = ((f32[4,129,128]{2,1,0:T(8,128)}), f32[4,129,128]{2,1,0:T(8,128)S(1)}, u32[]{:S(2)}, u32[]{:S(2)}) async-start(f32[4,129,128]{2,1,0:T(8,128)} %pad_maximum_fusion), calls=%async_computation | async-start | bytes 557056 | tf_op jit(solution)/shard_map/all_to_all | solution.py:195
  12.8 5.0 %all-to-all-done.mine_ref = f32[4,129,128]{2,1,0:T(8,128)S(1)} async-done(((f32[4,129,128]{2,1,0:T(8,128)}), f32[4,129,128]{2,1,0:T(8,128)S(1)}, u32[]{:S(2)}, u32[]{:S(2)}) %all-to-all-start) | async-done | bytes 264224 | tf_op jit(solution)/shard_map/all_to_all | solution.py:195
  17.8 0.7 copy-done.2
  18.5 1.7 %shard_map.101 = (f32[4,64,128]{2,1,0:T(8,128)}, f32[4,1,128]{2,1,0:T(1,128)}, f32[4,64,128]{2,1,0:T(8,128)}, f32[4,1,128]{2,1,0:T(1,128)}, f32[64,128]{1,0:T(8,...) custom-call(f32[4,129,128]{2,1,0:T(8,128)} %copy-done.2), custom_call_target="tpu_custom_call" | custom-call | tf_op jit(solution)/shard_map/pallas_call | solution.py:196
  20.2 0.7 copy-done.6
  20.9 0.9 maximum_bitcast_fusion
  21.7 0.8 broadcast_in_dim.126
  22.6 7.0 %all-to-all-start.1 = ((f32[4,1,129,128]{3,1,2,0:T(1,128)}), f32[4,1,129,128]{3,1,2,0:T(1,128)S(1)}, u32[]{:S(2)}, u32[]{:S(2)}) async-start(f32[4,1,129,128]{3,1,2,0:T(1,128)} %broadcast_in_dim.126), calls=%async_computation.1 | async-start | bytes 528384 | tf_op jit(solution)/shard_map/all_to_all | solution.py:116
  31.0 4.3 %all-to-all-done.1 = f32[4,1,129,128]{3,1,2,0:T(1,128)S(1)} async-done(((f32[4,1,129,128]{3,1,2,0:T(1,128)}), f32[4,1,129,128]{3,1,2,0:T(1,128)S(1)}, u32[]{:S(2)}, u32[]{:S(2)}) %all-to-all-start.1) | async-done | bytes 264224 | tf_op jit(solution)/shard_map/all_to_all | solution.py:116
  35.3 0.7 copy.64
  36.0 1.6 %shard_map.102 = (f32[64,128]{1,0:T(8,128)}, f32[1,128]{1,0:T(1,128)}, f32[64,128]{1,0:T(8,128)}, f32[1,128]{1,0:T(1,128)}, f32[64,128]{1,0:T(8,128)}, /*index=5*/f32[64,128]{1,0:T(8,128)}, f32[1,128]{1,0:T(1,128)}) custom-call(s32[1]{0:T(128)} %bitcast.11.here_ref, f32[4,129,128]{2,1,0:T(8,128)} %bitcast.122), custom_call_target="tpu_custom_call" | custom-call | tf_op jit(solution)/shard_map/pallas_call | solution.py:118
  37.6 0.8 select_bitcast_fusion.3
  39.2 0.8 copy.46
  40.0 15.8 %all-to-all-start.2 = ((f32[4,1,65,128]{3,1,2,0:T(1,128)}), f32[4,1,65,128]{3,1,2,0:T(1,128)S(1)}, u32[]{:S(2)}, u32[]{:S(2)}) async-start(f32[4,1,65,128]{3,1,2,0:T(1,128)} %copy.46), calls=%async_computation.2 | async-start | bytes 266240 | tf_op jit(solution)/shard_map/all_to_all | solution.py:116
  56.3 11.8 %all-to-all-done.2 = f32[4,1,65,128]{3,1,2,0:T(1,128)S(1)} async-done(((f32[4,1,65,128]{3,1,2,0:T(1,128)}), f32[4,1,65,128]{3,1,2,0:T(1,128)S(1)}, u32[]{:S(2)}, u32[]{:S(2)}) %all-to-all-start.2) | async-done | bytes 133152 | tf_op jit(solution)/shard_map/all_to_all | solution.py:116
  68.2 0.7 copy.48.got_ref
  68.9 1.6 %shard_map.103 = (f32[64,128]{1,0:T(8,128)}, f32[1,128]{1,0:T(1,128)}, f32[64,128]{1,0:T(8,128)}, f32[1,128]{1,0:T(1,128)}) custom-call(s32[1]{0:T(128)} %bitcast.18.here_ref, f32[4,65,128]{2,1,0:T(8,128)} %copy.48.got_ref), custom_call_target="tpu_custom_call" | custom-call | tf_op jit(solution)/shard_map/pallas_call | solution.py:118
  74.0 0.7 copy-done.8
  75.3 1.8 %shard_map.104 = f32[4,128,128]{2,1,0:T(8,128)} custom-call(f32[4,64,128]{2,1,0:T(8,128)} %get-tuple-element.23.refs_0_, f32[4,1,128]{2,1,0:T(1,128)} %get-tuple-element.24.refs_1_, f32[4,64,128]{2,1,0:T(8,128)} %get-tuple-element.25.refs_2_, f32[4,1,128]{2,1,0:T(1,128)} %get-tuple-element.26.refs_3_, f32[64,128]{1,0:T(8,128)} %get-tuple-element.30.refs_4_, ...), custom_call_target="tpu_custom_call" | custom-call | tf_op jit(solution)/shard_map/pallas_call | solution.py:203
  77.1 3.4 %all-to-all-start.3 = ((f32[4,128,128]{2,1,0:T(8,128)}), f32[4,128,128]{2,1,0:T(8,128)S(1)}, u32[]{:S(2)}, u32[]{:S(2)}) async-start(f32[4,128,128]{2,1,0:T(8,128)} %shard_map.104), calls=%async_computation.3 | async-start | bytes 524288 | tf_op jit(solution)/shard_map/all_to_all | solution.py:204
  80.7 5.2 %all-to-all-done.3 = f32[4,128,128]{2,1,0:T(8,128)S(1)} async-done(((f32[4,128,128]{2,1,0:T(8,128)}), f32[4,128,128]{2,1,0:T(8,128)S(1)}, u32[]{:S(2)}, u32[]{:S(2)}) %all-to-all-start.3) | async-done | bytes 262176 | tf_op jit(solution)/shard_map/all_to_all | solution.py:204
  87.6 0.7 pad_maximum_fusion.3
  88.3 13.2 %all-to-all-start.4 = ((f32[16,16,256]{2,1,0:T(8,128)}), f32[16,16,256]{2,1,0:T(8,128)S(1)}, u32[]{:S(2)}, u32[]{:S(2)}) async-start(f32[16,16,256]{2,1,0:T(8,128)} %pad_maximum_fusion.3), calls=%async_computation.4 | async-start | bytes 524288 | tf_op jit(solution)/shard_map/all_to_all | solution.py:211
  101.8 0.7 fusion.5
  102.8 0.7 fusion.4
  104.2 0.8 copy.54
  106.6 0.8 copy.53
  107.5 5.6 %all-to-all-done.4 = f32[16,16,256]{2,1,0:T(8,128)S(1)} async-done(((f32[16,16,256]{2,1,0:T(8,128)}), f32[16,16,256]{2,1,0:T(8,128)S(1)}, u32[]{:S(2)}, u32[]{:S(2)}) %all-to-all-start.4) | async-done | bytes 262176 | tf_op jit(solution)/shard_map/all_to_all | solution.py:211
  (68 shorter events, 15.8 us)
Async XLA Ops:
  0.6 0.9 copy-start.7
  2.1 1.2 %copy-start.3 = (f32[256,256]{1,0:T(8,128)S(1)}, f32[256,256]{1,0:T(8,128)}, u32[]{:S(2)}) copy-start(f32[256,256]{1,0:T(8,128)} %param.11) | copy-start | bytes 786436
  3.2 0.7 copy-start.4
  3.9 0.9 copy-start
  4.8 0.9 copy-start.1
  7.3 10.4 %all-to-all-start = ((f32[4,129,128]{2,1,0:T(8,128)}), f32[4,129,128]{2,1,0:T(8,128)S(1)}, u32[]{:S(2)}, u32[]{:S(2)}) async-start(f32[4,129,128]{2,1,0:T(8,128)} %pad_maximum_fusion), calls=%async_computation | async-start | bytes 557056 | tf_op jit(solution)/shard_map/all_to_all | solution.py:195
  17.8 0.7 copy-start.2
  20.2 0.7 copy-start.6
  22.6 12.7 %all-to-all-start.1 = ((f32[4,1,129,128]{3,1,2,0:T(1,128)}), f32[4,1,129,128]{3,1,2,0:T(1,128)S(1)}, u32[]{:S(2)}, u32[]{:S(2)}) async-start(f32[4,1,129,128]{3,1,2,0:T(1,128)} %broadcast_in_dim.126), calls=%async_computation.1 | async-start | bytes 528384 | tf_op jit(solution)/shard_map/all_to_all | solution.py:116
  38.4 0.6 copy-start.5
  40.0 28.2 %all-to-all-start.2 = ((f32[4,1,65,128]{3,1,2,0:T(1,128)}), f32[4,1,65,128]{3,1,2,0:T(1,128)S(1)}, u32[]{:S(2)}, u32[]{:S(2)}) async-start(f32[4,1,65,128]{3,1,2,0:T(1,128)} %copy.46), calls=%async_computation.2 | async-start | bytes 266240 | tf_op jit(solution)/shard_map/all_to_all | solution.py:116
  70.4 0.6 copy-start.11
  71.6 0.6 copy-start.10
  72.8 0.7 copy-start.9
  74.0 0.7 copy-start.8
  77.1 8.9 %all-to-all-start.3 = ((f32[4,128,128]{2,1,0:T(8,128)}), f32[4,128,128]{2,1,0:T(8,128)S(1)}, u32[]{:S(2)}, u32[]{:S(2)}) async-start(f32[4,128,128]{2,1,0:T(8,128)} %shard_map.104), calls=%async_computation.3 | async-start | bytes 524288 | tf_op jit(solution)/shard_map/all_to_all | solution.py:204
  88.3 24.8 %all-to-all-start.4 = ((f32[16,16,256]{2,1,0:T(8,128)}), f32[16,16,256]{2,1,0:T(8,128)S(1)}, u32[]{:S(2)}, u32[]{:S(2)}) async-start(f32[16,16,256]{2,1,0:T(8,128)} %pad_maximum_fusion.3), calls=%async_computation.4 | async-start | bytes 524288 | tf_op jit(solution)/shard_map/all_to_all | solution.py:211

commit v8 on v7

--- a/solution.py
+++ b/solution.py
@@ -103,9 +103,8 @@
 
 def level_exchange(aggregate, axis, last):
     count, here = (lax.axis_size(axis), lax.axis_index(axis))
-    decay, fwd, bwd = aggregate
+    tail, fwd, bwd = aggregate
     width = fwd.shape[1]
-    tail = jnp.broadcast_to(decay[:, None, None], decay.shape[:1] + (1,) + fwd.shape[2:])
     if last:
         sent = jnp.stack(
             [jnp.concatenate([jnp.where(m < here, bwd, fwd), tail], axis=1) for m in range(count)]
@@ -116,11 +115,9 @@
     got = lax.all_to_all(sent, axis, 0, 0)
     got = got.reshape((count,) + got.shape[2:])
     outs = level_kernel(count, width, last)(jnp.reshape(here, (1,)).astype(jnp.int32), got)
-    before = (outs[1][:, 0], outs[0][None])
-    after = (outs[3][:, 0], outs[2][None])
     if last:
-        return (before, after, None)
-    return (before, after, (outs[6][:, 0], outs[4][None], outs[5][None]))
+        return (outs, None)
+    return (outs[:4], (outs[6][None], outs[4][None], outs[5][None]))
 
 
 def inner_kernel(members, width):
@@ -194,12 +191,11 @@
     )
     mine = lax.all_to_all(packed, "inner", 0, 0, tiled=True)
     prefixes = inner_kernel(members, width)(mine)
-    aggregate = (prefixes[6][:, 0], prefixes[4][None], prefixes[5][None])
+    aggregate = (prefixes[6][None], prefixes[4][None], prefixes[5][None])
     level_parts = []
     for at, axis in enumerate(levels):
-        before, after, aggregate = level_exchange(aggregate, axis, at == len(levels) - 1)
-        level_parts += [before[1][0], jnp.broadcast_to(before[0][:, None], (1, 128)),
-                        after[1][0], jnp.broadcast_to(after[0][:, None], (1, 128))]
+        parts, aggregate = level_exchange(aggregate, axis, at == len(levels) - 1)
+        level_parts += list(parts)
     back = back_kernel(members, width, len(levels))(*prefixes[:4], *level_parts)
     shared = lax.all_to_all(back, "inner", 0, 0, tiled=True)
     return (shared[:, :width], shared[:, width:])

time: 115 us -> 110 us (0.957)
  local copies, waits for them, and re-layouts: 16 us -> 11 us
    unnamed x29 -> x21, local copies, waits for them, and re-layouts: 10.2 us -> 7.76 us
    broadcast_in_dim x4 -> x0, local copies, waits for them, and re-layouts: 2.3 us -> none  [the longest x2 1.18 us: both_prefixes(): jnp.broadcast_to(after[0][:, None], (1, 128))]
where the time goes in v8:
time: 110 us; the launch traced here: 109 us
  starting transfers between devices  44.2 us (40%)
  waiting for transfers between devices  32 us (29%)
  local copies, waits for them, and re-layouts  11 us (10%)
  matrix products  9.95 us (9%)
  Pallas kernels  6.64 us (6%)
  other arithmetic  3.95 us (4%)
    all_to_all x2, starting transfers between devices, level_exchange(): got = lax.all_to_all(sent, axis, 0, 0)  22.8 us
    all_to_all x2, waiting for transfers between devices, level_exchange(): got = lax.all_to_all(sent, axis, 0, 0)  16.1 us
    all_to_all x1, starting transfers between devices, head_scatter(): return jnp.sum(lax.all_to_all(pieces, axis, 0, 0), axis=0)  13.2 us
    unnamed x21, local copies, waits for them, and re-layouts  7.76 us
    all_to_all x1, waiting for transfers between devices, head_scatter(): return jnp.sum(lax.all_to_all(pieces, axis, 0, 0), axis=0)  5.65 us
    all_to_all x1, waiting for transfers between devices, both_prefixes(): shared = lax.all_to_all(back, 'inner', 0, 0, tiled=True)  5.23 us
    all_to_all x1, waiting for transfers between devices, both_prefixes(): mine = lax.all_to_all(packed, 'inner', 0, 0, tiled=True)  4.96 us
    all_to_all x1, starting transfers between devices, both_prefixes(): mine = lax.all_to_all(packed, 'inner', 0, 0, tiled=True)  4.83 us
  transfers between devices with their start and end apart: 5, of which 5 were waited for; matrix products, arithmetic and copies ran while one was open for 8% of the time, Pallas kernels for 0%

profile of v8, /device:TPU:1, one launch (start us, length us, event | category | flops | bytes accessed | tf_op | source)
XLA Modules:
  0.0 108.7 jit_solution(7425929445757518792)
XLA Ops:
  0.6 0.9 convolution_bitcast_fusion.8
  2.1 1.1 %copy.42 = f32[256,256]{0,1:T(8,128)S(1)} copy(f32[256,256]{1,0:T(8,128)} %param.6) | data formatting | bytes 524288 | tf_op args[0]
  3.9 0.9 copy-done
  6.6 0.7 pad_maximum_fusion
  7.3 4.8 %all-to-all-start = ((f32[4,129,128]{2,1,0:T(8,128)}), f32[4,129,128]{2,1,0:T(8,128)S(1)}, u32[]{:S(2)}, u32[]{:S(2)}) async-start(f32[4,129,128]{2,1,0:T(8,128)} %pad_maximum_fusion), calls=%async_computation | async-start | bytes 557056 | tf_op jit(solution)/shard_map/all_to_all | solution.py:192
  12.8 5.0 %all-to-all-done.mine_ref = f32[4,129,128]{2,1,0:T(8,128)S(1)} async-done(((f32[4,129,128]{2,1,0:T(8,128)}), f32[4,129,128]{2,1,0:T(8,128)S(1)}, u32[]{:S(2)}, u32[]{:S(2)}) %all-to-all-start) | async-done | bytes 264224 | tf_op jit(solution)/shard_map/all_to_all | solution.py:192
  17.8 0.7 copy-done.2
  18.5 1.7 %shard_map.101 = (f32[4,64,128]{2,1,0:T(8,128)}, f32[4,1,128]{2,1,0:T(1,128)}, f32[4,64,128]{2,1,0:T(8,128)}, f32[4,1,128]{2,1,0:T(1,128)}, f32[64,128]{1,0:T(8,...) custom-call(f32[4,129,128]{2,1,0:T(8,128)} %copy-done.2), custom_call_target="tpu_custom_call" | custom-call | tf_op jit(solution)/shard_map/pallas_call | solution.py:193
  20.2 0.7 copy-done.6
  20.8 0.8 maximum_bitcast_fusion
  21.6 0.8 broadcast_in_dim.91
  22.5 7.0 %all-to-all-start.1 = ((f32[4,1,129,128]{3,1,2,0:T(1,128)}), f32[4,1,129,128]{3,1,2,0:T(1,128)S(1)}, u32[]{:S(2)}, u32[]{:S(2)}) async-start(f32[4,1,129,128]{3,1,2,0:T(1,128)} %broadcast_in_dim.91), calls=%async_computation.1 | async-start | bytes 528384 | tf_op jit(solution)/shard_map/all_to_all | solution.py:115
  30.9 4.3 %all-to-all-done.1 = f32[4,1,129,128]{3,1,2,0:T(1,128)S(1)} async-done(((f32[4,1,129,128]{3,1,2,0:T(1,128)}), f32[4,1,129,128]{3,1,2,0:T(1,128)S(1)}, u32[]{:S(2)}, u32[]{:S(2)}) %all-to-all-start.1) | async-done | bytes 264224 | tf_op jit(solution)/shard_map/all_to_all | solution.py:115
  35.1 0.7 copy.64
  35.9 1.6 %shard_map.102 = (f32[64,128]{1,0:T(8,128)}, f32[1,128]{1,0:T(1,128)}, f32[64,128]{1,0:T(8,128)}, f32[1,128]{1,0:T(1,128)}, f32[64,128]{1,0:T(8,128)}, /*index=5*/f32[64,128]{1,0:T(8,128)}, f32[1,128]{1,0:T(1,128)}) custom-call(s32[1]{0:T(128)} %bitcast.11.here_ref, f32[4,129,128]{2,1,0:T(8,128)} %bitcast.110), custom_call_target="tpu_custom_call" | custom-call | tf_op jit(solution)/shard_map/pallas_call | solution.py:117
  37.5 0.8 select_bitcast_fusion.3
  38.3 0.7 copy-done.5
  39.0 0.8 copy.46
  39.8 15.8 %all-to-all-start.2 = ((f32[4,1,65,128]{3,1,2,0:T(1,128)}), f32[4,1,65,128]{3,1,2,0:T(1,128)S(1)}, u32[]{:S(2)}, u32[]{:S(2)}) async-start(f32[4,1,65,128]{3,1,2,0:T(1,128)} %copy.46), calls=%async_computation.2 | async-start | bytes 266240 | tf_op jit(solution)/shard_map/all_to_all | solution.py:115
  56.1 11.8 %all-to-all-done.2 = f32[4,1,65,128]{3,1,2,0:T(1,128)S(1)} async-done(((f32[4,1,65,128]{3,1,2,0:T(1,128)}), f32[4,1,65,128]{3,1,2,0:T(1,128)S(1)}, u32[]{:S(2)}, u32[]{:S(2)}) %all-to-all-start.2) | async-done | bytes 133152 | tf_op jit(solution)/shard_map/all_to_all | solution.py:115
  68.0 0.7 copy.48.got_ref
  68.7 1.6 %shard_map.103 = (f32[64,128]{1,0:T(8,128)}, f32[1,128]{1,0:T(1,128)}, f32[64,128]{1,0:T(8,128)}, f32[1,128]{1,0:T(1,128)}) custom-call(s32[1]{0:T(128)} %bitcast.16.here_ref, f32[4,65,128]{2,1,0:T(8,128)} %copy.48.got_ref), custom_call_target="tpu_custom_call" | custom-call | tf_op jit(solution)/shard_map/pallas_call | solution.py:117
  70.2 1.8 %shard_map.104 = f32[4,128,128]{2,1,0:T(8,128)} custom-call(f32[4,64,128]{2,1,0:T(8,128)} %get-tuple-element.23.refs_0_, f32[4,1,128]{2,1,0:T(1,128)} %get-tuple-element.24.refs_1_, f32[4,64,128]{2,1,0:T(8,128)} %get-tuple-element.25.refs_2_, f32[4,1,128]{2,1,0:T(1,128)} %get-tuple-element.26.refs_3_, f32[64,128]{1,0:T(8,128)} %get-tuple-element.30.refs_4_, ...), custom_call_target="tpu_custom_call" | custom-call | tf_op jit(solution)/shard_map/pallas_call | solution.py:199
  72.0 3.4 %all-to-all-start.3 = ((f32[4,128,128]{2,1,0:T(8,128)}), f32[4,128,128]{2,1,0:T(8,128)S(1)}, u32[]{:S(2)}, u32[]{:S(2)}) async-start(f32[4,128,128]{2,1,0:T(8,128)} %shard_map.104), calls=%async_computation.3 | async-start | bytes 524288 | tf_op jit(solution)/shard_map/all_to_all | solution.py:200
  75.7 5.2 %all-to-all-done.3 = f32[4,128,128]{2,1,0:T(8,128)S(1)} async-done(((f32[4,128,128]{2,1,0:T(8,128)}), f32[4,128,128]{2,1,0:T(8,128)S(1)}, u32[]{:S(2)}, u32[]{:S(2)}) %all-to-all-start.3) | async-done | bytes 262176 | tf_op jit(solution)/shard_map/all_to_all | solution.py:200
  82.6 0.7 pad_maximum_fusion.3
  83.3 13.2 %all-to-all-start.4 = ((f32[16,16,256]{2,1,0:T(8,128)}), f32[16,16,256]{2,1,0:T(8,128)S(1)}, u32[]{:S(2)}, u32[]{:S(2)}) async-start(f32[16,16,256]{2,1,0:T(8,128)} %pad_maximum_fusion.3), calls=%async_computation.4 | async-start | bytes 524288 | tf_op jit(solution)/shard_map/all_to_all | solution.py:207
  96.8 0.7 fusion.5
  97.8 0.7 fusion.4
  99.1 0.8 copy.54
  101.5 0.8 copy.53
  102.4 5.7 %all-to-all-done.4 = f32[16,16,256]{2,1,0:T(8,128)S(1)} async-done(((f32[16,16,256]{2,1,0:T(8,128)}), f32[16,16,256]{2,1,0:T(8,128)S(1)}, u32[]{:S(2)}, u32[]{:S(2)}) %all-to-all-start.4) | async-done | bytes 262176 | tf_op jit(solution)/shard_map/all_to_all | solution.py:207
  (52 shorter events, 10.9 us)
Async XLA Ops:
  0.6 0.9 copy-start.7
  2.1 1.2 %copy-start.3 = (f32[256,256]{1,0:T(8,128)S(1)}, f32[256,256]{1,0:T(8,128)}, u32[]{:S(2)}) copy-start(f32[256,256]{1,0:T(8,128)} %param.11) | copy-start | bytes 786436
  3.2 0.7 copy-start.4
  3.9 0.9 copy-start
  4.8 0.9 copy-start.1
  7.3 10.4 %all-to-all-start = ((f32[4,129,128]{2,1,0:T(8,128)}), f32[4,129,128]{2,1,0:T(8,128)S(1)}, u32[]{:S(2)}, u32[]{:S(2)}) async-start(f32[4,129,128]{2,1,0:T(8,128)} %pad_maximum_fusion), calls=%async_computation | async-start | bytes 557056 | tf_op jit(solution)/shard_map/all_to_all | solution.py:192
  17.8 0.7 copy-start.2
  20.2 0.7 copy-start.6
  22.5 12.7 %all-to-all-start.1 = ((f32[4,1,129,128]{3,1,2,0:T(1,128)}), f32[4,1,129,128]{3,1,2,0:T(1,128)S(1)}, u32[]{:S(2)}, u32[]{:S(2)}) async-start(f32[4,1,129,128]{3,1,2,0:T(1,128)} %broadcast_in_dim.91), calls=%async_computation.1 | async-start | bytes 528384 | tf_op jit(solution)/shard_map/all_to_all | solution.py:115
  38.3 0.7 copy-start.5
  39.8 28.2 %all-to-all-start.2 = ((f32[4,1,65,128]{3,1,2,0:T(1,128)}), f32[4,1,65,128]{3,1,2,0:T(1,128)S(1)}, u32[]{:S(2)}, u32[]{:S(2)}) async-start(f32[4,1,65,128]{3,1,2,0:T(1,128)} %copy.46), calls=%async_computation.2 | async-start | bytes 266240 | tf_op jit(solution)/shard_map/all_to_all | solution.py:115
  72.0 8.9 %all-to-all-start.3 = ((f32[4,128,128]{2,1,0:T(8,128)}), f32[4,128,128]{2,1,0:T(8,128)S(1)}, u32[]{:S(2)}, u32[]{:S(2)}) async-start(f32[4,128,128]{2,1,0:T(8,128)} %shard_map.104), calls=%async_computation.3 | async-start | bytes 524288 | tf_op jit(solution)/shard_map/all_to_all | solution.py:200
  83.3 24.8 %all-to-all-start.4 = ((f32[16,16,256]{2,1,0:T(8,128)}), f32[16,16,256]{2,1,0:T(8,128)S(1)}, u32[]{:S(2)}, u32[]{:S(2)}) async-start(f32[16,16,256]{2,1,0:T(8,128)} %pad_maximum_fusion.3), calls=%async_computation.4 | async-start | bytes 524288 | tf_op jit(solution)/shard_map/all_to_all | solution.py:207

commit v9 on v8

--- a/solution.py
+++ b/solution.py
@@ -1,4 +1,5 @@
 import functools
+import math
 
 import jax
 import jax.numpy as jnp
@@ -201,10 +202,12 @@
     return (shared[:, :width], shared[:, width:])
 
 
-def head_scatter(total, axis):
-    size = lax.axis_size(axis)
-    pieces = total.reshape((size, total.shape[0] // size) + total.shape[1:])
-    return jnp.sum(lax.all_to_all(pieces, axis, 0, 0), axis=0)
+def head_scatter(total, axes):
+    sizes = [lax.axis_size(axis) for axis in axes]
+    blocks = total.reshape(tuple(sizes) + (total.shape[0] // math.prod(sizes),) + total.shape[1:])
+    for place in range(len(axes) - 1, -1, -1):
+        blocks = jnp.sum(lax.all_to_all(blocks, axes[place], place, place, tiled=True), axis=place)
+    return blocks
 
 
 def combine_forward(first_part, second_part):
@@ -221,7 +224,7 @@
     )
 
 
-def shards(head_input, step_size, log_decay, write_proj, read_proj, grad_out, levels):
+def shards(head_input, step_size, log_decay, write_proj, read_proj, grad_out, levels, head_axes):
     highest = lax.Precision.HIGHEST
     head_count = step_size.shape[0]
     row_count = head_input.shape[0]
@@ -325,7 +328,7 @@
     read_carried = jnp.concatenate(read_far, axis=0)
     write_total = jnp.concatenate([entry[9] for entry in blocks], axis=0) + write_carried
     read_total = jnp.concatenate([entry[10] for entry in blocks], axis=0) + read_carried
-    both_grads = head_scatter(jnp.concatenate([write_total, read_total], axis=1), "head")
+    both_grads = head_scatter(jnp.concatenate([write_total, read_total], axis=1), head_axes)
     write_grad, read_grad = (both_grads[:, :state_width], both_grads[:, state_width:])
     grad_input = (
         (step_size[:, None, :] * back_rows)
@@ -351,29 +354,33 @@
             factors.append(factor)
             rest //= factor
         levels = tuple(f"level{k}" for k in range(len(factors)))
+        head_count = mesh.shape["head"]
+        pair = 2 if head_count % 2 == 0 else 1
+        head_axes = ("head_outer", "head_inner")
         fine = Mesh(
-            mesh.devices.reshape(tuple(reversed(factors)) + (inner,) + mesh.devices.shape[1:]),
-            tuple(reversed(levels)) + ("inner", "head"),
-        )
+            mesh.devices.reshape(tuple(reversed(factors)) + (inner, head_count // pair, pair)),
+            tuple(reversed(levels)) + ("inner",) + head_axes,
+        )
+        head = head_axes
         ctx = tuple(reversed(levels)) + ("inner",)
         placed = (
-            P(ctx, "head"),
-            P("head", ctx),
-            P("head", ctx),
+            P(ctx, head),
+            P(head, ctx),
+            P(head, ctx),
             P(ctx, None),
             P(ctx, None),
-            P(ctx, "head"),
+            P(ctx, head),
         )
         return jax.shard_map(
-            functools.partial(shards, levels=levels),
+            functools.partial(shards, levels=levels, head_axes=head_axes),
             mesh=fine,
             in_specs=placed,
             out_specs=(
-                P(ctx, "head"),
-                P(ctx, "head"),
-                P("head", ctx),
-                P(ctx + ("head",), None),
-                P(ctx + ("head",), None),
+                P(ctx, head),
+                P(ctx, head),
+                P(head, ctx),
+                P(ctx + head, None),
+                P(ctx + head, None),
             ),
             check_vma=False,
         )(*args)

time: 110 us -> 109 us (level)
  blocking collectives: 0 us -> 9.64 us
  starting transfers between devices: 44.2 us -> 37.9 us
  waiting for transfers between devices: 32 us -> 28.3 us
    all_to_all x0 -> x1, blocking collectives: none -> 9.64 us  [head_scatter(): lax.all_to_all(blocks, axes[place], place, place, tiled=True)]
    all_to_all x1, starting transfers between devices: 13.2 us -> 6.81 us  [head_scatter(): lax.all_to_all(blocks, axes[place], place, place, tiled=True)]
    all_to_all x1, waiting for transfers between devices: 5.65 us -> 1.98 us  [head_scatter(): lax.all_to_all(blocks, axes[place], place, place, tiled=True)]
where the time goes in v9:
time: 109 us; the launch traced here: 108 us
  starting transfers between devices  37.9 us (35%)
  waiting for transfers between devices  28.3 us (26%)
  local copies, waits for them, and re-layouts  11 us (10%)
  matrix products  9.95 us (9%)
  blocking collectives  9.64 us (9%)
  Pallas kernels  6.66 us (6%)
  other arithmetic  3.91 us (4%)
    all_to_all x2, starting transfers between devices, level_exchange(): got = lax.all_to_all(sent, axis, 0, 0)  22.8 us
    all_to_all x2, waiting for transfers between devices, level_exchange(): got = lax.all_to_all(sent, axis, 0, 0)  16.1 us
    all_to_all x1, blocking collectives, head_scatter(): lax.all_to_all(blocks, axes[place], place, place, tiled=True)  9.64 us
    unnamed x21, local copies, waits for them, and re-layouts  7.7 us
    all_to_all x1, starting transfers between devices, head_scatter(): lax.all_to_all(blocks, axes[place], place, place, tiled=True)  6.81 us
    all_to_all x1, waiting for transfers between devices, both_prefixes(): shared = lax.all_to_all(back, 'inner', 0, 0, tiled=True)  5.23 us
    all_to_all x1, waiting for transfers between devices, both_prefixes(): mine = lax.all_to_all(packed, 'inner', 0, 0, tiled=True)  4.96 us
    all_to_all x1, starting transfers between devices, both_prefixes(): mine = lax.all_to_all(packed, 'inner', 0, 0, tiled=True)  4.83 us
  transfers between devices with their start and end apart: 5, of which 5 were waited for; matrix products, arithmetic and copies ran while one was open for 8% of the time, Pallas kernels for 0%

profile of v9, /device:TPU:1, one launch (start us, length us, event | category | flops | bytes accessed | tf_op | source)
XLA Modules:
  0.0 108.2 jit_solution(6251795328045423164)
XLA Ops:
  0.6 0.9 convolution_bitcast_fusion.8
  2.1 1.1 %copy.59 = f32[256,256]{0,1:T(8,128)S(1)} copy(f32[256,256]{1,0:T(8,128)} %param.6) | data formatting | bytes 524288 | tf_op args[0]
  3.9 0.9 copy-done
  6.6 0.7 pad_maximum_fusion
  7.3 4.8 %all-to-all-start = ((f32[4,129,128]{2,1,0:T(8,128)}), f32[4,129,128]{2,1,0:T(8,128)S(1)}, u32[]{:S(2)}, u32[]{:S(2)}) async-start(f32[4,129,128]{2,1,0:T(8,128)} %pad_maximum_fusion), calls=%async_computation | async-start | bytes 557056 | tf_op jit(solution)/shard_map/all_to_all | solution.py:193
  12.8 5.0 %all-to-all-done.mine_ref = f32[4,129,128]{2,1,0:T(8,128)S(1)} async-done(((f32[4,129,128]{2,1,0:T(8,128)}), f32[4,129,128]{2,1,0:T(8,128)S(1)}, u32[]{:S(2)}, u32[]{:S(2)}) %all-to-all-start) | async-done | bytes 264224 | tf_op jit(solution)/shard_map/all_to_all | solution.py:193
  17.8 0.7 copy-done.2
  18.5 1.7 %shard_map.101 = (f32[4,64,128]{2,1,0:T(8,128)}, f32[4,1,128]{2,1,0:T(1,128)}, f32[4,64,128]{2,1,0:T(8,128)}, f32[4,1,128]{2,1,0:T(1,128)}, f32[64,128]{1,0:T(8,...) custom-call(f32[4,129,128]{2,1,0:T(8,128)} %copy-done.2), custom_call_target="tpu_custom_call" | custom-call | tf_op jit(solution)/shard_map/pallas_call | solution.py:194
  20.2 0.7 copy-done.6
  20.8 0.8 maximum_bitcast_fusion
  21.6 0.8 broadcast_in_dim.91
  22.4 7.1 %all-to-all-start.1 = ((f32[4,1,129,128]{3,1,2,0:T(1,128)}), f32[4,1,129,128]{3,1,2,0:T(1,128)S(1)}, u32[]{:S(2)}, u32[]{:S(2)}) async-start(f32[4,1,129,128]{3,1,2,0:T(1,128)} %broadcast_in_dim.91), calls=%async_computation.1 | async-start | bytes 528384 | tf_op jit(solution)/shard_map/all_to_all | solution.py:116
  30.8 4.3 %all-to-all-done.1 = f32[4,1,129,128]{3,1,2,0:T(1,128)S(1)} async-done(((f32[4,1,129,128]{3,1,2,0:T(1,128)}), f32[4,1,129,128]{3,1,2,0:T(1,128)S(1)}, u32[]{:S(2)}, u32[]{:S(2)}) %all-to-all-start.1) | async-done | bytes 264224 | tf_op jit(solution)/shard_map/all_to_all | solution.py:116
  35.1 0.7 copy.84
  35.9 1.6 %shard_map.102 = (f32[64,128]{1,0:T(8,128)}, f32[1,128]{1,0:T(1,128)}, f32[64,128]{1,0:T(8,128)}, f32[1,128]{1,0:T(1,128)}, f32[64,128]{1,0:T(8,128)}, /*index=5*/f32[64,128]{1,0:T(8,128)}, f32[1,128]{1,0:T(1,128)}) custom-call(s32[1]{0:T(128)} %bitcast.11.here_ref, f32[4,129,128]{2,1,0:T(8,128)} %bitcast.110), custom_call_target="tpu_custom_call" | custom-call | tf_op jit(solution)/shard_map/pallas_call | solution.py:118
  37.5 0.8 select_bitcast_fusion.3
  38.9 0.8 copy.63
  39.7 15.8 %all-to-all-start.2 = ((f32[4,1,65,128]{3,1,2,0:T(1,128)}), f32[4,1,65,128]{3,1,2,0:T(1,128)S(1)}, u32[]{:S(2)}, u32[]{:S(2)}) async-start(f32[4,1,65,128]{3,1,2,0:T(1,128)} %copy.63), calls=%async_computation.2 | async-start | bytes 266240 | tf_op jit(solution)/shard_map/all_to_all | solution.py:116
  56.0 11.8 %all-to-all-done.2 = f32[4,1,65,128]{3,1,2,0:T(1,128)S(1)} async-done(((f32[4,1,65,128]{3,1,2,0:T(1,128)}), f32[4,1,65,128]{3,1,2,0:T(1,128)S(1)}, u32[]{:S(2)}, u32[]{:S(2)}) %all-to-all-start.2) | async-done | bytes 133152 | tf_op jit(solution)/shard_map/all_to_all | solution.py:116
  67.9 0.7 copy.65.got_ref
  68.6 1.6 %shard_map.103 = (f32[64,128]{1,0:T(8,128)}, f32[1,128]{1,0:T(1,128)}, f32[64,128]{1,0:T(8,128)}, f32[1,128]{1,0:T(1,128)}) custom-call(s32[1]{0:T(128)} %bitcast.16.here_ref, f32[4,65,128]{2,1,0:T(8,128)} %copy.65.got_ref), custom_call_target="tpu_custom_call" | custom-call | tf_op jit(solution)/shard_map/pallas_call | solution.py:118
  70.2 1.8 %shard_map.104 = f32[4,128,128]{2,1,0:T(8,128)} custom-call(f32[4,64,128]{2,1,0:T(8,128)} %get-tuple-element.23.refs_0_, f32[4,1,128]{2,1,0:T(1,128)} %get-tuple-element.24.refs_1_, f32[4,64,128]{2,1,0:T(8,128)} %get-tuple-element.25.refs_2_, f32[4,1,128]{2,1,0:T(1,128)} %get-tuple-element.26.refs_3_, f32[64,128]{1,0:T(8,128)} %get-tuple-element.30.refs_4_, ...), custom_call_target="tpu_custom_call" | custom-call | tf_op jit(solution)/shard_map/pallas_call | solution.py:200
  71.9 3.4 %all-to-all-start.3 = ((f32[4,128,128]{2,1,0:T(8,128)}), f32[4,128,128]{2,1,0:T(8,128)S(1)}, u32[]{:S(2)}, u32[]{:S(2)}) async-start(f32[4,128,128]{2,1,0:T(8,128)} %shard_map.104), calls=%async_computation.3 | async-start | bytes 524288 | tf_op jit(solution)/shard_map/all_to_all | solution.py:201
  75.6 5.2 %all-to-all-done.3 = f32[4,128,128]{2,1,0:T(8,128)S(1)} async-done(((f32[4,128,128]{2,1,0:T(8,128)}), f32[4,128,128]{2,1,0:T(8,128)S(1)}, u32[]{:S(2)}, u32[]{:S(2)}) %all-to-all-start.3) | async-done | bytes 262176 | tf_op jit(solution)/shard_map/all_to_all | solution.py:201
  82.5 9.6 %all_to_all.30 = f32[8,2,16,256]{3,2,0,1:T(8,128)S(1)} all-to-all(f32[8,2,16,256]{3,2,0,1:T(8,128)S(1)} %copy.80), channel_id=1, replica_groups=mesh['level1'=4,'level0'=4,'inner'=4,'head_outer'=8,'head_inner'=2] {'he..., dimensions={1} | all-to-all | bytes 524288 | tf_op jit(solution)/shard_map/all_to_all | solution.py:209
  92.2 0.7 reduce_sum.48
  92.9 6.8 %all-to-all-start.5 = ((f32[8,16,256]{2,1,0:T(8,128)}), f32[8,16,256]{2,1,0:T(8,128)S(1)}, u32[]{:S(2)}, u32[]{:S(2)}) async-start(f32[8,16,256]{2,1,0:T(8,128)} %reduce_sum.48), calls=%async_computation.5 | async-start | bytes 262144 | tf_op jit(solution)/shard_map/all_to_all | solution.py:209
  100.0 0.7 fusion.5
  101.7 0.7 fusion.4
  103.9 0.8 copy.73
  104.8 0.8 copy.72
  105.6 2.0 %all-to-all-done.5 = f32[8,16,256]{2,1,0:T(8,128)S(1)} async-done(((f32[8,16,256]{2,1,0:T(8,128)}), f32[8,16,256]{2,1,0:T(8,128)S(1)}, u32[]{:S(2)}, u32[]{:S(2)}) %all-to-all-start.5) | async-done | bytes 131104 | tf_op jit(solution)/shard_map/all_to_all | solution.py:209
  (55 shorter events, 11.5 us)
Async XLA Ops:
  0.6 0.9 copy-start.7
  2.1 1.2 %copy-start.3 = (f32[256,256]{1,0:T(8,128)S(1)}, f32[256,256]{1,0:T(8,128)}, u32[]{:S(2)}) copy-start(f32[256,256]{1,0:T(8,128)} %param.11) | copy-start | bytes 786436
  3.2 0.7 copy-start.4
  3.9 0.9 copy-start
  4.8 0.9 copy-start.1
  7.3 10.5 %all-to-all-start = ((f32[4,129,128]{2,1,0:T(8,128)}), f32[4,129,128]{2,1,0:T(8,128)S(1)}, u32[]{:S(2)}, u32[]{:S(2)}) async-start(f32[4,129,128]{2,1,0:T(8,128)} %pad_maximum_fusion), calls=%async_computation | async-start | bytes 557056 | tf_op jit(solution)/shard_map/all_to_all | solution.py:193
  17.8 0.7 copy-start.2
  20.2 0.7 copy-start.6
  22.4 12.7 %all-to-all-start.1 = ((f32[4,1,129,128]{3,1,2,0:T(1,128)}), f32[4,1,129,128]{3,1,2,0:T(1,128)S(1)}, u32[]{:S(2)}, u32[]{:S(2)}) async-start(f32[4,1,129,128]{3,1,2,0:T(1,128)} %broadcast_in_dim.91), calls=%async_computation.1 | async-start | bytes 528384 | tf_op jit(solution)/shard_map/all_to_all | solution.py:116
  38.3 0.6 copy-start.5
  39.7 28.1 %all-to-all-start.2 = ((f32[4,1,65,128]{3,1,2,0:T(1,128)}), f32[4,1,65,128]{3,1,2,0:T(1,128)S(1)}, u32[]{:S(2)}, u32[]{:S(2)}) async-start(f32[4,1,65,128]{3,1,2,0:T(1,128)} %copy.63), calls=%async_computation.2 | async-start | bytes 266240 | tf_op jit(solution)/shard_map/all_to_all | solution.py:116
  71.9 8.9 %all-to-all-start.3 = ((f32[4,128,128]{2,1,0:T(8,128)}), f32[4,128,128]{2,1,0:T(8,128)S(1)}, u32[]{:S(2)}, u32[]{:S(2)}) async-start(f32[4,128,128]{2,1,0:T(8,128)} %shard_map.104), calls=%async_computation.3 | async-start | bytes 524288 | tf_op jit(solution)/shard_map/all_to_all | solution.py:201
  92.9 14.7 %all-to-all-start.5 = ((f32[8,16,256]{2,1,0:T(8,128)}), f32[8,16,256]{2,1,0:T(8,128)S(1)}, u32[]{:S(2)}, u32[]{:S(2)}) async-start(f32[8,16,256]{2,1,0:T(8,128)} %reduce_sum.48), calls=%async_computation.5 | async-start | bytes 262144 | tf_op jit(solution)/shard_map/all_to_all | solution.py:209

commit v10 on v9

--- a/solution.py
+++ b/solution.py
@@ -284,16 +284,32 @@
                 bwd_part,
             )
         )
-    unit_decay = jnp.ones((head_count,), dtype=jnp.float32)
-    zero_state = jnp.zeros((head_count, head_width, state_width), dtype=jnp.float32)
-    fwd_decay, fwd_state = (unit_decay, zero_state)
-    for entry in blocks:
-        fwd_decay = fwd_decay * entry[6]
-        fwd_state = entry[6][:, None, None] * fwd_state + entry[11]
-    bwd_decay, bwd_state = (unit_decay, zero_state)
-    for entry in reversed(blocks):
-        bwd_decay = bwd_decay * entry[6]
-        bwd_state = entry[12] + entry[6][:, None, None] * bwd_state
+    block_cum = jnp.dot(
+        log_decay.reshape(head_count * group_count, GROUP), lower_ones.T, precision=highest
+    ).reshape(head_count, group_count, GROUP)
+    block_final = block_cum[:, :, -1:]
+    block_decay = jnp.exp(block_final)
+    later = [None] * group_count
+    earlier = [None] * group_count
+    running = jnp.ones((head_count, 1), jnp.float32)
+    for position in range(group_count - 1, -1, -1):
+        later[position] = running
+        running = running * block_decay[:, position]
+    fwd_decay = running[:, 0]
+    running = jnp.ones((head_count, 1), jnp.float32)
+    for position in range(group_count):
+        earlier[position] = running
+        running = running * block_decay[:, position]
+    fwd_weight = jnp.concatenate(
+        [later[b] * jnp.exp(block_final[:, b] - block_cum[:, b]) for b in range(group_count)], axis=1
+    )
+    bwd_weight = jnp.concatenate(
+        [earlier[b] * jnp.exp(block_cum[:, b]) for b in range(group_count)], axis=1
+    )
+    fwd_rows = head_input.reshape(row_count, head_count, head_width) * (step_size * fwd_weight).T[:, :, None]
+    fwd_state = jnp.einsum("thp,tn->hpn", fwd_rows, write_proj, precision=highest)
+    bwd_rows = grad_out.reshape(row_count, head_count, head_width) * bwd_weight.T[:, :, None]
+    bwd_state = jnp.einsum("thp,tn->hpn", bwd_rows, read_proj, precision=highest)
     state_in, grad_in = both_prefixes(fwd_decay, fwd_state, bwd_state, levels)
     entering = []
     current = state_in

time: 109 us -> 112 us (1.028)
  blocking collectives: 9.64 us -> 20.2 us
  starting transfers between devices: 37.9 us -> 33.2 us
  waiting for transfers between devices: 28.3 us -> 27.1 us
    all_to_all x0 -> x1, blocking collectives: none -> 10.4 us  [both_prefixes(): mine = lax.all_to_all(packed, 'inner', 0, 0, tiled=True)]
    all_to_all x1 -> x0, waiting for transfers between devices: 4.96 us -> none  [both_prefixes(): mine = lax.all_to_all(packed, 'inner', 0, 0, tiled=True)]
    all_to_all x1 -> x0, starting transfers between devices: 4.83 us -> none  [both_prefixes(): mine = lax.all_to_all(packed, 'inner', 0, 0, tiled=True)]
    all_to_all x1, waiting for transfers between devices: 1.98 us -> 4.98 us  [head_scatter(): lax.all_to_all(blocks, axes[place], place, place, tiled=True)]
    unnamed x21 -> x22, local copies, waits for them, and re-layouts: 7.7 us -> 6.43 us
  transfers between devices with their start and end apart: 5 -> 4, of which waited for: 5 -> 4; matrix products, arithmetic and copies ran while one was open for 8% -> 4% of each run, Pallas kernels for 0% -> 0%
where the time goes in v10:
time: 112 us
  starting transfers between devices  33.2 us (30%)
  waiting for transfers between devices  27.1 us (24%)
  blocking collectives  20.2 us (18%)
  local copies, waits for them, and re-layouts  10.7 us (10%)
  matrix products  9.43 us (8%)
  Pallas kernels  6.65 us (6%)
  other arithmetic  3.29 us (3%)
    all_to_all x2, starting transfers between devices, level_exchange(): got = lax.all_to_all(sent, axis, 0, 0)  22.9 us
    all_to_all x2, waiting for transfers between devices, level_exchange(): got = lax.all_to_all(sent, axis, 0, 0)  16.7 us
    all_to_all x1, blocking collectives, both_prefixes(): mine = lax.all_to_all(packed, 'inner', 0, 0, tiled=True)  10.4 us
    all_to_all x1, blocking collectives, head_scatter(): lax.all_to_all(blocks, axes[place], place, place, tiled=True)  9.86 us
    all_to_all x1, starting transfers between devices, head_scatter(): lax.all_to_all(blocks, axes[place], place, place, tiled=True)  6.83 us
    unnamed x22, local copies, waits for them, and re-layouts  6.43 us
    all_to_all x1, waiting for transfers between devices, both_prefixes(): shared = lax.all_to_all(back, 'inner', 0, 0, tiled=True)  5.42 us
    all_to_all x1, waiting for transfers between devices, head_scatter(): lax.all_to_all(blocks, axes[place], place, place, tiled=True)  4.98 us
  transfers between devices with their start and end apart: 4, of which 4 were waited for; matrix products, arithmetic and copies ran while one was open for 4% of the time, Pallas kernels for 0%

profile of v10, /device:TPU:1, one launch (start us, length us, event | category | flops | bytes accessed | tf_op | source)
XLA Modules:
  0.0 111.6 jit_solution(3123718419311537432)
XLA Ops:
  0.6 0.7 reshape.100
  1.9 1.1 %copy.79 = f32[256,256]{0,1:T(8,128)S(1)} copy(f32[256,256]{1,0:T(8,128)} %param.6) | data formatting | bytes 524288 | tf_op args[0]
  3.3 0.7 copy-done.3
  5.4 10.4 %all_to_all.30.mine_ref = f32[4,129,128]{2,1,0:T(8,128)} all-to-all(f32[4,129,128]{2,1,0:T(8,128)S(1)} %pad_maximum_fusion), channel_id=1, replica_groups=mesh['level1'=4,'level0'=4,'inner'=4,'head_outer'=8,'head_inner'=2] {'in..., dimensions={0} | all-to-all | bytes 528384 | tf_op jit(solution)/shard_map/all_to_all | solution.py:193
  15.8 1.7 %shard_map.101 = (f32[4,64,128]{2,1,0:T(8,128)}, f32[4,1,128]{2,1,0:T(1,128)}, f32[4,64,128]{2,1,0:T(8,128)}, f32[4,1,128]{2,1,0:T(1,128)}, f32[64,128]{1,0:T(8,...) custom-call(f32[4,129,128]{2,1,0:T(8,128)} %all_to_all.30.mine_ref), custom_call_target="tpu_custom_call" | custom-call | tf_op jit(solution)/shard_map/pallas_call | solution.py:194
  17.5 0.7 copy-done.6
  18.1 0.8 maximum_bitcast_fusion
  18.9 0.8 broadcast_in_dim.87
  19.7 7.2 %all-to-all-start.1 = ((f32[4,1,129,128]{3,1,2,0:T(1,128)}), f32[4,1,129,128]{3,1,2,0:T(1,128)S(1)}, u32[]{:S(2)}, u32[]{:S(2)}) async-start(f32[4,1,129,128]{3,1,2,0:T(1,128)} %broadcast_in_dim.87), calls=%async_computation.1 | async-start | bytes 528384 | tf_op jit(solution)/shard_map/all_to_all | solution.py:116
  27.9 4.6 %all-to-all-done.1 = f32[4,1,129,128]{3,1,2,0:T(1,128)S(1)} async-done(((f32[4,1,129,128]{3,1,2,0:T(1,128)}), f32[4,1,129,128]{3,1,2,0:T(1,128)S(1)}, u32[]{:S(2)}, u32[]{:S(2)}) %all-to-all-start.1) | async-done | bytes 264224 | tf_op jit(solution)/shard_map/all_to_all | solution.py:116
  32.5 0.7 copy.114
  33.3 1.6 %shard_map.102 = (f32[64,128]{1,0:T(8,128)}, f32[1,128]{1,0:T(1,128)}, f32[64,128]{1,0:T(8,128)}, f32[1,128]{1,0:T(1,128)}, f32[64,128]{1,0:T(8,128)}, /*index=5*/f32[64,128]{1,0:T(8,128)}, f32[1,128]{1,0:T(1,128)}) custom-call(s32[1]{0:T(128)} %bitcast.18.here_ref, f32[4,129,128]{2,1,0:T(8,128)} %bitcast.139), custom_call_target="tpu_custom_call" | custom-call | tf_op jit(solution)/shard_map/pallas_call | solution.py:118
  34.9 0.8 select_bitcast_fusion.3
  36.4 0.8 copy.88
  37.1 15.8 %all-to-all-start.2 = ((f32[4,1,65,128]{3,1,2,0:T(1,128)}), f32[4,1,65,128]{3,1,2,0:T(1,128)S(1)}, u32[]{:S(2)}, u32[]{:S(2)}) async-start(f32[4,1,65,128]{3,1,2,0:T(1,128)} %copy.88), calls=%async_computation.2 | async-start | bytes 266240 | tf_op jit(solution)/shard_map/all_to_all | solution.py:116
  53.2 12.0 %all-to-all-done.2 = f32[4,1,65,128]{3,1,2,0:T(1,128)S(1)} async-done(((f32[4,1,65,128]{3,1,2,0:T(1,128)}), f32[4,1,65,128]{3,1,2,0:T(1,128)S(1)}, u32[]{:S(2)}, u32[]{:S(2)}) %all-to-all-start.2) | async-done | bytes 133152 | tf_op jit(solution)/shard_map/all_to_all | solution.py:116
  65.3 0.7 copy.90.got_ref
  66.0 1.6 %shard_map.103 = (f32[64,128]{1,0:T(8,128)}, f32[1,128]{1,0:T(1,128)}, f32[64,128]{1,0:T(8,128)}, f32[1,128]{1,0:T(1,128)}) custom-call(s32[1]{0:T(128)} %bitcast.23.here_ref, f32[4,65,128]{2,1,0:T(8,128)} %copy.90.got_ref), custom_call_target="tpu_custom_call" | custom-call | tf_op jit(solution)/shard_map/pallas_call | solution.py:118
  67.6 1.8 %shard_map.104 = f32[4,128,128]{2,1,0:T(8,128)} custom-call(f32[4,64,128]{2,1,0:T(8,128)} %get-tuple-element.23.refs_0_, f32[4,1,128]{2,1,0:T(1,128)} %get-tuple-element.24.refs_1_, f32[4,64,128]{2,1,0:T(8,128)} %get-tuple-element.25.refs_2_, f32[4,1,128]{2,1,0:T(1,128)} %get-tuple-element.26.refs_3_, f32[64,128]{1,0:T(8,128)} %get-tuple-element.30.refs_4_, ...), custom_call_target="tpu_custom_call" | custom-call | tf_op jit(solution)/shard_map/pallas_call | solution.py:200
  69.3 3.4 %all-to-all-start.3 = ((f32[4,128,128]{2,1,0:T(8,128)}), f32[4,128,128]{2,1,0:T(8,128)S(1)}, u32[]{:S(2)}, u32[]{:S(2)}) async-start(f32[4,128,128]{2,1,0:T(8,128)} %shard_map.104), calls=%async_computation.3 | async-start | bytes 524288 | tf_op jit(solution)/shard_map/all_to_all | solution.py:201
  72.8 5.4 %all-to-all-done.3 = f32[4,128,128]{2,1,0:T(8,128)S(1)} async-done(((f32[4,128,128]{2,1,0:T(8,128)}), f32[4,128,128]{2,1,0:T(8,128)S(1)}, u32[]{:S(2)}, u32[]{:S(2)}) %all-to-all-start.3) | async-done | bytes 262176 | tf_op jit(solution)/shard_map/all_to_all | solution.py:201
  78.8 0.7 fusion.5
  79.8 0.7 fusion.4
  80.5 0.7 multiply_reduce_fusion
  81.6 0.6 fusion.2
  82.2 0.6 fusion.3
  85.7 9.9 %all_to_all.31 = f32[8,2,16,256]{3,2,0,1:T(8,128)S(1)} all-to-all(f32[8,2,16,256]{3,2,0,1:T(8,128)S(1)} %copy.105), channel_id=1, replica_groups=mesh['level1'=4,'level0'=4,'inner'=4,'head_outer'=8,'head_inner'=2] {'he..., dimensions={1} | all-to-all | bytes 524288 | tf_op jit(solution)/shard_map/all_to_all | solution.py:209
  95.5 0.7 reduce_sum.48
  96.2 6.8 %all-to-all-start.5 = ((f32[8,16,256]{2,1,0:T(8,128)}), f32[8,16,256]{2,1,0:T(8,128)S(1)}, u32[]{:S(2)}, u32[]{:S(2)}) async-start(f32[8,16,256]{2,1,0:T(8,128)} %reduce_sum.48), calls=%async_computation.5 | async-start | bytes 262144 | tf_op jit(solution)/shard_map/all_to_all | solution.py:209
  104.3 0.8 copy.97
  105.1 0.8 copy.98
  106.0 5.0 %all-to-all-done.5 = f32[8,16,256]{2,1,0:T(8,128)S(1)} async-done(((f32[8,16,256]{2,1,0:T(8,128)}), f32[8,16,256]{2,1,0:T(8,128)S(1)}, u32[]{:S(2)}, u32[]{:S(2)}) %all-to-all-start.5) | async-done | bytes 131104 | tf_op jit(solution)/shard_map/all_to_all | solution.py:209
  (66 shorter events, 10.0 us)
Async XLA Ops:
  1.9 1.1 %copy-start.2 = (f32[256,256]{1,0:T(8,128)S(1)}, f32[256,256]{1,0:T(8,128)}, u32[]{:S(2)}) copy-start(f32[256,256]{1,0:T(8,128)} %param.11) | copy-start | bytes 786436
  3.1 0.9 copy-start
  3.3 0.7 copy-start.3
  4.0 0.9 copy-start.1
  17.5 0.7 copy-start.6
  19.7 7.2 %copy-start.4 = (f32[4,256]{1,0:T(4,128)S(1)}, f32[4,256]{1,0:T(4,128)}, u32[]{:S(2)}) copy-start(f32[4,256]{1,0:T(4,128)} %param.8) | copy-start | bytes 12292
  19.7 12.8 %all-to-all-start.1 = ((f32[4,1,129,128]{3,1,2,0:T(1,128)}), f32[4,1,129,128]{3,1,2,0:T(1,128)S(1)}, u32[]{:S(2)}, u32[]{:S(2)}) async-start(f32[4,1,129,128]{3,1,2,0:T(1,128)} %broadcast_in_dim.87), calls=%async_computation.1 | async-start | bytes 528384 | tf_op jit(solution)/shard_map/all_to_all | solution.py:116
  35.7 0.6 copy-start.5
  37.1 28.1 %all-to-all-start.2 = ((f32[4,1,65,128]{3,1,2,0:T(1,128)}), f32[4,1,65,128]{3,1,2,0:T(1,128)S(1)}, u32[]{:S(2)}, u32[]{:S(2)}) async-start(f32[4,1,65,128]{3,1,2,0:T(1,128)} %copy.88), calls=%async_computation.2 | async-start | bytes 266240 | tf_op jit(solution)/shard_map/all_to_all | solution.py:116
  69.3 8.9 %all-to-all-start.3 = ((f32[4,128,128]{2,1,0:T(8,128)}), f32[4,128,128]{2,1,0:T(8,128)S(1)}, u32[]{:S(2)}, u32[]{:S(2)}) async-start(f32[4,128,128]{2,1,0:T(8,128)} %shard_map.104), calls=%async_computation.3 | async-start | bytes 524288 | tf_op jit(solution)/shard_map/all_to_all | solution.py:201
  96.2 14.7 %all-to-all-start.5 = ((f32[8,16,256]{2,1,0:T(8,128)}), f32[8,16,256]{2,1,0:T(8,128)S(1)}, u32[]{:S(2)}, u32[]{:S(2)}) async-start(f32[8,16,256]{2,1,0:T(8,128)} %reduce_sum.48), calls=%async_computation.5 | async-start | bytes 262144 | tf_op jit(solution)/shard_map/all_to_all | solution.py:209

commit v11 on v9

--- a/solution.py
+++ b/solution.py
@@ -206,7 +206,14 @@
     sizes = [lax.axis_size(axis) for axis in axes]
     blocks = total.reshape(tuple(sizes) + (total.shape[0] // math.prod(sizes),) + total.shape[1:])
     for place in range(len(axes) - 1, -1, -1):
-        blocks = jnp.sum(lax.all_to_all(blocks, axes[place], place, place, tiled=True), axis=place)
+        if sizes[place] == 2:
+            upper = lax.axis_index(axes[place]) == 1
+            low = lax.index_in_dim(blocks, 0, place, keepdims=False)
+            high = lax.index_in_dim(blocks, 1, place, keepdims=False)
+            got = lax.ppermute(jnp.where(upper, low, high), axes[place], [(0, 1), (1, 0)])
+            blocks = jnp.where(upper, high, low) + got
+        else:
+            blocks = jnp.sum(lax.all_to_all(blocks, axes[place], place, place, tiled=True), axis=place)
     return blocks
 
 

time: 109 us -> 112 us (1.028)
  blocking collectives: 9.64 us -> 0 us
  starting transfers between devices: 37.9 us -> 45.8 us
  waiting for transfers between devices: 28.3 us -> 32.6 us
    all_to_all x1 -> x0, blocking collectives: 9.64 us -> none  [head_scatter(): lax.all_to_all(blocks, axes[place], place, place, tiled=True)]
    ppermute x0 -> x1, starting transfers between devices: none -> 7.97 us  [head_scatter(): lax.ppermute(jnp.where(upper, low, high), axes[place], [(0, 1), (1, 0)])]
    all_to_all x1, waiting for transfers between devices: 1.98 us -> 6.3 us  [head_scatter(): lax.all_to_all(blocks, axes[place], place, place, tiled=True)]
  transfers between devices with their start and end apart: 5 -> 6, of which waited for: 5 -> 5; matrix products, arithmetic and copies ran while one was open for 8% -> 8% of each run, Pallas kernels for 0% -> 0%
where the time goes in v11:
time: 112 us; the launch traced here: 111 us
  starting transfers between devices  45.8 us (41%)
  waiting for transfers between devices  32.6 us (29%)
  local copies, waits for them, and re-layouts  10.9 us (10%)
  matrix products  9.95 us (9%)
  Pallas kernels  6.66 us (6%)
  other arithmetic  3.91 us (3%)
    all_to_all x2, starting transfers between devices, level_exchange(): got = lax.all_to_all(sent, axis, 0, 0)  22.8 us
    all_to_all x2, waiting for transfers between devices, level_exchange(): got = lax.all_to_all(sent, axis, 0, 0)  16.1 us
    ppermute x1, starting transfers between devices, head_scatter(): lax.ppermute(jnp.where(upper, low, high), axes[place], [(0, 1), (1, 0)])  7.97 us
    unnamed x21, local copies, waits for them, and re-layouts  7.67 us
    all_to_all x1, starting transfers between devices, head_scatter(): lax.all_to_all(blocks, axes[place], place, place, tiled=True)  6.82 us
    all_to_all x1, waiting for transfers between devices, head_scatter(): lax.all_to_all(blocks, axes[place], place, place, tiled=True)  6.3 us
    all_to_all x1, waiting for transfers between devices, both_prefixes(): shared = lax.all_to_all(back, 'inner', 0, 0, tiled=True)  5.23 us
    all_to_all x1, waiting for transfers between devices, both_prefixes(): mine = lax.all_to_all(packed, 'inner', 0, 0, tiled=True)  4.96 us
  transfers between devices with their start and end apart: 6, of which 5 were waited for; matrix products, arithmetic and copies ran while one was open for 8% of the time, Pallas kernels for 0%

profile of v11, /device:TPU:1, one launch (start us, length us, event | category | flops | bytes accessed | tf_op | source)
XLA Modules:
  0.0 110.8 jit_solution(7240583534438240101)
XLA Ops:
  0.6 0.9 convolution_bitcast_fusion.8
  2.1 1.1 %copy.54 = f32[256,256]{0,1:T(8,128)S(1)} copy(f32[256,256]{1,0:T(8,128)} %param.6) | data formatting | bytes 524288 | tf_op args[0]
  3.9 0.9 copy-done
  6.6 0.7 pad_maximum_fusion
  7.3 4.8 %all-to-all-start = ((f32[4,129,128]{2,1,0:T(8,128)}), f32[4,129,128]{2,1,0:T(8,128)S(1)}, u32[]{:S(2)}, u32[]{:S(2)}) async-start(f32[4,129,128]{2,1,0:T(8,128)} %pad_maximum_fusion), calls=%async_computation | async-start | bytes 557056 | tf_op jit(solution)/shard_map/all_to_all | solution.py:193
  12.8 5.0 %all-to-all-done.mine_ref = f32[4,129,128]{2,1,0:T(8,128)S(1)} async-done(((f32[4,129,128]{2,1,0:T(8,128)}), f32[4,129,128]{2,1,0:T(8,128)S(1)}, u32[]{:S(2)}, u32[]{:S(2)}) %all-to-all-start) | async-done | bytes 264224 | tf_op jit(solution)/shard_map/all_to_all | solution.py:193
  17.8 0.7 copy-done.2
  18.5 1.7 %shard_map.101 = (f32[4,64,128]{2,1,0:T(8,128)}, f32[4,1,128]{2,1,0:T(1,128)}, f32[4,64,128]{2,1,0:T(8,128)}, f32[4,1,128]{2,1,0:T(1,128)}, f32[64,128]{1,0:T(8,...) custom-call(f32[4,129,128]{2,1,0:T(8,128)} %copy-done.2), custom_call_target="tpu_custom_call" | custom-call | tf_op jit(solution)/shard_map/pallas_call | solution.py:194
  20.2 0.7 copy-done.6
  20.8 0.8 maximum_bitcast_fusion
  21.6 0.8 broadcast_in_dim.91
  22.5 7.0 %all-to-all-start.1 = ((f32[4,1,129,128]{3,1,2,0:T(1,128)}), f32[4,1,129,128]{3,1,2,0:T(1,128)S(1)}, u32[]{:S(2)}, u32[]{:S(2)}) async-start(f32[4,1,129,128]{3,1,2,0:T(1,128)} %broadcast_in_dim.91), calls=%async_computation.1 | async-start | bytes 528384 | tf_op jit(solution)/shard_map/all_to_all | solution.py:116
  30.9 4.3 %all-to-all-done.1 = f32[4,1,129,128]{3,1,2,0:T(1,128)S(1)} async-done(((f32[4,1,129,128]{3,1,2,0:T(1,128)}), f32[4,1,129,128]{3,1,2,0:T(1,128)S(1)}, u32[]{:S(2)}, u32[]{:S(2)}) %all-to-all-start.1) | async-done | bytes 264224 | tf_op jit(solution)/shard_map/all_to_all | solution.py:116
  35.1 0.7 copy.81
  35.9 1.6 %shard_map.102 = (f32[64,128]{1,0:T(8,128)}, f32[1,128]{1,0:T(1,128)}, f32[64,128]{1,0:T(8,128)}, f32[1,128]{1,0:T(1,128)}, f32[64,128]{1,0:T(8,128)}, /*index=5*/f32[64,128]{1,0:T(8,128)}, f32[1,128]{1,0:T(1,128)}) custom-call(s32[1]{0:T(128)} %bitcast.11.here_ref, f32[4,129,128]{2,1,0:T(8,128)} %bitcast.132), custom_call_target="tpu_custom_call" | custom-call | tf_op jit(solution)/shard_map/pallas_call | solution.py:118
  37.5 0.8 select_bitcast_fusion.4
  38.9 0.8 copy.58
  39.7 15.8 %all-to-all-start.2 = ((f32[4,1,65,128]{3,1,2,0:T(1,128)}), f32[4,1,65,128]{3,1,2,0:T(1,128)S(1)}, u32[]{:S(2)}, u32[]{:S(2)}) async-start(f32[4,1,65,128]{3,1,2,0:T(1,128)} %copy.58), calls=%async_computation.2 | async-start | bytes 266240 | tf_op jit(solution)/shard_map/all_to_all | solution.py:116
  56.0 11.8 %all-to-all-done.2 = f32[4,1,65,128]{3,1,2,0:T(1,128)S(1)} async-done(((f32[4,1,65,128]{3,1,2,0:T(1,128)}), f32[4,1,65,128]{3,1,2,0:T(1,128)S(1)}, u32[]{:S(2)}, u32[]{:S(2)}) %all-to-all-start.2) | async-done | bytes 133152 | tf_op jit(solution)/shard_map/all_to_all | solution.py:116
  67.9 0.7 copy.60.got_ref
  68.6 1.6 %shard_map.103 = (f32[64,128]{1,0:T(8,128)}, f32[1,128]{1,0:T(1,128)}, f32[64,128]{1,0:T(8,128)}, f32[1,128]{1,0:T(1,128)}) custom-call(s32[1]{0:T(128)} %bitcast.16.here_ref, f32[4,65,128]{2,1,0:T(8,128)} %copy.60.got_ref), custom_call_target="tpu_custom_call" | custom-call | tf_op jit(solution)/shard_map/pallas_call | solution.py:118
  70.1 1.8 %shard_map.104 = f32[4,128,128]{2,1,0:T(8,128)} custom-call(f32[4,64,128]{2,1,0:T(8,128)} %get-tuple-element.23.refs_0_, f32[4,1,128]{2,1,0:T(1,128)} %get-tuple-element.24.refs_1_, f32[4,64,128]{2,1,0:T(8,128)} %get-tuple-element.25.refs_2_, f32[4,1,128]{2,1,0:T(1,128)} %get-tuple-element.26.refs_3_, f32[64,128]{1,0:T(8,128)} %get-tuple-element.30.refs_4_, ...), custom_call_target="tpu_custom_call" | custom-call | tf_op jit(solution)/shard_map/pallas_call | solution.py:200
  71.9 3.4 %all-to-all-start.3 = ((f32[4,128,128]{2,1,0:T(8,128)}), f32[4,128,128]{2,1,0:T(8,128)S(1)}, u32[]{:S(2)}, u32[]{:S(2)}) async-start(f32[4,128,128]{2,1,0:T(8,128)} %shard_map.104), calls=%async_computation.3 | async-start | bytes 524288 | tf_op jit(solution)/shard_map/all_to_all | solution.py:201
  75.6 5.2 %all-to-all-done.3 = f32[4,128,128]{2,1,0:T(8,128)S(1)} async-done(((f32[4,128,128]{2,1,0:T(8,128)}), f32[4,128,128]{2,1,0:T(8,128)S(1)}, u32[]{:S(2)}, u32[]{:S(2)}) %all-to-all-start.3) | async-done | bytes 262176 | tf_op jit(solution)/shard_map/all_to_all | solution.py:201
  82.5 8.0 %collective-permute-start = (f32[8,16,256]{2,1,0:T(8,128)S(1)}, f32[8,16,256]{2,1,0:T(8,128)S(1)}, u32[]{:S(2)}, u32[]{:S(2)}) collective-permute-start(f32[8,16,256]{2,1,0:T(8,128)S(1)} %select_bitcast_fusion), channel_id=1, source_target_pairs={{0,1},{1,0},{2,3},{3,2},{4,5},{5,4},{6,7},{7,6},{8,9},{9,8},{10,11... | collective-permute-start | bytes 393224 | tf_op jit(solution)/shard_map/ppermute | solution.py:213
  90.8 0.7 fusion.5
  92.5 0.7 fusion.4
  94.2 0.7 fusion.15
  94.9 6.8 %all-to-all-start.4 = ((f32[8,16,256]{2,1,0:T(8,128)}), f32[8,16,256]{2,1,0:T(8,128)S(1)}, u32[]{:S(2)}, u32[]{:S(2)}) async-start(f32[8,16,256]{2,1,0:T(8,128)} %fusion.15), calls=%async_computation.4 | async-start | bytes 262144 | tf_op jit(solution)/shard_map/all_to_all | solution.py:216
  102.2 0.8 copy.70
  103.1 0.8 copy.69
  103.9 6.3 %all-to-all-done.4 = f32[8,16,256]{2,1,0:T(8,128)S(1)} async-done(((f32[8,16,256]{2,1,0:T(8,128)}), f32[8,16,256]{2,1,0:T(8,128)S(1)}, u32[]{:S(2)}, u32[]{:S(2)}) %all-to-all-start.4) | async-done | bytes 131104 | tf_op jit(solution)/shard_map/all_to_all | solution.py:216
  (55 shorter events, 11.5 us)
Async XLA Ops:
  0.6 0.9 copy-start.7
  2.1 1.2 %copy-start.3 = (f32[256,256]{1,0:T(8,128)S(1)}, f32[256,256]{1,0:T(8,128)}, u32[]{:S(2)}) copy-start(f32[256,256]{1,0:T(8,128)} %param.11) | copy-start | bytes 786436
  3.2 0.7 copy-start.4
  3.9 0.9 copy-start
  4.8 0.9 copy-start.1
  7.3 10.4 %all-to-all-start = ((f32[4,129,128]{2,1,0:T(8,128)}), f32[4,129,128]{2,1,0:T(8,128)S(1)}, u32[]{:S(2)}, u32[]{:S(2)}) async-start(f32[4,129,128]{2,1,0:T(8,128)} %pad_maximum_fusion), calls=%async_computation | async-start | bytes 557056 | tf_op jit(solution)/shard_map/all_to_all | solution.py:193
  17.8 0.7 copy-start.2
  20.2 0.7 copy-start.6
  22.5 12.7 %all-to-all-start.1 = ((f32[4,1,129,128]{3,1,2,0:T(1,128)}), f32[4,1,129,128]{3,1,2,0:T(1,128)S(1)}, u32[]{:S(2)}, u32[]{:S(2)}) async-start(f32[4,1,129,128]{3,1,2,0:T(1,128)} %broadcast_in_dim.91), calls=%async_computation.1 | async-start | bytes 528384 | tf_op jit(solution)/shard_map/all_to_all | solution.py:116
  38.3 0.6 copy-start.5
  39.7 28.1 %all-to-all-start.2 = ((f32[4,1,65,128]{3,1,2,0:T(1,128)}), f32[4,1,65,128]{3,1,2,0:T(1,128)S(1)}, u32[]{:S(2)}, u32[]{:S(2)}) async-start(f32[4,1,65,128]{3,1,2,0:T(1,128)} %copy.58), calls=%async_computation.2 | async-start | bytes 266240 | tf_op jit(solution)/shard_map/all_to_all | solution.py:116
  71.9 8.9 %all-to-all-start.3 = ((f32[4,128,128]{2,1,0:T(8,128)}), f32[4,128,128]{2,1,0:T(8,128)S(1)}, u32[]{:S(2)}, u32[]{:S(2)}) async-start(f32[4,128,128]{2,1,0:T(8,128)} %shard_map.104), calls=%async_computation.3 | async-start | bytes 524288 | tf_op jit(solution)/shard_map/all_to_all | solution.py:201
  82.5 11.7 %collective-permute-start = (f32[8,16,256]{2,1,0:T(8,128)S(1)}, f32[8,16,256]{2,1,0:T(8,128)S(1)}, u32[]{:S(2)}, u32[]{:S(2)}) collective-permute-start(f32[8,16,256]{2,1,0:T(8,128)S(1)} %select_bitcast_fusion), channel_id=1, source_target_pairs={{0,1},{1,0},{2,3},{3,2},{4,5},{5,4},{6,7},{7,6},{8,9},{9,8},{10,11... | collective-permute-start | bytes 393224 | tf_op jit(solution)/shard_map/ppermute | solution.py:213
  94.9 15.3 %all-to-all-start.4 = ((f32[8,16,256]{2,1,0:T(8,128)}), f32[8,16,256]{2,1,0:T(8,128)S(1)}, u32[]{:S(2)}, u32[]{:S(2)}) async-start(f32[8,16,256]{2,1,0:T(8,128)} %fusion.15), calls=%async_computation.4 | async-start | bytes 262144 | tf_op jit(solution)/shard_map/all_to_all | solution.py:216

commit v12 on v9

--- a/solution.py
+++ b/solution.py
@@ -102,7 +102,7 @@
     )
 
 
-def level_exchange(aggregate, axis, last):
+def level_exchange(aggregate, axis, last, ready=None):
     count, here = (lax.axis_size(axis), lax.axis_index(axis))
     tail, fwd, bwd = aggregate
     width = fwd.shape[1]
@@ -110,6 +110,8 @@
         sent = jnp.stack(
             [jnp.concatenate([jnp.where(m < here, bwd, fwd), tail], axis=1) for m in range(count)]
         )
+    elif ready is not None:
+        sent = ready
     else:
         packed = jnp.concatenate([fwd, bwd, tail], axis=1)
         sent = jnp.broadcast_to(packed[None], (count,) + packed.shape)
@@ -121,8 +123,8 @@
     return (outs[:4], (outs[6][None], outs[4][None], outs[5][None]))
 
 
-def inner_kernel(members, width):
-    def kernel(mine_ref, bs_ref, bd_ref, as_ref, ad_ref, sf_ref, sb_ref, sd_ref):
+def inner_kernel(members, width, copies):
+    def kernel(mine_ref, bs_ref, bd_ref, as_ref, ad_ref, sf_ref, sb_ref, sd_ref, packed_ref):
         rows = 2 * width + 1
         decays = [mine_ref[m, rows - 1 : rows, :] for m in range(members)]
         run_state = jnp.zeros((width, 128), jnp.float32)
@@ -142,12 +144,17 @@
             run_state = mine_ref[m, width : 2 * width, :] + decays[m] * run_state
             run_decay = run_decay * decays[m]
         sb_ref[...] = run_state
+        for c in range(copies):
+            packed_ref[c, 0, 0:width, :] = sf_ref[...]
+            packed_ref[c, 0, width : 2 * width, :] = run_state
+            packed_ref[c, 0, 2 * width : 2 * width + 1, :] = sd_ref[...]
 
     many = jax.ShapeDtypeStruct((members, width, 128), jnp.float32)
     many_rows = jax.ShapeDtypeStruct((members, 1, 128), jnp.float32)
     state = jax.ShapeDtypeStruct((width, 128), jnp.float32)
     row = jax.ShapeDtypeStruct((1, 128), jnp.float32)
-    shapes = (many, many_rows, many, many_rows, state, state, row)
+    packed = jax.ShapeDtypeStruct((copies, 1, 2 * width + 1, 128), jnp.float32)
+    shapes = (many, many_rows, many, many_rows, state, state, row, packed)
     vmem = pl.BlockSpec(memory_space=pltpu.VMEM)
     return pl.pallas_call(
         kernel, out_shape=shapes, in_specs=[vmem], out_specs=tuple(vmem for _ in shapes), interpret=INTERPRET
@@ -191,11 +198,12 @@
         axis=1,
     )
     mine = lax.all_to_all(packed, "inner", 0, 0, tiled=True)
-    prefixes = inner_kernel(members, width)(mine)
+    prefixes = inner_kernel(members, width, lax.axis_size(levels[0]))(mine)
     aggregate = (prefixes[6][None], prefixes[4][None], prefixes[5][None])
     level_parts = []
     for at, axis in enumerate(levels):
-        parts, aggregate = level_exchange(aggregate, axis, at == len(levels) - 1)
+        ready = prefixes[7] if at == 0 and len(levels) > 1 else None
+        parts, aggregate = level_exchange(aggregate, axis, at == len(levels) - 1, ready)
         level_parts += list(parts)
     back = back_kernel(members, width, len(levels))(*prefixes[:4], *level_parts)
     shared = lax.all_to_all(back, "inner", 0, 0, tiled=True)

time: 109 us -> 109 us (level)
    pallas_call x0 -> x1, local copies, waits for them, and re-layouts: none -> 1.94 us  [both_prefixes(): prefixes = inner_kernel(members, width, lax.axis_size(levels[0]))(mine)]
    unnamed x21 -> x19, local copies, waits for them, and re-layouts: 7.7 us -> 7.1 us
where the time goes in v12:
time: 109 us; the launch traced here: 108 us
  starting transfers between devices  37.9 us (35%)
  waiting for transfers between devices  28.3 us (26%)
  local copies, waits for them, and re-layouts  11.5 us (11%)
  matrix products  9.95 us (9%)
  blocking collectives  9.64 us (9%)
  Pallas kernels  6.74 us (6%)
  other arithmetic  3.12 us (3%)
    all_to_all x2, starting transfers between devices, level_exchange(): got = lax.all_to_all(sent, axis, 0, 0)  22.8 us
    all_to_all x2, waiting for transfers between devices, level_exchange(): got = lax.all_to_all(sent, axis, 0, 0)  16.1 us
    all_to_all x1, blocking collectives, head_scatter(): lax.all_to_all(blocks, axes[place], place, place, tiled=True)  9.64 us
    unnamed x19, local copies, waits for them, and re-layouts  7.1 us
    all_to_all x1, starting transfers between devices, head_scatter(): lax.all_to_all(blocks, axes[place], place, place, tiled=True)  6.81 us
    all_to_all x1, waiting for transfers between devices, both_prefixes(): shared = lax.all_to_all(back, 'inner', 0, 0, tiled=True)  5.23 us
    all_to_all x1, waiting for transfers between devices, both_prefixes(): mine = lax.all_to_all(packed, 'inner', 0, 0, tiled=True)  4.96 us
    all_to_all x1, starting transfers between devices, both_prefixes(): mine = lax.all_to_all(packed, 'inner', 0, 0, tiled=True)  4.83 us
  transfers between devices with their start and end apart: 5, of which 5 were waited for; matrix products, arithmetic and copies ran while one was open for 8% of the time, Pallas kernels for 0%

profile of v12, /device:TPU:1, one launch (start us, length us, event | category | flops | bytes accessed | tf_op | source)
XLA Modules:
  0.0 108.0 jit_solution(9523860435095941759)
XLA Ops:
  0.6 0.9 convolution_bitcast_fusion.8
  2.1 1.1 %copy.63 = f32[256,256]{0,1:T(8,128)S(1)} copy(f32[256,256]{1,0:T(8,128)} %param.6) | data formatting | bytes 524288 | tf_op args[0]
  3.9 0.9 copy-done
  6.6 0.7 pad_maximum_fusion
  7.3 4.8 %all-to-all-start = ((f32[4,129,128]{2,1,0:T(8,128)}), f32[4,129,128]{2,1,0:T(8,128)S(1)}, u32[]{:S(2)}, u32[]{:S(2)}) async-start(f32[4,129,128]{2,1,0:T(8,128)} %pad_maximum_fusion), calls=%async_computation | async-start | bytes 557056 | tf_op jit(solution)/shard_map/all_to_all | solution.py:200
  12.8 5.0 %all-to-all-done.mine_ref = f32[4,129,128]{2,1,0:T(8,128)S(1)} async-done(((f32[4,129,128]{2,1,0:T(8,128)}), f32[4,129,128]{2,1,0:T(8,128)S(1)}, u32[]{:S(2)}, u32[]{:S(2)}) %all-to-all-start) | async-done | bytes 264224 | tf_op jit(solution)/shard_map/all_to_all | solution.py:200
  17.8 0.7 copy-done.2
  18.5 1.8 %shard_map.101 = (f32[4,64,128]{2,1,0:T(8,128)}, f32[4,1,128]{2,1,0:T(1,128)}, f32[4,64,128]{2,1,0:T(8,128)}, f32[4,1,128]{2,1,0:T(1,128)}, f32[64,128]{1,0:T(8,...) custom-call(f32[4,129,128]{2,1,0:T(8,128)} %copy-done.2), custom_call_target="tpu_custom_call" | custom-call | tf_op jit(solution)/shard_map/pallas_call | solution.py:201
  20.3 1.9 %copy.67 = f32[4,1,129,128]{3,1,2,0:T(1,128)} copy(f32[4,1,129,128]{3,2,1,0:T(8,128)} %get-tuple-element.25) | data formatting | bytes 528384 | tf_op jit(solution)/shard_map/pallas_call | solution.py:201
  22.2 7.1 %all-to-all-start.1 = ((f32[4,1,129,128]{3,1,2,0:T(1,128)}), f32[4,1,129,128]{3,1,2,0:T(1,128)S(1)}, u32[]{:S(2)}, u32[]{:S(2)}) async-start(f32[4,1,129,128]{3,1,2,0:T(1,128)} %copy.67), calls=%async_computation.1 | async-start | bytes 528384 | tf_op jit(solution)/shard_map/all_to_all | solution.py:118
  30.6 4.3 %all-to-all-done.1 = f32[4,1,129,128]{3,1,2,0:T(1,128)S(1)} async-done(((f32[4,1,129,128]{3,1,2,0:T(1,128)}), f32[4,1,129,128]{3,1,2,0:T(1,128)S(1)}, u32[]{:S(2)}, u32[]{:S(2)}) %all-to-all-start.1) | async-done | bytes 264224 | tf_op jit(solution)/shard_map/all_to_all | solution.py:118
  34.9 0.7 copy.89
  35.6 1.6 %shard_map.102 = (f32[64,128]{1,0:T(8,128)}, f32[1,128]{1,0:T(1,128)}, f32[64,128]{1,0:T(8,128)}, f32[1,128]{1,0:T(1,128)}, f32[64,128]{1,0:T(8,128)}, /*index=5*/f32[64,128]{1,0:T(8,128)}, f32[1,128]{1,0:T(1,128)}) custom-call(s32[1]{0:T(128)} %bitcast.11.here_ref, f32[4,129,128]{2,1,0:T(8,128)} %bitcast.105), custom_call_target="tpu_custom_call" | custom-call | tf_op jit(solution)/shard_map/pallas_call | solution.py:120
  37.3 0.8 select_bitcast_fusion.3
  38.1 0.7 copy-done.5
  38.8 0.8 copy.68
  39.5 15.8 %all-to-all-start.2 = ((f32[4,1,65,128]{3,1,2,0:T(1,128)}), f32[4,1,65,128]{3,1,2,0:T(1,128)S(1)}, u32[]{:S(2)}, u32[]{:S(2)}) async-start(f32[4,1,65,128]{3,1,2,0:T(1,128)} %copy.68), calls=%async_computation.2 | async-start | bytes 266240 | tf_op jit(solution)/shard_map/all_to_all | solution.py:118
  55.9 11.8 %all-to-all-done.2 = f32[4,1,65,128]{3,1,2,0:T(1,128)S(1)} async-done(((f32[4,1,65,128]{3,1,2,0:T(1,128)}), f32[4,1,65,128]{3,1,2,0:T(1,128)S(1)}, u32[]{:S(2)}, u32[]{:S(2)}) %all-to-all-start.2) | async-done | bytes 133152 | tf_op jit(solution)/shard_map/all_to_all | solution.py:118
  67.7 0.7 copy.70.got_ref
  68.4 1.6 %shard_map.103 = (f32[64,128]{1,0:T(8,128)}, f32[1,128]{1,0:T(1,128)}, f32[64,128]{1,0:T(8,128)}, f32[1,128]{1,0:T(1,128)}) custom-call(s32[1]{0:T(128)} %bitcast.12.here_ref, f32[4,65,128]{2,1,0:T(8,128)} %copy.70.got_ref), custom_call_target="tpu_custom_call" | custom-call | tf_op jit(solution)/shard_map/pallas_call | solution.py:120
  70.0 1.8 %shard_map.104 = f32[4,128,128]{2,1,0:T(8,128)} custom-call(f32[4,64,128]{2,1,0:T(8,128)} %get-tuple-element.21.refs_0_, f32[4,1,128]{2,1,0:T(1,128)} %get-tuple-element.22.refs_1_, f32[4,64,128]{2,1,0:T(8,128)} %get-tuple-element.23.refs_2_, f32[4,1,128]{2,1,0:T(1,128)} %get-tuple-element.24.refs_3_, f32[64,128]{1,0:T(8,128)} %get-tuple-element.26.refs_4_, ...), custom_call_target="tpu_custom_call" | custom-call | tf_op jit(solution)/shard_map/pallas_call | solution.py:208
  71.7 3.4 %all-to-all-start.3 = ((f32[4,128,128]{2,1,0:T(8,128)}), f32[4,128,128]{2,1,0:T(8,128)S(1)}, u32[]{:S(2)}, u32[]{:S(2)}) async-start(f32[4,128,128]{2,1,0:T(8,128)} %shard_map.104), calls=%async_computation.3 | async-start | bytes 524288 | tf_op jit(solution)/shard_map/all_to_all | solution.py:209
  75.4 5.2 %all-to-all-done.3 = f32[4,128,128]{2,1,0:T(8,128)S(1)} async-done(((f32[4,128,128]{2,1,0:T(8,128)}), f32[4,128,128]{2,1,0:T(8,128)S(1)}, u32[]{:S(2)}, u32[]{:S(2)}) %all-to-all-start.3) | async-done | bytes 262176 | tf_op jit(solution)/shard_map/all_to_all | solution.py:209
  82.4 9.6 %all_to_all.30 = f32[8,2,16,256]{3,2,0,1:T(8,128)S(1)} all-to-all(f32[8,2,16,256]{3,2,0,1:T(8,128)S(1)} %copy.85), channel_id=1, replica_groups=mesh['level1'=4,'level0'=4,'inner'=4,'head_outer'=8,'head_inner'=2] {'he..., dimensions={1} | all-to-all | bytes 524288 | tf_op jit(solution)/shard_map/all_to_all | solution.py:217
  92.0 0.7 reduce_sum.48
  92.7 6.8 %all-to-all-start.5 = ((f32[8,16,256]{2,1,0:T(8,128)}), f32[8,16,256]{2,1,0:T(8,128)S(1)}, u32[]{:S(2)}, u32[]{:S(2)}) async-start(f32[8,16,256]{2,1,0:T(8,128)} %reduce_sum.48), calls=%async_computation.5 | async-start | bytes 262144 | tf_op jit(solution)/shard_map/all_to_all | solution.py:217
  99.8 0.7 fusion.5
  101.6 0.7 fusion.4
  102.3 0.6 multiply_reduce_fusion
  103.7 0.8 copy.78
  104.6 0.8 copy.77
  105.4 2.0 %all-to-all-done.5 = f32[8,16,256]{2,1,0:T(8,128)S(1)} async-done(((f32[8,16,256]{2,1,0:T(8,128)}), f32[8,16,256]{2,1,0:T(8,128)S(1)}, u32[]{:S(2)}, u32[]{:S(2)}) %all-to-all-start.5) | async-done | bytes 131104 | tf_op jit(solution)/shard_map/all_to_all | solution.py:217
  (52 shorter events, 10.3 us)
Async XLA Ops:
  0.6 0.9 copy-start.6
  2.1 1.2 %copy-start.3 = (f32[256,256]{1,0:T(8,128)S(1)}, f32[256,256]{1,0:T(8,128)}, u32[]{:S(2)}) copy-start(f32[256,256]{1,0:T(8,128)} %param.11) | copy-start | bytes 786436
  3.2 0.7 copy-start.4
  3.9 0.9 copy-start
  4.8 0.9 copy-start.1
  7.3 10.5 %all-to-all-start = ((f32[4,129,128]{2,1,0:T(8,128)}), f32[4,129,128]{2,1,0:T(8,128)S(1)}, u32[]{:S(2)}, u32[]{:S(2)}) async-start(f32[4,129,128]{2,1,0:T(8,128)} %pad_maximum_fusion), calls=%async_computation | async-start | bytes 557056 | tf_op jit(solution)/shard_map/all_to_all | solution.py:200
  17.8 0.7 copy-start.2
  22.2 12.7 %all-to-all-start.1 = ((f32[4,1,129,128]{3,1,2,0:T(1,128)}), f32[4,1,129,128]{3,1,2,0:T(1,128)S(1)}, u32[]{:S(2)}, u32[]{:S(2)}) async-start(f32[4,1,129,128]{3,1,2,0:T(1,128)} %copy.67), calls=%async_computation.1 | async-start | bytes 528384 | tf_op jit(solution)/shard_map/all_to_all | solution.py:118
  38.0 0.7 copy-start.5
  39.5 28.1 %all-to-all-start.2 = ((f32[4,1,65,128]{3,1,2,0:T(1,128)}), f32[4,1,65,128]{3,1,2,0:T(1,128)S(1)}, u32[]{:S(2)}, u32[]{:S(2)}) async-start(f32[4,1,65,128]{3,1,2,0:T(1,128)} %copy.68), calls=%async_computation.2 | async-start | bytes 266240 | tf_op jit(solution)/shard_map/all_to_all | solution.py:118
  71.7 8.9 %all-to-all-start.3 = ((f32[4,128,128]{2,1,0:T(8,128)}), f32[4,128,128]{2,1,0:T(8,128)S(1)}, u32[]{:S(2)}, u32[]{:S(2)}) async-start(f32[4,128,128]{2,1,0:T(8,128)} %shard_map.104), calls=%async_computation.3 | async-start | bytes 524288 | tf_op jit(solution)/shard_map/all_to_all | solution.py:209
  92.7 14.7 %all-to-all-start.5 = ((f32[8,16,256]{2,1,0:T(8,128)}), f32[8,16,256]{2,1,0:T(8,128)S(1)}, u32[]{:S(2)}, u32[]{:S(2)}) async-start(f32[8,16,256]{2,1,0:T(8,128)} %reduce_sum.48), calls=%async_computation.5 | async-start | bytes 262144 | tf_op jit(solution)/shard_map/all_to_all | solution.py:217

commit v13 on v12

--- a/solution.py
+++ b/solution.py
@@ -50,7 +50,7 @@
 INTERPRET = False
 
 
-def level_kernel(count, width, last):
+def level_kernel(count, width, last, next_count=0):
     rows = width + 1 if last else 2 * width + 1
 
     def kernel(here_ref, got_ref, *outs):
@@ -88,10 +88,17 @@
             outs[4][...] = span_fwd
             outs[5][...] = span_bwd
             outs[6][...] = span_decay
+            if next_count:
+                following = here_ref[1]
+                for m in range(next_count):
+                    outs[7][m, 0, 0:width, :] = jnp.where(m < following, span_bwd, span_fwd)
+                    outs[7][m, 0, width : width + 1, :] = span_decay
 
     state = jax.ShapeDtypeStruct((width, 128), jnp.float32)
     row = jax.ShapeDtypeStruct((1, 128), jnp.float32)
     shapes = (state, row, state, row) + (() if last else (state, state, row))
+    if next_count:
+        shapes = shapes + (jax.ShapeDtypeStruct((next_count, 1, width + 1, 128), jnp.float32),)
     vmem = pl.BlockSpec(memory_space=pltpu.VMEM)
     return pl.pallas_call(
         kernel,
@@ -102,11 +109,14 @@
     )
 
 
-def level_exchange(aggregate, axis, last, ready=None):
+def level_exchange(aggregate, axis, last, ready=None, next_axis=None):
     count, here = (lax.axis_size(axis), lax.axis_index(axis))
-    tail, fwd, bwd = aggregate
-    width = fwd.shape[1]
-    if last:
+    width = aggregate[1].shape[1] if isinstance(aggregate, tuple) else aggregate.shape[2] - 1
+    if isinstance(aggregate, tuple):
+        tail, fwd, bwd = aggregate
+    if last and not isinstance(aggregate, tuple):
+        sent = aggregate
+    elif last:
         sent = jnp.stack(
             [jnp.concatenate([jnp.where(m < here, bwd, fwd), tail], axis=1) for m in range(count)]
         )
@@ -117,9 +127,14 @@
         sent = jnp.broadcast_to(packed[None], (count,) + packed.shape)
     got = lax.all_to_all(sent, axis, 0, 0)
     got = got.reshape((count,) + got.shape[2:])
-    outs = level_kernel(count, width, last)(jnp.reshape(here, (1,)).astype(jnp.int32), got)
+    next_count = lax.axis_size(next_axis) if next_axis is not None else 0
+    following = lax.axis_index(next_axis) if next_axis is not None else 0
+    indices = jnp.stack([jnp.asarray(here, jnp.int32), jnp.asarray(following, jnp.int32)])
+    outs = level_kernel(count, width, last, next_count)(indices, got)
     if last:
         return (outs, None)
+    if next_count:
+        return (outs[:4], outs[7])
     return (outs[:4], (outs[6][None], outs[4][None], outs[5][None]))
 
 
@@ -203,7 +218,8 @@
     level_parts = []
     for at, axis in enumerate(levels):
         ready = prefixes[7] if at == 0 and len(levels) > 1 else None
-        parts, aggregate = level_exchange(aggregate, axis, at == len(levels) - 1, ready)
+        following = levels[at + 1] if at + 2 == len(levels) else None
+        parts, aggregate = level_exchange(aggregate, axis, at == len(levels) - 1, ready, following)
         level_parts += list(parts)
     back = back_kernel(members, width, len(levels))(*prefixes[:4], *level_parts)
     shared = lax.all_to_all(back, "inner", 0, 0, tiled=True)

time: 109 us -> 108 us (level)
  waiting for transfers between devices: 28.3 us -> 27.1 us
    pallas_call x0 -> x1, local copies, waits for them, and re-layouts: none -> 1.7 us  [level_exchange(): outs = level_kernel(count, width, last, next_count)(indices, got)]
    another operation x2, other arithmetic: 0.03 us -> 1.17 us  [level_exchange(): jnp.stack([jnp.asarray(here, jnp.int32), jnp.asarray(following, jnp.int32)])]
    unnamed x19 -> x17, local copies, waits for them, and re-layouts: 7.1 us -> 6.44 us
  transfers between devices with their start and end apart: 5 -> 5, of which waited for: 5 -> 5; matrix products, arithmetic and copies ran while one was open for 8% -> 9% of each run, Pallas kernels for 0% -> 0%
where the time goes in v13:
time: 108 us; the launch traced here: 107 us
  starting transfers between devices  37.9 us (35%)
  waiting for transfers between devices  27.1 us (25%)
  local copies, waits for them, and re-layouts  11.7 us (11%)
  matrix products  9.94 us (9%)
  blocking collectives  9.64 us (9%)
  Pallas kernels  6.82 us (6%)
  other arithmetic  3.48 us (3%)
    all_to_all x2, starting transfers between devices, level_exchange(): got = lax.all_to_all(sent, axis, 0, 0)  22.8 us
    all_to_all x2, waiting for transfers between devices, level_exchange(): got = lax.all_to_all(sent, axis, 0, 0)  15.6 us
    all_to_all x1, blocking collectives, head_scatter(): lax.all_to_all(blocks, axes[place], place, place, tiled=True)  9.64 us
    all_to_all x1, starting transfers between devices, head_scatter(): lax.all_to_all(blocks, axes[place], place, place, tiled=True)  6.82 us
    unnamed x17, local copies, waits for them, and re-layouts  6.44 us
    all_to_all x1, waiting for transfers between devices, both_prefixes(): shared = lax.all_to_all(back, 'inner', 0, 0, tiled=True)  5.23 us
    all_to_all x1, starting transfers between devices, both_prefixes(): mine = lax.all_to_all(packed, 'inner', 0, 0, tiled=True)  4.83 us
    all_to_all x1, waiting for transfers between devices, both_prefixes(): mine = lax.all_to_all(packed, 'inner', 0, 0, tiled=True)  4.32 us
  transfers between devices with their start and end apart: 5, of which 5 were waited for; matrix products, arithmetic and copies ran while one was open for 9% of the time, Pallas kernels for 0%

profile of v13, /device:TPU:1, one launch (start us, length us, event | category | flops | bytes accessed | tf_op | source)
XLA Modules:
  0.0 107.5 jit_solution(14307951595604678698)
XLA Ops:
  0.6 0.9 convolution_bitcast_fusion.8
  2.1 1.1 %copy.65 = f32[256,256]{0,1:T(8,128)S(1)} copy(f32[256,256]{1,0:T(8,128)} %param.6) | data formatting | bytes 524288 | tf_op args[0]
  3.9 0.9 copy-done
  5.1 0.6 copy-done.1
  6.6 0.7 pad_maximum_fusion
  7.3 4.8 %all-to-all-start = ((f32[4,129,128]{2,1,0:T(8,128)}), f32[4,129,128]{2,1,0:T(8,128)S(1)}, u32[]{:S(2)}, u32[]{:S(2)}) async-start(f32[4,129,128]{2,1,0:T(8,128)} %pad_maximum_fusion), calls=%async_computation | async-start | bytes 557056 | tf_op jit(solution)/shard_map/all_to_all | solution.py:215
  12.8 0.6 fusion.2
  13.5 4.3 %all-to-all-done.mine_ref = f32[4,129,128]{2,1,0:T(8,128)S(1)} async-done(((f32[4,129,128]{2,1,0:T(8,128)}), f32[4,129,128]{2,1,0:T(8,128)S(1)}, u32[]{:S(2)}, u32[]{:S(2)}) %all-to-all-start) | async-done | bytes 264224 | tf_op jit(solution)/shard_map/all_to_all | solution.py:215
  17.8 0.7 copy-done.2
  18.5 1.8 %shard_map.101 = (f32[4,64,128]{2,1,0:T(8,128)}, f32[4,1,128]{2,1,0:T(1,128)}, f32[4,64,128]{2,1,0:T(8,128)}, f32[4,1,128]{2,1,0:T(1,128)}, f32[64,128]{1,0:T(8,...) custom-call(f32[4,129,128]{2,1,0:T(8,128)} %copy-done.2), custom_call_target="tpu_custom_call" | custom-call | tf_op jit(solution)/shard_map/pallas_call | solution.py:216
  20.3 1.9 %copy.69 = f32[4,1,129,128]{3,1,2,0:T(1,128)} copy(f32[4,1,129,128]{3,2,1,0:T(8,128)} %get-tuple-element.23) | data formatting | bytes 528384 | tf_op jit(solution)/shard_map/pallas_call | solution.py:216
  22.2 7.0 %all-to-all-start.1 = ((f32[4,1,129,128]{3,1,2,0:T(1,128)}), f32[4,1,129,128]{3,1,2,0:T(1,128)S(1)}, u32[]{:S(2)}, u32[]{:S(2)}) async-start(f32[4,1,129,128]{3,1,2,0:T(1,128)} %copy.69), calls=%async_computation.1 | async-start | bytes 528384 | tf_op jit(solution)/shard_map/all_to_all | solution.py:128
  30.5 4.3 %all-to-all-done.1 = f32[4,1,129,128]{3,1,2,0:T(1,128)S(1)} async-done(((f32[4,1,129,128]{3,1,2,0:T(1,128)}), f32[4,1,129,128]{3,1,2,0:T(1,128)S(1)}, u32[]{:S(2)}, u32[]{:S(2)}) %all-to-all-start.1) | async-done | bytes 264224 | tf_op jit(solution)/shard_map/all_to_all | solution.py:128
  34.9 0.7 copy.91
  35.6 1.7 %shard_map.102 = (f32[64,128]{1,0:T(8,128)}, f32[1,128]{1,0:T(1,128)}, f32[64,128]{1,0:T(8,128)}, f32[1,128]{1,0:T(1,128)}, f32[64,128]{1,0:T(8,128)}, /*index=5...) custom-call(s32[2]{0:T(128)} %pad_add_fusion.here_ref, f32[4,129,128]{2,1,0:T(8,128)} %bitcast.88), custom_call_target="tpu_custom_call" | custom-call | tf_op jit(solution)/shard_map/pallas_call | solution.py:133
  37.3 1.7 %copy.70 = f32[4,1,65,128]{3,1,2,0:T(1,128)} copy(f32[4,1,65,128]{3,2,1,0:T(8,128)} %get-tuple-element.28) | data formatting | bytes 266240 | tf_op jit(solution)/shard_map/pallas_call | solution.py:133
  39.0 15.8 %all-to-all-start.2 = ((f32[4,1,65,128]{3,1,2,0:T(1,128)}), f32[4,1,65,128]{3,1,2,0:T(1,128)S(1)}, u32[]{:S(2)}, u32[]{:S(2)}) async-start(f32[4,1,65,128]{3,1,2,0:T(1,128)} %copy.70), calls=%async_computation.2 | async-start | bytes 266240 | tf_op jit(solution)/shard_map/all_to_all | solution.py:128
  55.9 11.2 %all-to-all-done.2 = f32[4,1,65,128]{3,1,2,0:T(1,128)S(1)} async-done(((f32[4,1,65,128]{3,1,2,0:T(1,128)}), f32[4,1,65,128]{3,1,2,0:T(1,128)S(1)}, u32[]{:S(2)}, u32[]{:S(2)}) %all-to-all-start.2) | async-done | bytes 133152 | tf_op jit(solution)/shard_map/all_to_all | solution.py:128
  67.2 0.7 copy.72.got_ref
  67.9 1.6 %shard_map.103 = (f32[64,128]{1,0:T(8,128)}, f32[1,128]{1,0:T(1,128)}, f32[64,128]{1,0:T(8,128)}, f32[1,128]{1,0:T(1,128)}) custom-call(s32[2]{0:T(128)} %pad_add_fusion.1.here_ref, f32[4,65,128]{2,1,0:T(8,128)} %copy.72.got_ref), custom_call_target="tpu_custom_call" | custom-call | tf_op jit(solution)/shard_map/pallas_call | solution.py:133
  69.5 1.8 %shard_map.104 = f32[4,128,128]{2,1,0:T(8,128)} custom-call(f32[4,64,128]{2,1,0:T(8,128)} %get-tuple-element.19.refs_0_, f32[4,1,128]{2,1,0:T(1,128)} %get-tuple-element.20.refs_1_, f32[4,64,128]{2,1,0:T(8,128)} %get-tuple-element.21.refs_2_, f32[4,1,128]{2,1,0:T(1,128)} %get-tuple-element.22.refs_3_, f32[64,128]{1,0:T(8,128)} %get-tuple-element.24.refs_4_, ...), custom_call_target="tpu_custom_call" | custom-call | tf_op jit(solution)/shard_map/pallas_call | solution.py:224
  71.2 3.4 %all-to-all-start.3 = ((f32[4,128,128]{2,1,0:T(8,128)}), f32[4,128,128]{2,1,0:T(8,128)S(1)}, u32[]{:S(2)}, u32[]{:S(2)}) async-start(f32[4,128,128]{2,1,0:T(8,128)} %shard_map.104), calls=%async_computation.3 | async-start | bytes 524288 | tf_op jit(solution)/shard_map/all_to_all | solution.py:225
  74.9 5.2 %all-to-all-done.3 = f32[4,128,128]{2,1,0:T(8,128)S(1)} async-done(((f32[4,128,128]{2,1,0:T(8,128)}), f32[4,128,128]{2,1,0:T(8,128)S(1)}, u32[]{:S(2)}, u32[]{:S(2)}) %all-to-all-start.3) | async-done | bytes 262176 | tf_op jit(solution)/shard_map/all_to_all | solution.py:225
  81.8 9.6 %all_to_all.30 = f32[8,2,16,256]{3,2,0,1:T(8,128)S(1)} all-to-all(f32[8,2,16,256]{3,2,0,1:T(8,128)S(1)} %copy.87), channel_id=1, replica_groups=mesh['level1'=4,'level0'=4,'inner'=4,'head_outer'=8,'head_inner'=2] {'he..., dimensions={1} | all-to-all | bytes 524288 | tf_op jit(solution)/shard_map/all_to_all | solution.py:233
  91.5 0.7 reduce_sum.48
  92.1 6.8 %all-to-all-start.5 = ((f32[8,16,256]{2,1,0:T(8,128)}), f32[8,16,256]{2,1,0:T(8,128)S(1)}, u32[]{:S(2)}, u32[]{:S(2)}) async-start(f32[8,16,256]{2,1,0:T(8,128)} %reduce_sum.48), calls=%async_computation.5 | async-start | bytes 262144 | tf_op jit(solution)/shard_map/all_to_all | solution.py:233
  99.3 0.7 fusion.5
  101.0 0.7 fusion.4
  101.8 0.6 multiply_reduce_fusion
  103.2 0.8 copy.80
  104.0 0.8 copy.79
  104.9 2.0 %all-to-all-done.5 = f32[8,16,256]{2,1,0:T(8,128)S(1)} async-done(((f32[8,16,256]{2,1,0:T(8,128)}), f32[8,16,256]{2,1,0:T(8,128)S(1)}, u32[]{:S(2)}, u32[]{:S(2)}) %all-to-all-start.5) | async-done | bytes 131104 | tf_op jit(solution)/shard_map/all_to_all | solution.py:233
  (49 shorter events, 10.1 us)
Async XLA Ops:
  0.6 0.9 copy-start.5
  2.1 1.2 %copy-start.3 = (f32[256,256]{1,0:T(8,128)S(1)}, f32[256,256]{1,0:T(8,128)}, u32[]{:S(2)}) copy-start(f32[256,256]{1,0:T(8,128)} %param.11) | copy-start | bytes 786436
  3.2 0.7 copy-start.4
  3.9 0.9 copy-start
  4.8 0.9 copy-start.1
  7.3 10.4 %all-to-all-start = ((f32[4,129,128]{2,1,0:T(8,128)}), f32[4,129,128]{2,1,0:T(8,128)S(1)}, u32[]{:S(2)}, u32[]{:S(2)}) async-start(f32[4,129,128]{2,1,0:T(8,128)} %pad_maximum_fusion), calls=%async_computation | async-start | bytes 557056 | tf_op jit(solution)/shard_map/all_to_all | solution.py:215
  17.8 0.7 copy-start.2
  22.2 12.7 %all-to-all-start.1 = ((f32[4,1,129,128]{3,1,2,0:T(1,128)}), f32[4,1,129,128]{3,1,2,0:T(1,128)S(1)}, u32[]{:S(2)}, u32[]{:S(2)}) async-start(f32[4,1,129,128]{3,1,2,0:T(1,128)} %copy.69), calls=%async_computation.1 | async-start | bytes 528384 | tf_op jit(solution)/shard_map/all_to_all | solution.py:128
  39.0 28.1 %all-to-all-start.2 = ((f32[4,1,65,128]{3,1,2,0:T(1,128)}), f32[4,1,65,128]{3,1,2,0:T(1,128)S(1)}, u32[]{:S(2)}, u32[]{:S(2)}) async-start(f32[4,1,65,128]{3,1,2,0:T(1,128)} %copy.70), calls=%async_computation.2 | async-start | bytes 266240 | tf_op jit(solution)/shard_map/all_to_all | solution.py:128
  71.2 8.9 %all-to-all-start.3 = ((f32[4,128,128]{2,1,0:T(8,128)}), f32[4,128,128]{2,1,0:T(8,128)S(1)}, u32[]{:S(2)}, u32[]{:S(2)}) async-start(f32[4,128,128]{2,1,0:T(8,128)} %shard_map.104), calls=%async_computation.3 | async-start | bytes 524288 | tf_op jit(solution)/shard_map/all_to_all | solution.py:225
  92.1 14.7 %all-to-all-start.5 = ((f32[8,16,256]{2,1,0:T(8,128)}), f32[8,16,256]{2,1,0:T(8,128)S(1)}, u32[]{:S(2)}, u32[]{:S(2)}) async-start(f32[8,16,256]{2,1,0:T(8,128)} %reduce_sum.48), calls=%async_computation.5 | async-start | bytes 262144 | tf_op jit(solution)/shard_map/all_to_all | solution.py:233
